TPU v7x, 256 devices: a whole 4x4x8 slice. The times are simulated.
256 devices in a mesh: lon: 16 (over y_hi, z), lat: 8 (over x, core), band: 2 (over y_lo).
Axes of the slice: x: 4, y: 4 (y_hi: 2, y_lo: 2; y = y_hi * 2 + y_lo), z: 8, core: 2. Of those that a mesh axis runs over, the one named last changes fastest.
Arguments:
- spectrum: float32 [128, 256, 576], P('lat', 'lon', 'band'), may hold values from 0.02 to 13, as said below
- sea_mask: int32 [128, 256], P('lat', 'lon'), may hold values 0 or 1
- ice_mask: int32 [128, 256], P('lat', 'lon'), may hold values 0 or 1
- depth_class: int32 [128, 256], P('lat', 'lon'), may hold values from 0 to 7
- speed_table: float32 [8, 16], replicated, may hold values from 0.2 to 0.8
- refraction_table: float32 [8, 16], replicated, may hold values from 0.05 to 0.5
- depth_slope: float32 [2, 128, 256], P(None, 'lat', 'lon'), may hold values from -1 to 1
- wind_speed: float32 [128, 256], P('lat', 'lon'), may hold values from 0.3 to 3
- wind_dir: float32 [128, 256], P('lat', 'lon'), may hold values from -3.140625 to 3.140625
- ice_rate: float32 [16], replicated, may hold values from 0.1 to 1
Outputs:
- spectrum_out: float32 [128, 256, 576], P('lat', 'lon', 'band')
Inputs may be any that keep to these rules, and one draw needn't show every extreme that they name: `spectrum`: densities are positive.
All inputs are finite; a program needn't handle non-finite values. No bound on the sum of `sea_mask` or of `ice_mask` on one device may be relied on, other than what follows from the above.
Results may differ from a plain program's by a relative error of at most 0.0003.
Values sent between devices are 32-bit elements; how exact they have to be, the bound alone decides.
A program may use at most 64 MiB of HBM per device.

v0:
```python
import math

import jax
import jax.numpy as jnp
from jax import lax
from jax.sharding import PartitionSpec as P

NDIR = 36
ITERS = 4
NCOMP = 576


freq_ratio = 1.1
wind_gain = 0.12
break_coef = 0.05
south_edge = -30.0
band_span = 60.0


def with_halo(cells, sides, width, closed):
    for axis, dim in sides:
        count = lax.axis_size(axis)
        ends = count if closed else count - 1
        head = lax.slice_in_dim(cells, 0, width, axis=dim)
        tail = lax.slice_in_dim(cells, cells.shape[dim] - width, cells.shape[dim], axis=dim)
        cells = jnp.concatenate(
            [
                lax.ppermute(tail, axis, [(i, (i + 1) % count) for i in range(ends)]),
                cells,
                lax.ppermute(head, axis, [((i + 1) % count, i) for i in range(ends)]),
            ],
            axis=dim,
        )
    return cells


def quickest(behind, center, forward, beyond, courant):
    curvature = jnp.where(
        courant >= 0.0, forward - 2.0 * center + behind, beyond - 2.0 * forward + center
    )
    face_value = (
        0.5 * (center + forward)
        - 0.5 * courant * (forward - center)
        - (1.0 - courant * courant) / 6.0 * curvature
    )
    return courant * face_value


def advect(density, cell_speed, axis_dim):
    length = density.shape[axis_dim]

    def piece(array, low, high):
        return lax.slice_in_dim(array, low, high, axis=axis_dim)

    courant = 0.5 * (piece(cell_speed, 1, length - 2) + piece(cell_speed, 2, length - 1))
    fluxes = quickest(
        piece(density, 0, length - 3),
        piece(density, 1, length - 2),
        piece(density, 2, length - 1),
        piece(density, 3, length),
        courant,
    )
    faces = fluxes.shape[axis_dim]
    return piece(density, 2, length - 2) - (piece(fluxes, 1, faces) - piece(fluxes, 0, faces - 1))


def rotate(density, offset):
    dir_index = jnp.arange(density.shape[-1]) % NDIR
    target = dir_index + offset
    inner_roll = jnp.roll(density, -offset, axis=-1)
    if offset > 0:
        outer_roll = jnp.roll(density, NDIR - offset, axis=-1)
        return jnp.where(target >= NDIR, outer_roll, inner_roll)
    outer_roll = jnp.roll(density, -(offset + NDIR), axis=-1)
    return jnp.where(target < 0, outer_roll, inner_roll)


def refract(density, courant):
    fluxes = quickest(rotate(density, -1), density, rotate(density, 1), rotate(density, 2), courant)
    return density - (fluxes - rotate(fluxes, -1))


def expand(per_freq, spread):
    return jnp.dot(per_freq, spread, precision=lax.Precision.HIGHEST)


def lookup(classes, lookup_table):
    onehot = (classes[..., None] == jnp.arange(lookup_table.shape[0])).astype(jnp.float32)
    return jnp.dot(onehot, lookup_table, precision=lax.Precision.HIGHEST)


def stretch(rows, total_rows):
    latitude = (south_edge + band_span * (rows.astype(jnp.float32) + 0.5) / total_rows) * (
        math.pi / 180.0
    )
    return 1.0 / jnp.cos(latitude)


def sources(
    density,
    energy_sum,
    moment,
    levels,
    heading,
    ice_loss,
    sea_share,
    ice_share,
    wind_speed,
    wind_dir,
):
    mean_level = jnp.maximum(moment, 1.0) / jnp.maximum(energy_sum, 1.0)
    energy = energy_sum / NCOMP
    breaking = break_coef * levels * levels / mean_level[..., None] * (energy * energy)[..., None]
    growth = (
        wind_gain
        * wind_speed[..., None]
        * levels
        * jnp.maximum(jnp.cos(heading - wind_dir[..., None]), 0.0)
    )
    damping = ice_share[..., None] * ice_loss
    return sea_share[..., None] * density * jnp.exp(growth - breaking - damping)


def edge_cols(stacked):
    return with_halo(stacked, (("lon", 1),), 2, True)


def edge_rows(stacked):
    return with_halo(stacked, (("lat", 0),), 2, False)


def per_device(
    spectrum,
    sea_mask,
    ice_mask,
    depth_class,
    speed_table,
    refraction_table,
    depth_slope,
    wind_speed,
    wind_dir,
    ice_rate,
):
    rows_dev, cols_dev, comps_dev = spectrum.shape
    freqs_dev = comps_dev // NDIR
    band_index = lax.axis_index("band")
    first_comp = band_index * comps_dev
    local_comp = jnp.arange(comps_dev)
    comp_index = first_comp + local_comp
    spread = (local_comp[None, :] // NDIR == jnp.arange(freqs_dev)[:, None]).astype(jnp.float32)
    heading = 2.0 * math.pi * (comp_index % NDIR).astype(jnp.float32) / NDIR
    face_angle = heading + math.pi / NDIR
    cos_head = jnp.cos(heading)
    sin_head = jnp.sin(heading)
    sin_face = jnp.sin(face_angle)
    cos_face = jnp.cos(face_angle)
    ice_loss_all = jnp.repeat(ice_rate, NDIR)
    sea_share = sea_mask.astype(jnp.float32)
    ice_share = ice_mask.astype(jnp.float32)
    speed_local = lax.dynamic_slice_in_dim(speed_table, band_index * freqs_dev, freqs_dev, 1)
    refr_local = lax.dynamic_slice_in_dim(refraction_table, band_index * freqs_dev, freqs_dev, 1)
    group_speed = lookup(depth_class, speed_local) * sea_share[..., None]
    turning = lookup(depth_class, refr_local) * sea_share[..., None]
    turn_x = turning * depth_slope[0][..., None]
    turn_y = turning * depth_slope[1][..., None]
    total_rows = rows_dev * lax.axis_size("lat")
    first_row = lax.axis_index("lat") * rows_dev
    density = spectrum * sea_share[..., None]
    stretch_rows = stretch(first_row + jnp.arange(rows_dev), total_rows)
    along_t = expand(turn_x, spread) * sin_face - expand(turn_y, spread) * cos_face
    for substep in range(ITERS):
        if substep == 0:
            wide_rims = edge_cols(jnp.concatenate([density, group_speed], axis=-1))
            along_x = (
                expand(wide_rims[..., comps_dev:], spread) * cos_head * stretch_rows[:, None, None]
            )
        else:
            wide_rims = edge_cols(density)
        density = advect(wide_rims[..., :comps_dev], along_x, 1)
        if substep == 0:
            tall_rims = edge_rows(jnp.concatenate([density, group_speed], axis=-1))
            along_y = expand(tall_rims[..., comps_dev:], spread) * sin_head
        else:
            tall_rims = edge_rows(density)
        density = advect(tall_rims[..., :comps_dev], along_y, 0)
        density = refract(density, along_t)
    points = lax.all_to_all(density, "band", split_axis=1, concat_axis=2, tiled=True)
    half_cols = points.shape[1]
    first_col = band_index * half_cols

    def slice_cols(array):
        return lax.dynamic_slice_in_dim(array, first_col, half_cols, 1)

    all_comp = jnp.arange(NCOMP)
    heading_all = 2.0 * math.pi * (all_comp % NDIR).astype(jnp.float32) / NDIR
    levels_all = jnp.exp(math.log(freq_ratio) * (all_comp // NDIR).astype(jnp.float32))
    energy_sum = jnp.sum(points, axis=-1)
    moment = jnp.sum(points * levels_all, axis=-1)
    result = sources(
        points,
        energy_sum,
        moment,
        levels_all,
        heading_all,
        ice_loss_all,
        slice_cols(sea_share),
        slice_cols(ice_share),
        slice_cols(wind_speed),
        slice_cols(wind_dir),
    )
    return lax.all_to_all(result, "band", split_axis=2, concat_axis=1, tiled=True)


def solution(mesh):
    return jax.shard_map(
        per_device,
        mesh=mesh,
        in_specs=(
            P("lat", "lon", "band"),
            P("lat", "lon"),
            P("lat", "lon"),
            P("lat", "lon"),
            P(),
            P(),
            P(None, "lat", "lon"),
            P("lat", "lon"),
            P("lat", "lon"),
            P(),
        ),
        out_specs=P("lat", "lon", "band"),
        check_vma=False,
    )
```

profile of v0, /device:TPU:2, one launch (start us, length us, event | category | flops | bytes accessed | tf_op | source)
XLA Modules:
  0.0 110.2 jit_solution(14666003795829669338)
XLA Ops:
  0.7 1.1 broadcast_multiply_fusion
  1.8 1.0 convolution_multiply_fusion.5
  3.0 2.0 %collective-permute-start = (f32[16,2,296]{2,0,1:T(8,128)S(1)}, f32[16,2,296]{2,0,1:T(8,128)S(1)}, u32[]{:S(2)}, u32[]{:S(2)}) collective-permute-start(f32[16,2,296]{2,0,1:T(8,128)S(1)} %copy.421), channel_id=1, source_target_pairs={{0,16},{16,32},{32,48},{48,64},{64,80},{80,96},{96,112},{112,128},... | collective-permute-start | bytes 113672 | tf_op jit(solution)/shard_map/ppermute | solution.py:28
  5.0 6.7 %collective-permute-start.1 = (f32[16,2,296]{2,0,1:T(8,128)S(1)}, f32[16,2,296]{2,0,1:T(8,128)S(1)}, u32[]{:S(2)}, u32[]{:S(2)}) collective-permute-start(f32[16,2,296]{2,0,1:T(8,128)S(1)} %copy.422), channel_id=1, source_target_pairs={{16,0},{32,16},{48,32},{64,48},{80,64},{96,80},{112,96},{128,112},... | collective-permute-start | bytes 113672 | tf_op jit(solution)/shard_map/ppermute | solution.py:30
  11.8 1.0 convolution_multiply_fusion.4
  15.9 1.9 %collective-permute-start.2 = (f32[2,16,296]{2,1,0:T(8,128)S(1)}, f32[2,16,296]{2,1,0:T(8,128)S(1)}, u32[]{:S(2)}, u32[]{:S(2)}) collective-permute-start(f32[2,16,296]{2,1,0:T(8,128)S(1)} %get-tuple-element.13), channel_id=1, source_target_pairs={{0,2},{2,4},{4,6},{6,8},{8,10},{10,12},{12,14},{1,3},{3,5},{5,7},{... | collective-permute-start | bytes 113672 | tf_op jit(solution)/shard_map/ppermute | solution.py:28
  17.8 3.6 %collective-permute-start.3 = (f32[2,16,296]{2,1,0:T(8,128)S(1)}, f32[2,16,296]{2,1,0:T(8,128)S(1)}, u32[]{:S(2)}, u32[]{:S(2)}) collective-permute-start(f32[2,16,296]{2,1,0:T(8,128)S(1)} %get-tuple-element.14), channel_id=1, source_target_pairs={{2,0},{4,2},{6,4},{8,6},{10,8},{12,10},{14,12},{3,1},{5,3},{7,5},{... | collective-permute-start | bytes 113672 | tf_op jit(solution)/shard_map/ppermute | solution.py:30
  21.5 1.7 %collective-permute-done.3 = f32[2,16,296]{2,1,0:T(8,128)S(1)} collective-permute-done((f32[2,16,296]{2,1,0:T(8,128)S(1)}, f32[2,16,296]{2,1,0:T(8,128)S(1)}, u32[]{:S(2)}, u32[]{:S(2)}) %collective-permute-start.3) | collective-permute-done | bytes 37920 | tf_op jit(solution)/shard_map/ppermute | solution.py:30
  26.5 5.6 %collective-permute-start.5 = (f32[16,2,288]{2,0,1:T(8,128)S(1)}, f32[16,2,288]{2,0,1:T(8,128)S(1)}, u32[]{:S(2)}, u32[]{:S(2)}) collective-permute-start(f32[16,2,288]{2,0,1:T(8,128)S(1)} %copy.436), channel_id=1, source_target_pairs={{16,0},{32,16},{48,32},{64,48},{80,64},{96,80},{112,96},{128,112},... | collective-permute-start | bytes 110600 | tf_op jit(solution)/shard_map/ppermute | solution.py:30
  32.1 2.1 %collective-permute-done.4 = f32[16,2,288]{2,0,1:T(8,128)S(1)} collective-permute-done((f32[16,2,288]{2,0,1:T(8,128)S(1)}, f32[16,2,288]{2,0,1:T(8,128)S(1)}, u32[]{:S(2)}, u32[]{:S(2)}) %collective-permute-start.4) | collective-permute-done | bytes 36896 | tf_op jit(solution)/shard_map/ppermute | solution.py:28
  34.9 2.4 %collective-permute-start.6 = (f32[2,16,288]{2,1,0:T(8,128)S(1)}, f32[2,16,288]{2,1,0:T(8,128)S(1)}, u32[]{:S(2)}, u32[]{:S(2)}) collective-permute-start(f32[2,16,288]{2,1,0:T(8,128)S(1)} %get-tuple-element.51), channel_id=1, source_target_pairs={{0,2},{2,4},{4,6},{6,8},{8,10},{10,12},{12,14},{1,3},{3,5},{5,7},{... | collective-permute-start | bytes 110600 | tf_op jit(solution)/shard_map/ppermute | solution.py:28
  37.3 3.2 %collective-permute-start.7 = (f32[2,16,288]{2,1,0:T(8,128)S(1)}, f32[2,16,288]{2,1,0:T(8,128)S(1)}, u32[]{:S(2)}, u32[]{:S(2)}) collective-permute-start(f32[2,16,288]{2,1,0:T(8,128)S(1)} %get-tuple-element.52), channel_id=1, source_target_pairs={{2,0},{4,2},{6,4},{8,6},{10,8},{12,10},{14,12},{3,1},{5,3},{7,5},{... | collective-permute-start | bytes 110600 | tf_op jit(solution)/shard_map/ppermute | solution.py:30
  40.5 1.7 %collective-permute-done.7 = f32[2,16,288]{2,1,0:T(8,128)S(1)} collective-permute-done((f32[2,16,288]{2,1,0:T(8,128)S(1)}, f32[2,16,288]{2,1,0:T(8,128)S(1)}, u32[]{:S(2)}, u32[]{:S(2)}) %collective-permute-start.7) | collective-permute-done | bytes 36896 | tf_op jit(solution)/shard_map/ppermute | solution.py:30
  44.7 6.1 %collective-permute-start.9 = (f32[16,2,288]{2,0,1:T(8,128)S(1)}, f32[16,2,288]{2,0,1:T(8,128)S(1)}, u32[]{:S(2)}, u32[]{:S(2)}) collective-permute-start(f32[16,2,288]{2,0,1:T(8,128)S(1)} %copy.440), channel_id=1, source_target_pairs={{16,0},{32,16},{48,32},{64,48},{80,64},{96,80},{112,96},{128,112},... | collective-permute-start | bytes 110600 | tf_op jit(solution)/shard_map/ppermute | solution.py:30
  50.8 1.7 %collective-permute-done.8 = f32[16,2,288]{2,0,1:T(8,128)S(1)} collective-permute-done((f32[16,2,288]{2,0,1:T(8,128)S(1)}, f32[16,2,288]{2,0,1:T(8,128)S(1)}, u32[]{:S(2)}, u32[]{:S(2)}) %collective-permute-start.8) | collective-permute-done | bytes 36896 | tf_op jit(solution)/shard_map/ppermute | solution.py:28
  53.3 2.9 %collective-permute-start.10 = (f32[2,16,288]{2,1,0:T(8,128)S(1)}, f32[2,16,288]{2,1,0:T(8,128)S(1)}, u32[]{:S(2)}, u32[]{:S(2)}) collective-permute-start(f32[2,16,288]{2,1,0:T(8,128)S(1)} %get-tuple-element.39), channel_id=1, source_target_pairs={{0,2},{2,4},{4,6},{6,8},{8,10},{10,12},{12,14},{1,3},{3,5},{5,7},{... | collective-permute-start | bytes 110600 | tf_op jit(solution)/shard_map/ppermute | solution.py:28
  56.2 2.7 %collective-permute-start.11 = (f32[2,16,288]{2,1,0:T(8,128)S(1)}, f32[2,16,288]{2,1,0:T(8,128)S(1)}, u32[]{:S(2)}, u32[]{:S(2)}) collective-permute-start(f32[2,16,288]{2,1,0:T(8,128)S(1)} %get-tuple-element.40), channel_id=1, source_target_pairs={{2,0},{4,2},{6,4},{8,6},{10,8},{12,10},{14,12},{3,1},{5,3},{7,5},{... | collective-permute-start | bytes 110600 | tf_op jit(solution)/shard_map/ppermute | solution.py:30
  58.9 1.7 %collective-permute-done.11 = f32[2,16,288]{2,1,0:T(8,128)S(1)} collective-permute-done((f32[2,16,288]{2,1,0:T(8,128)S(1)}, f32[2,16,288]{2,1,0:T(8,128)S(1)}, u32[]{:S(2)}, u32[]{:S(2)}) %collective-permute-start.11) | collective-permute-done | bytes 36896 | tf_op jit(solution)/shard_map/ppermute | solution.py:30
  63.1 5.9 %collective-permute-start.13 = (f32[16,2,288]{2,0,1:T(8,128)S(1)}, f32[16,2,288]{2,0,1:T(8,128)S(1)}, u32[]{:S(2)}, u32[]{:S(2)}) collective-permute-start(f32[16,2,288]{2,0,1:T(8,128)S(1)} %copy.444), channel_id=1, source_target_pairs={{16,0},{32,16},{48,32},{64,48},{80,64},{96,80},{112,96},{128,112},... | collective-permute-start | bytes 110600 | tf_op jit(solution)/shard_map/ppermute | solution.py:30
  69.1 1.9 %collective-permute-done.12 = f32[16,2,288]{2,0,1:T(8,128)S(1)} collective-permute-done((f32[16,2,288]{2,0,1:T(8,128)S(1)}, f32[16,2,288]{2,0,1:T(8,128)S(1)}, u32[]{:S(2)}, u32[]{:S(2)}) %collective-permute-start.12) | collective-permute-done | bytes 36896 | tf_op jit(solution)/shard_map/ppermute | solution.py:28
  71.8 3.3 %collective-permute-start.14 = (f32[2,16,288]{2,1,0:T(8,128)S(1)}, f32[2,16,288]{2,1,0:T(8,128)S(1)}, u32[]{:S(2)}, u32[]{:S(2)}) collective-permute-start(f32[2,16,288]{2,1,0:T(8,128)S(1)} %get-tuple-element.27), channel_id=1, source_target_pairs={{0,2},{2,4},{4,6},{6,8},{8,10},{10,12},{12,14},{1,3},{3,5},{5,7},{... | collective-permute-start | bytes 110600 | tf_op jit(solution)/shard_map/ppermute | solution.py:28
  75.1 2.2 %collective-permute-start.15 = (f32[2,16,288]{2,1,0:T(8,128)S(1)}, f32[2,16,288]{2,1,0:T(8,128)S(1)}, u32[]{:S(2)}, u32[]{:S(2)}) collective-permute-start(f32[2,16,288]{2,1,0:T(8,128)S(1)} %get-tuple-element.28), channel_id=1, source_target_pairs={{2,0},{4,2},{6,4},{8,6},{10,8},{12,10},{14,12},{3,1},{5,3},{7,5},{... | collective-permute-start | bytes 110600 | tf_op jit(solution)/shard_map/ppermute | solution.py:30
  77.4 1.7 %collective-permute-done.15 = f32[2,16,288]{2,1,0:T(8,128)S(1)} collective-permute-done((f32[2,16,288]{2,1,0:T(8,128)S(1)}, f32[2,16,288]{2,1,0:T(8,128)S(1)}, u32[]{:S(2)}, u32[]{:S(2)}) %collective-permute-start.15) | collective-permute-done | bytes 36896 | tf_op jit(solution)/shard_map/ppermute | solution.py:30
  81.4 0.9 copy.446
  82.3 3.5 %all-to-all-start = ((f32[16,16,288]{2,0,1:T(8,128)}), f32[16,16,288]{2,0,1:T(8,128)S(1)}, u32[]{:S(2)}, u32[]{:S(2)}) async-start(f32[16,16,288]{2,0,1:T(8,128)} %copy.446), calls=%async_computation | async-start | bytes 786432 | tf_op jit(solution)/shard_map/all_to_all | solution.py:187
  86.1 6.0 %all-to-all-done = f32[16,16,288]{2,0,1:T(8,128)S(1)} async-done(((f32[16,16,288]{2,0,1:T(8,128)}), f32[16,16,288]{2,0,1:T(8,128)S(1)}, u32[]{:S(2)}, u32[]{:S(2)}) %all-to-all-start) | async-done | bytes 294944 | tf_op jit(solution)/shard_map/all_to_all | solution.py:187
  92.9 1.3 %fusion.108 = f32[16,8,576]{2,1,0:T(8,128)S(1)} fusion(f32[16,8,576]{2,1,0:T(8,128)S(1)} %all_to_all.29, f32[576]{0:T(1024)S(1)} %mul.613, f32[16,8]{1,0:T(8,128)S(1)} %dynamic-slice_convert_fusion, f32[16,8]{1,0:T(8,128)S(1)} %get-tuple-element.66, f32[16,8]{1,0:T(8,128)S(1)} %get-tuple-element.65, f32[576]{0:T(1024)S(1)} %get-tuple-element.75, ...), kind=kLoop, calls=%fused_computation.190 | loop fusion | flops 811008 | bytes 602112 | tf_op jit(solution)/shard_map/mul | solution.py:121
  94.2 0.9 copy.449
  95.1 0.9 reshape.114
  96.0 8.8 %all_to_all.36 = f32[2,1,36864]{2,1,0:T(1,128)S(1)} all-to-all(f32[2,1,36864]{2,1,0:T(1,128)S(1)} %reshape.114), channel_id=1, replica_groups=mesh['lon'=16,'lat'=8,'band'=2] {'band'}, dimensions={0} | all-to-all | bytes 589824 | tf_op jit(solution)/shard_map/all_to_all | solution.py:211
  105.3 1.6 %reduce.2 = f32[2,36864]{1,0:T(2,128)S(1)} reduce(f32[2,1,36864]{2,1,0:T(1,128)S(1)} %all_to_all.36, f32[]{:T(128)} %broadcast.442), dimensions={1}, to_apply=%all_to_all.30.reduce_sub_computation | reduce | bytes 589828 | tf_op jit(solution)/shard_map/all_to_all | solution.py:211
  107.7 1.7 %copy.458 = f32[16,8,2,288]{3,2,1,0:T(2,128)S(1)} copy(f32[16,8,2,288]{0,1,3,2:T(8,128)S(1)} %bitcast.40) | data formatting | bytes 589824 | tf_op jit(solution)/shard_map/all_to_all | solution.py:211
  (145 shorter events, 19.6 us)
Async XLA Ops:
  0.0 1.8 %copy-start = (f32[8,16]{1,0:T(8,128)S(1)}, f32[8,16]{1,0:T(8,128)}, u32[]{:S(2)}) copy-start(f32[8,16]{1,0:T(8,128)} %param.14) | copy-start | bytes 1540
  3.0 11.0 %collective-permute-start = (f32[16,2,296]{2,0,1:T(8,128)S(1)}, f32[16,2,296]{2,0,1:T(8,128)S(1)}, u32[]{:S(2)}, u32[]{:S(2)}) collective-permute-start(f32[16,2,296]{2,0,1:T(8,128)S(1)} %copy.421), channel_id=1, source_target_pairs={{0,16},{16,32},{32,48},{48,64},{64,80},{80,96},{96,112},{112,128},... | collective-permute-start | bytes 113672 | tf_op jit(solution)/shard_map/ppermute | solution.py:28
  5.0 9.1 %collective-permute-start.1 = (f32[16,2,296]{2,0,1:T(8,128)S(1)}, f32[16,2,296]{2,0,1:T(8,128)S(1)}, u32[]{:S(2)}, u32[]{:S(2)}) collective-permute-start(f32[16,2,296]{2,0,1:T(8,128)S(1)} %copy.422), channel_id=1, source_target_pairs={{16,0},{32,16},{48,32},{64,48},{80,64},{96,80},{112,96},{128,112},... | collective-permute-start | bytes 113672 | tf_op jit(solution)/shard_map/ppermute | solution.py:30
  14.7 1.0 copy-start.1
  15.9 5.6 %collective-permute-start.2 = (f32[2,16,296]{2,1,0:T(8,128)S(1)}, f32[2,16,296]{2,1,0:T(8,128)S(1)}, u32[]{:S(2)}, u32[]{:S(2)}) collective-permute-start(f32[2,16,296]{2,1,0:T(8,128)S(1)} %get-tuple-element.13), channel_id=1, source_target_pairs={{0,2},{2,4},{4,6},{6,8},{8,10},{10,12},{12,14},{1,3},{3,5},{5,7},{... | collective-permute-start | bytes 113672 | tf_op jit(solution)/shard_map/ppermute | solution.py:28
  17.8 5.4 %collective-permute-start.3 = (f32[2,16,296]{2,1,0:T(8,128)S(1)}, f32[2,16,296]{2,1,0:T(8,128)S(1)}, u32[]{:S(2)}, u32[]{:S(2)}) collective-permute-start(f32[2,16,296]{2,1,0:T(8,128)S(1)} %get-tuple-element.14), channel_id=1, source_target_pairs={{2,0},{4,2},{6,4},{8,6},{10,8},{12,10},{14,12},{3,1},{5,3},{7,5},{... | collective-permute-start | bytes 113672 | tf_op jit(solution)/shard_map/ppermute | solution.py:30
  26.4 7.8 %collective-permute-start.4 = (f32[16,2,288]{2,0,1:T(8,128)S(1)}, f32[16,2,288]{2,0,1:T(8,128)S(1)}, u32[]{:S(2)}, u32[]{:S(2)}) collective-permute-start(f32[16,2,288]{2,0,1:T(8,128)S(1)} %copy.434), channel_id=1, source_target_pairs={{0,16},{16,32},{32,48},{48,64},{64,80},{80,96},{96,112},{112,128},... | collective-permute-start | bytes 110600 | tf_op jit(solution)/shard_map/ppermute | solution.py:28
  26.5 7.7 %collective-permute-start.5 = (f32[16,2,288]{2,0,1:T(8,128)S(1)}, f32[16,2,288]{2,0,1:T(8,128)S(1)}, u32[]{:S(2)}, u32[]{:S(2)}) collective-permute-start(f32[16,2,288]{2,0,1:T(8,128)S(1)} %copy.436), channel_id=1, source_target_pairs={{16,0},{32,16},{48,32},{64,48},{80,64},{96,80},{112,96},{128,112},... | collective-permute-start | bytes 110600 | tf_op jit(solution)/shard_map/ppermute | solution.py:30
  34.9 5.6 %collective-permute-start.6 = (f32[2,16,288]{2,1,0:T(8,128)S(1)}, f32[2,16,288]{2,1,0:T(8,128)S(1)}, u32[]{:S(2)}, u32[]{:S(2)}) collective-permute-start(f32[2,16,288]{2,1,0:T(8,128)S(1)} %get-tuple-element.51), channel_id=1, source_target_pairs={{0,2},{2,4},{4,6},{6,8},{8,10},{10,12},{12,14},{1,3},{3,5},{5,7},{... | collective-permute-start | bytes 110600 | tf_op jit(solution)/shard_map/ppermute | solution.py:28
  37.3 4.9 %collective-permute-start.7 = (f32[2,16,288]{2,1,0:T(8,128)S(1)}, f32[2,16,288]{2,1,0:T(8,128)S(1)}, u32[]{:S(2)}, u32[]{:S(2)}) collective-permute-start(f32[2,16,288]{2,1,0:T(8,128)S(1)} %get-tuple-element.52), channel_id=1, source_target_pairs={{2,0},{4,2},{6,4},{8,6},{10,8},{12,10},{14,12},{3,1},{5,3},{7,5},{... | collective-permute-start | bytes 110600 | tf_op jit(solution)/shard_map/ppermute | solution.py:30
  44.6 8.0 %collective-permute-start.8 = (f32[16,2,288]{2,0,1:T(8,128)S(1)}, f32[16,2,288]{2,0,1:T(8,128)S(1)}, u32[]{:S(2)}, u32[]{:S(2)}) collective-permute-start(f32[16,2,288]{2,0,1:T(8,128)S(1)} %copy.438), channel_id=1, source_target_pairs={{0,16},{16,32},{32,48},{48,64},{64,80},{80,96},{96,112},{112,128},... | collective-permute-start | bytes 110600 | tf_op jit(solution)/shard_map/ppermute | solution.py:28
  44.7 7.9 %collective-permute-start.9 = (f32[16,2,288]{2,0,1:T(8,128)S(1)}, f32[16,2,288]{2,0,1:T(8,128)S(1)}, u32[]{:S(2)}, u32[]{:S(2)}) collective-permute-start(f32[16,2,288]{2,0,1:T(8,128)S(1)} %copy.440), channel_id=1, source_target_pairs={{16,0},{32,16},{48,32},{64,48},{80,64},{96,80},{112,96},{128,112},... | collective-permute-start | bytes 110600 | tf_op jit(solution)/shard_map/ppermute | solution.py:30
  53.3 5.6 %collective-permute-start.10 = (f32[2,16,288]{2,1,0:T(8,128)S(1)}, f32[2,16,288]{2,1,0:T(8,128)S(1)}, u32[]{:S(2)}, u32[]{:S(2)}) collective-permute-start(f32[2,16,288]{2,1,0:T(8,128)S(1)} %get-tuple-element.39), channel_id=1, source_target_pairs={{0,2},{2,4},{4,6},{6,8},{8,10},{10,12},{12,14},{1,3},{3,5},{5,7},{... | collective-permute-start | bytes 110600 | tf_op jit(solution)/shard_map/ppermute | solution.py:28
  56.2 4.4 %collective-permute-start.11 = (f32[2,16,288]{2,1,0:T(8,128)S(1)}, f32[2,16,288]{2,1,0:T(8,128)S(1)}, u32[]{:S(2)}, u32[]{:S(2)}) collective-permute-start(f32[2,16,288]{2,1,0:T(8,128)S(1)} %get-tuple-element.40), channel_id=1, source_target_pairs={{2,0},{4,2},{6,4},{8,6},{10,8},{12,10},{14,12},{3,1},{5,3},{7,5},{... | collective-permute-start | bytes 110600 | tf_op jit(solution)/shard_map/ppermute | solution.py:30
  62.4 6.6 %copy-start.2 = (s32[16,16]{1,0:T(8,128)S(1)}, s32[16,16]{1,0:T(8,128)}, u32[]{:S(2)}) copy-start(s32[16,16]{1,0:T(8,128)} %param.12) | copy-start | bytes 3076
  63.0 8.0 %collective-permute-start.12 = (f32[16,2,288]{2,0,1:T(8,128)S(1)}, f32[16,2,288]{2,0,1:T(8,128)S(1)}, u32[]{:S(2)}, u32[]{:S(2)}) collective-permute-start(f32[16,2,288]{2,0,1:T(8,128)S(1)} %copy.442), channel_id=1, source_target_pairs={{0,16},{16,32},{32,48},{48,64},{64,80},{80,96},{96,112},{112,128},... | collective-permute-start | bytes 110600 | tf_op jit(solution)/shard_map/ppermute | solution.py:28
  63.1 7.9 %collective-permute-start.13 = (f32[16,2,288]{2,0,1:T(8,128)S(1)}, f32[16,2,288]{2,0,1:T(8,128)S(1)}, u32[]{:S(2)}, u32[]{:S(2)}) collective-permute-start(f32[16,2,288]{2,0,1:T(8,128)S(1)} %copy.444), channel_id=1, source_target_pairs={{16,0},{32,16},{48,32},{64,48},{80,64},{96,80},{112,96},{128,112},... | collective-permute-start | bytes 110600 | tf_op jit(solution)/shard_map/ppermute | solution.py:30
  71.8 5.6 %collective-permute-start.14 = (f32[2,16,288]{2,1,0:T(8,128)S(1)}, f32[2,16,288]{2,1,0:T(8,128)S(1)}, u32[]{:S(2)}, u32[]{:S(2)}) collective-permute-start(f32[2,16,288]{2,1,0:T(8,128)S(1)} %get-tuple-element.27), channel_id=1, source_target_pairs={{0,2},{2,4},{4,6},{6,8},{8,10},{10,12},{12,14},{1,3},{3,5},{5,7},{... | collective-permute-start | bytes 110600 | tf_op jit(solution)/shard_map/ppermute | solution.py:28
  75.1 4.0 %collective-permute-start.15 = (f32[2,16,288]{2,1,0:T(8,128)S(1)}, f32[2,16,288]{2,1,0:T(8,128)S(1)}, u32[]{:S(2)}, u32[]{:S(2)}) collective-permute-start(f32[2,16,288]{2,1,0:T(8,128)S(1)} %get-tuple-element.28), channel_id=1, source_target_pairs={{2,0},{4,2},{6,4},{8,6},{10,8},{12,10},{14,12},{3,1},{5,3},{7,5},{... | collective-permute-start | bytes 110600 | tf_op jit(solution)/shard_map/ppermute | solution.py:30
  80.9 4.9 %copy-start.5 = (f32[16]{0:T(128)S(1)}, f32[16]{0:T(128)}, u32[]{:S(2)}) copy-start(f32[16]{0:T(128)} %param.19) | copy-start | bytes 196
  80.9 5.1 %copy-start.3 = (f32[16,16]{1,0:T(8,128)S(1)}, f32[16,16]{1,0:T(8,128)}, u32[]{:S(2)}) copy-start(f32[16,16]{1,0:T(8,128)} %param.17) | copy-start | bytes 3076
  80.9 5.1 %copy-start.4 = (f32[16,16]{1,0:T(8,128)S(1)}, f32[16,16]{1,0:T(8,128)}, u32[]{:S(2)}) copy-start(f32[16,16]{1,0:T(8,128)} %param.18) | copy-start | bytes 3076
  82.3 9.8 %all-to-all-start = ((f32[16,16,288]{2,0,1:T(8,128)}), f32[16,16,288]{2,0,1:T(8,128)S(1)}, u32[]{:S(2)}, u32[]{:S(2)}) async-start(f32[16,16,288]{2,0,1:T(8,128)} %copy.446), calls=%async_computation | async-start | bytes 786432 | tf_op jit(solution)/shard_map/all_to_all | solution.py:187
where the time goes:
time: 112 us; the launch traced here: 110 us
  starting transfers between devices  52.3 us (47%)
  waiting for transfers between devices  18.5 us (17%)
  local copies, waits for them, and re-layouts  12.8 us (11%)
  other arithmetic  12.7 us (11%)
  blocking collectives  8.85 us (8%)
  matrix products  4.06 us (4%)
    ppermute x8, starting transfers between devices, with_halo(): lax.ppermute(head, axis, [((i + 1) % count, i) for i in range(ends)])  36.1 us
    ppermute x8, starting transfers between devices, with_halo(): lax.ppermute(tail, axis, [(i, (i + 1) % count) for i in range(ends)])  12.7 us
    all_to_all x1, blocking collectives, per_device(): lax.all_to_all(result, 'band', split_axis=2, concat_axis=1, tiled=True)  8.85 us
    ppermute x8, waiting for transfers between devices, with_halo(): lax.ppermute(head, axis, [((i + 1) % count, i) for i in range(ends)])  6.84 us
    all_to_all x1, waiting for transfers between devices, per_device(): lax.all_to_all(density, 'band', split_axis=1, concat_axis=2, tiled=True)  6 us
    ppermute x8, waiting for transfers between devices, with_halo(): lax.ppermute(tail, axis, [(i, (i + 1) % count) for i in range(ends)])  5.67 us
    mul x11, other arithmetic, quickest(): return courant * face_value  5.36 us
    all_to_all x1, starting transfers between devices, per_device(): lax.all_to_all(density, 'band', split_axis=1, concat_axis=2, tiled=True)  3.47 us
  transfers between devices with their start and end apart: 17, of which 8 were waited for; matrix products, arithmetic and copies ran while one was open for 3% of the time, Pallas kernels for 0%

commit v1 on v0

--- a/solution.py
+++ b/solution.py
@@ -15,23 +15,6 @@
 break_coef = 0.05
 south_edge = -30.0
 band_span = 60.0
-
-
-def with_halo(cells, sides, width, closed):
-    for axis, dim in sides:
-        count = lax.axis_size(axis)
-        ends = count if closed else count - 1
-        head = lax.slice_in_dim(cells, 0, width, axis=dim)
-        tail = lax.slice_in_dim(cells, cells.shape[dim] - width, cells.shape[dim], axis=dim)
-        cells = jnp.concatenate(
-            [
-                lax.ppermute(tail, axis, [(i, (i + 1) % count) for i in range(ends)]),
-                cells,
-                lax.ppermute(head, axis, [((i + 1) % count, i) for i in range(ends)]),
-            ],
-            axis=dim,
-        )
-    return cells
 
 
 def quickest(behind, center, forward, beyond, courant):
@@ -121,12 +104,18 @@
     return sea_share[..., None] * density * jnp.exp(growth - breaking - damping)
 
 
-def edge_cols(stacked):
-    return with_halo(stacked, (("lon", 1),), 2, True)
-
-
-def edge_rows(stacked):
-    return with_halo(stacked, (("lat", 0),), 2, False)
+def exchange(cells, axis, dim, width, closed):
+    count = lax.axis_size(axis)
+    ends = count if closed else count - 1
+    head = lax.slice_in_dim(cells, 0, width, axis=dim)
+    tail = lax.slice_in_dim(cells, cells.shape[dim] - width, cells.shape[dim], axis=dim)
+    before = lax.ppermute(tail, axis, [(i, (i + 1) % count) for i in range(ends)])
+    after = lax.ppermute(head, axis, [((i + 1) % count, i) for i in range(ends)])
+    return jnp.concatenate([before, cells, after], axis=dim)
+
+
+def trim(array, dim, amount):
+    return lax.slice_in_dim(array, amount, array.shape[dim] - amount, axis=dim)
 
 
 def per_device(
@@ -143,6 +132,7 @@
 ):
     rows_dev, cols_dev, comps_dev = spectrum.shape
     freqs_dev = comps_dev // NDIR
+    halo = 2 * ITERS
     band_index = lax.axis_index("band")
     first_comp = band_index * comps_dev
     local_comp = jnp.arange(comps_dev)
@@ -154,7 +144,6 @@
     sin_head = jnp.sin(heading)
     sin_face = jnp.sin(face_angle)
     cos_face = jnp.cos(face_angle)
-    ice_loss_all = jnp.repeat(ice_rate, NDIR)
     sea_share = sea_mask.astype(jnp.float32)
     ice_share = ice_mask.astype(jnp.float32)
     speed_local = lax.dynamic_slice_in_dim(speed_table, band_index * freqs_dev, freqs_dev, 1)
@@ -163,52 +152,51 @@
     turning = lookup(depth_class, refr_local) * sea_share[..., None]
     turn_x = turning * depth_slope[0][..., None]
     turn_y = turning * depth_slope[1][..., None]
+    density = spectrum * sea_share[..., None]
+
+    fields = jnp.concatenate([group_speed, turn_x, turn_y], axis=-1)
+    density, fields = [exchange(a, "lon", 1, halo, True) for a in (density, fields)]
+    density, fields = [exchange(a, "lat", 0, halo, False) for a in (density, fields)]
+
     total_rows = rows_dev * lax.axis_size("lat")
-    first_row = lax.axis_index("lat") * rows_dev
-    density = spectrum * sea_share[..., None]
-    stretch_rows = stretch(first_row + jnp.arange(rows_dev), total_rows)
-    along_t = expand(turn_x, spread) * sin_face - expand(turn_y, spread) * cos_face
+    first_row = lax.axis_index("lat") * rows_dev - halo
+    rows_ext = first_row + jnp.arange(rows_dev + 2 * halo)
+    inside = ((rows_ext >= 0) & (rows_ext < total_rows))[:, None, None]
+    stretch_rows = stretch(rows_ext, total_rows)
+    gs_ext = expand(fields[..., :freqs_dev], spread)
+    along_x = gs_ext * cos_head * stretch_rows[:, None, None]
+    along_y = gs_ext * sin_head
+    along_t = (
+        expand(fields[..., freqs_dev : 2 * freqs_dev], spread) * sin_face
+        - expand(fields[..., 2 * freqs_dev :], spread) * cos_face
+    )
     for substep in range(ITERS):
-        if substep == 0:
-            wide_rims = edge_cols(jnp.concatenate([density, group_speed], axis=-1))
-            along_x = (
-                expand(wide_rims[..., comps_dev:], spread) * cos_head * stretch_rows[:, None, None]
-            )
-        else:
-            wide_rims = edge_cols(density)
-        density = advect(wide_rims[..., :comps_dev], along_x, 1)
-        if substep == 0:
-            tall_rims = edge_rows(jnp.concatenate([density, group_speed], axis=-1))
-            along_y = expand(tall_rims[..., comps_dev:], spread) * sin_head
-        else:
-            tall_rims = edge_rows(density)
-        density = advect(tall_rims[..., :comps_dev], along_y, 0)
+        density = advect(density, along_x, 1)
+        along_x, along_y, along_t = [trim(a, 1, 2) for a in (along_x, along_y, along_t)]
+        density = advect(density, along_y, 0)
+        inside = trim(inside, 0, 2)
+        density = jnp.where(inside, density, 0.0)
+        along_x, along_y, along_t = [trim(a, 0, 2) for a in (along_x, along_y, along_t)]
         density = refract(density, along_t)
-    points = lax.all_to_all(density, "band", split_axis=1, concat_axis=2, tiled=True)
-    half_cols = points.shape[1]
-    first_col = band_index * half_cols
-
-    def slice_cols(array):
-        return lax.dynamic_slice_in_dim(array, first_col, half_cols, 1)
-
-    all_comp = jnp.arange(NCOMP)
-    heading_all = 2.0 * math.pi * (all_comp % NDIR).astype(jnp.float32) / NDIR
-    levels_all = jnp.exp(math.log(freq_ratio) * (all_comp // NDIR).astype(jnp.float32))
-    energy_sum = jnp.sum(points, axis=-1)
-    moment = jnp.sum(points * levels_all, axis=-1)
-    result = sources(
-        points,
+
+    levels = jnp.exp(math.log(freq_ratio) * (comp_index // NDIR).astype(jnp.float32))
+    ice_loss = lax.dynamic_slice_in_dim(jnp.repeat(ice_rate, NDIR), first_comp, comps_dev, 0)
+    partial = jnp.stack([jnp.sum(density, axis=-1), jnp.sum(density * levels, axis=-1)])
+    other = lax.ppermute(partial, "band", [(0, 1), (1, 0)])
+    energy_sum = partial[0] + other[0]
+    moment = partial[1] + other[1]
+    return sources(
+        density,
         energy_sum,
         moment,
-        levels_all,
-        heading_all,
-        ice_loss_all,
-        slice_cols(sea_share),
-        slice_cols(ice_share),
-        slice_cols(wind_speed),
-        slice_cols(wind_dir),
-    )
-    return lax.all_to_all(result, "band", split_axis=2, concat_axis=1, tiled=True)
+        levels,
+        heading,
+        ice_loss,
+        sea_share,
+        ice_share,
+        wind_speed,
+        wind_dir,
+    )
 
 
 def solution(mesh):

time: 112 us -> 71.5 us (0.64)
  the two profiles are of different devices: /device:TPU:2 before, /device:TPU:1 now
where the time goes in v1:
time: 71.5 us; the launch traced here: 71 us
  starting transfers between devices  25.8 us (36%)
  other arithmetic  20.6 us (29%)
  waiting for transfers between devices  11.1 us (16%)
  local copies, waits for them, and re-layouts  8.07 us (11%)
  matrix products  4.78 us (7%)
    ppermute x4, starting transfers between devices, exchange(): lax.ppermute(head, axis, [((i + 1) % count, i) for i in range(ends)])  16.3 us
    mul x12, other arithmetic, quickest(): return courant * face_value  13 us
    ppermute x4, starting transfers between devices, exchange(): lax.ppermute(tail, axis, [(i, (i + 1) % count) for i in range(ends)])  9.07 us
    ppermute x4, waiting for transfers between devices, exchange(): lax.ppermute(head, axis, [((i + 1) % count, i) for i in range(ends)])  8.09 us
    slice x20, local copies, waits for them, and re-layouts, rotate(): inner_roll = jnp.roll(density, -offset, axis=-1)  3.53 us
    dot_general x3, matrix products, expand(): return jnp.dot(per_freq, spread, precision=lax.Precision.HIGHEST)  2.79 us
    mul x1, other arithmetic, sources(): return sea_share[..., None] * density * jnp.exp(growth - breaking - damping)  2.34 us
    slice x16, local copies, waits for them, and re-layouts, rotate(): outer_roll = jnp.roll(density, NDIR - offset, axis=-1)  2.15 us
  transfers between devices with their start and end apart: 9, of which 4 were waited for; matrix products, arithmetic and copies ran while one was open for 6% of the time, Pallas kernels for 0%

profile of v1, /device:TPU:1, one launch (start us, length us, event | category | flops | bytes accessed | tf_op | source)
XLA Modules:
  0.0 71.0 jit_solution(9213370702520834130)
XLA Ops:
  0.0 0.8 %convert_element_type.45 = f32[16,16]{1,0:T(8,128)S(1)} convert(s32[16,16]{1,0:T(8,128)} %param.11) | non-fusion elementwise | flops 256 | bytes 2048 | tf_op jit(solution)/shard_map/convert_element_type | solution.py:147
  0.8 0.7 %slice_bitcast_fusion.3 = (f32[16,16]{1,0:T(8,128)S(1)}, f32[16,16]{1,0:T(8,128)S(1)}) fusion(f32[2,16,16]{2,1,0:T(8,128)} %param.16), kind=kLoop, calls=%fused_computation.174 | loop fusion | bytes 4096 | tf_op jit(solution)/shard_map/mul | solution.py:153
  1.5 1.0 %convolution_multiply_fusion.1 = f32[16,16,8]{1,2,0:T(8,128)S(1)} fusion(f32[16,16]{1,0:T(8,128)S(1)} %convert_element_type.45, s32[16,16]{1,0:T(8,128)} %param.13, f32[8,16]{1,0:T(8,128)} %param.14, s32[]{:T(128)S(6)} %select_n.236), kind=kOutput, calls=%fused_computation.46 | convolution fusion | flops 200704 | bytes 10756 | tf_op jit(solution)/shard_map/dot_general | solution.py:72
  2.5 1.0 %broadcast_multiply_fusion.3 = (f32[16,16,8]{1,2,0:T(8,128)S(1)}, f32[16,16,8]{1,2,0:T(8,128)S(1)}) fusion(f32[16,16]{1,0:T(8,128)S(1)} %get-tuple-element.54, f32[16,16]{1,0:T(8,128)S(1)} %get-tuple-element.55, f32[16,16]{1,0:T(8,128)S(1)} %convert_element_type.45, f32[8,16]{1,0:T(8,128)S(1)} %copy-done, s32[]{:T(128)S(6)} %select_n.236, s32[16,16]{1,0:T(8,128)} %param.13), kind=kOutput, calls=%fused_computation.160 | convolution fusion | flops 204800 | bytes 20996 | tf_op jit(solution)/shard_map/dot_general | solution.py:72
  3.6 2.5 %collective-permute-start.4 = (f32[16,8,24]{1,2,0:T(8,128)S(1)}, f32[16,8,24]{1,2,0:T(8,128)S(1)}, u32[]{:S(2)}, u32[]{:S(2)}) collective-permute-start(f32[16,8,24]{1,2,0:T(8,128)S(1)} %get-tuple-element.48), channel_id=1, source_target_pairs={{0,16},{16,32},{32,48},{48,64},{64,80},{80,96},{96,112},{112,128},... | collective-permute-start | bytes 36872 | tf_op jit(solution)/shard_map/ppermute | solution.py:112
  6.2 6.7 %collective-permute-start.5 = (f32[16,8,24]{1,2,0:T(8,128)S(1)}, f32[16,8,24]{1,2,0:T(8,128)S(1)}, u32[]{:S(2)}, u32[]{:S(2)}) collective-permute-start(f32[16,8,24]{1,2,0:T(8,128)S(1)} %get-tuple-element.49), channel_id=1, source_target_pairs={{16,0},{32,16},{48,32},{64,48},{80,64},{96,80},{112,96},{128,112},... | collective-permute-start | bytes 36872 | tf_op jit(solution)/shard_map/ppermute | solution.py:113
  13.1 5.1 %collective-permute-start.1 = (f32[16,8,288]{2,1,0:T(8,128)S(1)}, f32[16,8,288]{2,1,0:T(8,128)S(1)}, u32[]{:S(2)}, u32[]{:S(2)}) collective-permute-start(f32[16,8,288]{2,1,0:T(8,128)S(1)} %get-tuple-element.45), channel_id=1, source_target_pairs={{16,0},{32,16},{48,32},{64,48},{80,64},{96,80},{112,96},{128,112},... | collective-permute-start | bytes 442376 | tf_op jit(solution)/shard_map/ppermute | solution.py:113
  18.6 4.5 %collective-permute-start.6 = (f32[8,32,24]{1,2,0:T(8,128)S(1)}, f32[8,32,24]{1,2,0:T(8,128)S(1)}, u32[]{:S(2)}, u32[]{:S(2)}) collective-permute-start(f32[8,32,24]{1,2,0:T(8,128)S(1)} %get-tuple-element.46), channel_id=1, source_target_pairs={{0,2},{2,4},{4,6},{6,8},{8,10},{10,12},{12,14},{1,3},{3,5},{5,7},{... | collective-permute-start | bytes 73736 | tf_op jit(solution)/shard_map/ppermute | solution.py:112
  23.1 1.9 %collective-permute-start.7 = (f32[8,32,24]{1,2,0:T(8,128)S(1)}, f32[8,32,24]{1,2,0:T(8,128)S(1)}, u32[]{:S(2)}, u32[]{:S(2)}) collective-permute-start(f32[8,32,24]{1,2,0:T(8,128)S(1)} %get-tuple-element.47), channel_id=1, source_target_pairs={{2,0},{4,2},{6,4},{8,6},{10,8},{12,10},{14,12},{3,1},{5,3},{7,5},{... | collective-permute-start | bytes 73736 | tf_op jit(solution)/shard_map/ppermute | solution.py:113
  25.4 3.7 %collective-permute-done.7 = f32[8,32,24]{1,2,0:T(8,128)S(1)} collective-permute-done((f32[8,32,24]{1,2,0:T(8,128)S(1)}, f32[8,32,24]{1,2,0:T(8,128)S(1)}, u32[]{:S(2)}, u32[]{:S(2)}) %collective-permute-start.7) | collective-permute-done | bytes 24608 | tf_op jit(solution)/shard_map/ppermute | solution.py:113
  29.3 0.9 %broadcast_multiply_fusion = (f32[32,32,288]{2,1,0:T(8,128)S(1)}, f32[32,32,288]{2,1,0:T(8,128)S(1)}) fusion(f32[288]{0:T(512)S(1)} %get-tuple-element.60, f32[32]{0:T(128)S(1)} %cosine_divide_fusion, f32[288]{0:T(512)S(1)} %get-tuple-element.61, s32[288]{0:T(512)S(1)} %add_select_fusion.2, f32[32,32,24]{1,2,0:T(8,128)S(1)} %pad_maximum_fusion.2), kind=kOutput, calls=%fused_computation.84 | convolution fusion | flops 29198592 | bytes 2497024 | tf_op jit(solution)/shard_map/dot_general | solution.py:67
  30.2 0.8 %fusion.93 = f32[32,32,288]{2,1,0:T(8,128)S(1)} fusion(f32[32,32,24]{1,2,0:T(8,128)S(1)} %pad_maximum_fusion.2, s32[288]{0:T(512)S(1)} %add_select_fusion.2), kind=kOutput, calls=%fused_computation.154 | convolution fusion | flops 28313856 | bytes 1312768 | tf_op jit(solution)/shard_map/dot_general | solution.py:67
  31.2 1.9 %collective-permute-start.2 = (f32[8,32,288]{2,1,0:T(8,128)S(1)}, f32[8,32,288]{2,1,0:T(8,128)S(1)}, u32[]{:S(2)}, u32[]{:S(2)}) collective-permute-start(f32[8,32,288]{2,1,0:T(8,128)S(1)} %get-tuple-element.26), channel_id=1, source_target_pairs={{0,2},{2,4},{4,6},{6,8},{8,10},{10,12},{12,14},{1,3},{3,5},{5,7},{... | collective-permute-start | bytes 884744 | tf_op jit(solution)/shard_map/ppermute | solution.py:112
  33.2 2.6 %collective-permute-start.3 = (f32[8,32,288]{2,1,0:T(8,128)S(1)}, f32[8,32,288]{2,1,0:T(8,128)S(1)}, u32[]{:S(2)}, u32[]{:S(2)}) collective-permute-start(f32[8,32,288]{2,1,0:T(8,128)S(1)} %get-tuple-element.27), channel_id=1, source_target_pairs={{2,0},{4,2},{6,4},{8,6},{10,8},{12,10},{14,12},{3,1},{5,3},{7,5},{... | collective-permute-start | bytes 884744 | tf_op jit(solution)/shard_map/ppermute | solution.py:113
  35.8 1.0 %multiply_subtract_fusion = f32[32,32,288]{2,1,0:T(8,128)S(1)} fusion(f32[32,32,288]{2,1,0:T(8,128)S(1)} %fusion.93, f32[288]{0:T(512)S(1)} %get-tuple-element.58, f32[288]{0:T(512)S(1)} %get-tuple-element.59, f32[32,32,24]{1,2,0:T(8,128)S(1)} %pad_maximum_fusion.2, s32[288]{0:T(512)S(1)} %add_select_fusion.2), kind=kOutput, calls=%fused_computation.11 | convolution fusion | flops 29198592 | bytes 2889728 | tf_op jit(solution)/shard_map/dot_general | solution.py:67
  36.8 1.1 %collective-permute-done.2 = f32[8,32,288]{2,1,0:T(8,128)S(1)} collective-permute-done((f32[8,32,288]{2,1,0:T(8,128)S(1)}, f32[8,32,288]{2,1,0:T(8,128)S(1)}, u32[]{:S(2)}, u32[]{:S(2)}) %collective-permute-start.2) | collective-permute-done | bytes 294944 | tf_op jit(solution)/shard_map/ppermute | solution.py:112
  37.9 4.4 %collective-permute-done.3 = f32[8,32,288]{2,1,0:T(8,128)S(1)} collective-permute-done((f32[8,32,288]{2,1,0:T(8,128)S(1)}, f32[8,32,288]{2,1,0:T(8,128)S(1)}, u32[]{:S(2)}, u32[]{:S(2)}) %collective-permute-start.3) | collective-permute-done | bytes 294944 | tf_op jit(solution)/shard_map/ppermute | solution.py:113
  42.4 1.6 %fusion.5 = f32[32,29,288]{2,1,0:T(8,128)S(1)} fusion(f32[32,32,288]{2,1,0:T(8,128)S(1)} %pad_maximum_fusion, f32[32,32,288]{2,1,0:T(8,128)S(1)} %get-tuple-element.9), kind=kLoop, calls=%fused_computation.7 | loop fusion | flops 5879808 | bytes 7483392 | tf_op jit(solution)/shard_map/mul | solution.py:29
  44.4 1.0 %fusion.10 = f32[29,28,288]{2,1,0:T(8,128)S(1)} fusion(f32[32,28,288]{2,1,0:T(8,128)S(1)} %fusion, f32[32,32,288]{2,1,0:T(8,128)S(1)} %get-tuple-element.8), kind=kLoop, calls=%fused_computation.18 | loop fusion | flops 5144832 | bytes 6547968 | tf_op jit(solution)/shard_map/mul | solution.py:29
  47.6 2.6 %fusion.22 = f32[28,28,288]{2,1,0:T(8,128)S(1)} fusion(f32[28,28,35]{2,1,0:T(8,128)S(1)} %get-tuple-element.11, f32[28,28,253]{2,1,0:T(8,128)S(1)} %get-tuple-element.13, f32[28,28,287]{2,1,0:T(8,128)S(1)} %get-tuple-element.15, f32[28,28,1]{2,1,0:T(8,128)S(1)} %get-tuple-element.17, f32[28,28,288]{2,1,0:T(8,128)S(1)} %fusion.17, ...), kind=kLoop, calls=%fused_computation.38 | loop fusion | flops 6547968 | bytes 8129376 | tf_op jit(solution)/shard_map/mul | solution.py:29
  50.7 0.7 %fusion.26 = f32[28,28,288]{2,1,0:T(8,128)S(1)} fusion(f32[28,28,288]{2,1,0:T(8,128)S(1)} %fusion.17, f32[28,28,288]{2,1,0:T(8,128)S(1)} %fusion.22, f32[28,28,35]{2,1,0:T(8,128)S(1)} %slice.783, f32[28,28,253]{2,1,0:T(8,128)S(1)} %slice.782, f32[28,28,287]{2,1,0:T(8,128)S(1)} %bitcast.43, f32[28,28,1]{2,1,0:T(8,128)S(1)} %slice.784, ...), kind=kLoop, calls=%fused_computation.44 | loop fusion | flops 1128960 | bytes 4516128 | tf_op jit(solution)/shard_map/sub | solution.py:63
  51.4 1.4 %fusion.15 = f32[28,25,288]{2,1,0:T(8,128)S(1)} fusion(f32[28,28,288]{2,1,0:T(8,128)S(1)} %fusion.26, f32[32,32,288]{2,1,0:T(8,128)S(1)} %get-tuple-element.9), kind=kLoop, calls=%fused_computation.26 | loop fusion | flops 4435200 | bytes 5644800 | tf_op jit(solution)/shard_map/mul | solution.py:29
  53.1 0.6 fusion.32
  55.3 1.2 %fusion.45 = f32[24,24,288]{2,1,0:T(8,128)S(1)} fusion(f32[24,24,35]{2,1,0:T(8,128)S(1)} %get-tuple-element.19, f32[24,24,253]{2,1,0:T(8,128)S(1)} %get-tuple-element.21, f32[24,24,287]{2,1,0:T(8,128)S(1)} %get-tuple-element.23, f32[24,24,1]{2,1,0:T(8,128)S(1)} %get-tuple-element.25, f32[24,24,288]{2,1,0:T(8,128)S(1)} %fusion.40, ...), kind=kLoop, calls=%fused_computation.76 | loop fusion | flops 4810752 | bytes 5972832 | tf_op jit(solution)/shard_map/mul | solution.py:29
  57.4 0.9 %fusion.38 = f32[24,21,288]{2,1,0:T(8,128)S(1)} fusion(f32[24,24,288]{2,1,0:T(8,128)S(1)} %fusion.49, f32[32,32,288]{2,1,0:T(8,128)S(1)} %get-tuple-element.9), kind=kLoop, calls=%fused_computation.64 | loop fusion | flops 3193344 | bytes 4064256 | tf_op jit(solution)/shard_map/mul | solution.py:29
  58.5 0.5 fusion.54
  60.4 1.1 %fusion.66 = f32[20,20,288]{2,1,0:T(8,128)S(1)} fusion(f32[20,20,35]{2,1,0:T(8,128)S(1)} %get-tuple-element.29, f32[20,20,253]{2,1,0:T(8,128)S(1)} %get-tuple-element.31, f32[20,20,287]{2,1,0:T(8,128)S(1)} %get-tuple-element.33, f32[20,20,1]{2,1,0:T(8,128)S(1)} %get-tuple-element.35, f32[20,20,288]{2,1,0:T(8,128)S(1)} %fusion.61, ...), kind=kLoop, calls=%fused_computation.110 | loop fusion | flops 3340800 | bytes 4148064 | tf_op jit(solution)/shard_map/mul | solution.py:29
  62.3 0.7 %fusion.59 = f32[20,17,288]{2,1,0:T(8,128)S(1)} fusion(f32[20,20,288]{2,1,0:T(8,128)S(1)} %fusion.70, f32[32,32,288]{2,1,0:T(8,128)S(1)} %get-tuple-element.9), kind=kLoop, calls=%fused_computation.98 | loop fusion | flops 2154240 | bytes 2741760 | tf_op jit(solution)/shard_map/mul | solution.py:29
  63.1 0.5 fusion.76
  64.6 0.6 fusion.87
  66.7 1.9 %collective-permute-done.8 = f32[2,16,16]{2,1,0:T(8,128)S(1)} collective-permute-done((f32[2,16,16]{2,1,0:T(8,128)S(1)}, f32[2,16,16]{2,1,0:T(8,128)S(1)}, u32[]{:S(2)}, u32[]{:S(2)}) %collective-permute-start.8) | collective-permute-done | bytes 2080 | tf_op jit(solution)/shard_map/ppermute | solution.py:185
  68.6 2.3 %fusion.80 = f32[16,16,288]{2,1,0:T(8,128)} fusion(f32[16,16,288]{2,1,0:T(8,128)S(1)} %get-tuple-element.7, f32[288]{0:T(512)S(1)} %dynamic_slice.11, f32[16,16]{1,0:T(8,128)S(1)} %convert_element_type.49, f32[16,16]{1,0:T(8,128)S(1)} %get-tuple-element.53, f32[16,16]{1,0:T(8,128)S(1)} %get-tuple-element.52, f32[288]{0:T(512)S(1)} %get-tuple-element.56, ...), kind=kLoop, calls=%fused_computation.131 | loop fusion | flops 811008 | bytes 600576 | tf_op jit(solution)/shard_map/mul | solution.py:104
  (104 shorter events, 11.7 us)
Async XLA Ops:
  0.0 2.5 %copy-start = (f32[8,16]{1,0:T(8,128)S(1)}, f32[8,16]{1,0:T(8,128)}, u32[]{:S(2)}) copy-start(f32[8,16]{1,0:T(8,128)} %param.15) | copy-start | bytes 1540
  0.0 12.8 %copy-start.1 = (f32[16,16,288]{2,1,0:T(8,128)S(1)}, f32[16,16,288]{2,1,0:T(8,128)}, u32[]{:S(2)}) copy-start(f32[16,16,288]{2,1,0:T(8,128)} %param.10) | copy-start | bytes 884740
  3.5 14.9 %copy-start.3 = (f32[16,16]{1,0:T(8,128)S(1)}, f32[16,16]{1,0:T(8,128)}, u32[]{:S(2)}) copy-start(f32[16,16]{1,0:T(8,128)} %param.17) | copy-start | bytes 3076
  3.6 14.8 %collective-permute-start.4 = (f32[16,8,24]{1,2,0:T(8,128)S(1)}, f32[16,8,24]{1,2,0:T(8,128)S(1)}, u32[]{:S(2)}, u32[]{:S(2)}) collective-permute-start(f32[16,8,24]{1,2,0:T(8,128)S(1)} %get-tuple-element.48), channel_id=1, source_target_pairs={{0,16},{16,32},{32,48},{48,64},{64,80},{80,96},{96,112},{112,128},... | collective-permute-start | bytes 36872 | tf_op jit(solution)/shard_map/ppermute | solution.py:112
  6.2 12.2 %collective-permute-start.5 = (f32[16,8,24]{1,2,0:T(8,128)S(1)}, f32[16,8,24]{1,2,0:T(8,128)S(1)}, u32[]{:S(2)}, u32[]{:S(2)}) collective-permute-start(f32[16,8,24]{1,2,0:T(8,128)S(1)} %get-tuple-element.49), channel_id=1, source_target_pairs={{16,0},{32,16},{48,32},{64,48},{80,64},{96,80},{112,96},{128,112},... | collective-permute-start | bytes 36872 | tf_op jit(solution)/shard_map/ppermute | solution.py:113
  13.0 18.1 %collective-permute-start = (f32[16,8,288]{2,1,0:T(8,128)S(1)}, f32[16,8,288]{2,1,0:T(8,128)S(1)}, u32[]{:S(2)}, u32[]{:S(2)}) collective-permute-start(f32[16,8,288]{2,1,0:T(8,128)S(1)} %get-tuple-element.44), channel_id=1, source_target_pairs={{0,16},{16,32},{32,48},{48,64},{64,80},{80,96},{96,112},{112,128},... | collective-permute-start | bytes 442376 | tf_op jit(solution)/shard_map/ppermute | solution.py:112
  13.1 18.0 %collective-permute-start.1 = (f32[16,8,288]{2,1,0:T(8,128)S(1)}, f32[16,8,288]{2,1,0:T(8,128)S(1)}, u32[]{:S(2)}, u32[]{:S(2)}) collective-permute-start(f32[16,8,288]{2,1,0:T(8,128)S(1)} %get-tuple-element.45), channel_id=1, source_target_pairs={{16,0},{32,16},{48,32},{64,48},{80,64},{96,80},{112,96},{128,112},... | collective-permute-start | bytes 442376 | tf_op jit(solution)/shard_map/ppermute | solution.py:113
  18.6 6.8 %collective-permute-start.6 = (f32[8,32,24]{1,2,0:T(8,128)S(1)}, f32[8,32,24]{1,2,0:T(8,128)S(1)}, u32[]{:S(2)}, u32[]{:S(2)}) collective-permute-start(f32[8,32,24]{1,2,0:T(8,128)S(1)} %get-tuple-element.46), channel_id=1, source_target_pairs={{0,2},{2,4},{4,6},{6,8},{8,10},{10,12},{12,14},{1,3},{3,5},{5,7},{... | collective-permute-start | bytes 73736 | tf_op jit(solution)/shard_map/ppermute | solution.py:112
  23.1 5.9 %collective-permute-start.7 = (f32[8,32,24]{1,2,0:T(8,128)S(1)}, f32[8,32,24]{1,2,0:T(8,128)S(1)}, u32[]{:S(2)}, u32[]{:S(2)}) collective-permute-start(f32[8,32,24]{1,2,0:T(8,128)S(1)} %get-tuple-element.47), channel_id=1, source_target_pairs={{2,0},{4,2},{6,4},{8,6},{10,8},{12,10},{14,12},{3,1},{5,3},{7,5},{... | collective-permute-start | bytes 73736 | tf_op jit(solution)/shard_map/ppermute | solution.py:113
  31.2 6.6 %collective-permute-start.2 = (f32[8,32,288]{2,1,0:T(8,128)S(1)}, f32[8,32,288]{2,1,0:T(8,128)S(1)}, u32[]{:S(2)}, u32[]{:S(2)}) collective-permute-start(f32[8,32,288]{2,1,0:T(8,128)S(1)} %get-tuple-element.26), channel_id=1, source_target_pairs={{0,2},{2,4},{4,6},{6,8},{8,10},{10,12},{12,14},{1,3},{3,5},{5,7},{... | collective-permute-start | bytes 884744 | tf_op jit(solution)/shard_map/ppermute | solution.py:112
  33.2 9.1 %collective-permute-start.3 = (f32[8,32,288]{2,1,0:T(8,128)S(1)}, f32[8,32,288]{2,1,0:T(8,128)S(1)}, u32[]{:S(2)}, u32[]{:S(2)}) collective-permute-start(f32[8,32,288]{2,1,0:T(8,128)S(1)} %get-tuple-element.27), channel_id=1, source_target_pairs={{2,0},{4,2},{6,4},{8,6},{10,8},{12,10},{14,12},{3,1},{5,3},{7,5},{... | collective-permute-start | bytes 884744 | tf_op jit(solution)/shard_map/ppermute | solution.py:113
  65.4 1.1 %copy-start.5 = (f32[16]{0:T(128)S(1)}, f32[16]{0:T(128)}, u32[]{:S(2)}) copy-start(f32[16]{0:T(128)} %param.19) | copy-start | bytes 196
  65.4 1.2 %copy-start.4 = (s32[16,16]{1,0:T(8,128)S(1)}, s32[16,16]{1,0:T(8,128)}, u32[]{:S(2)}) copy-start(s32[16,16]{1,0:T(8,128)} %param.12) | copy-start | bytes 3076
  65.4 3.2 %copy-start.2 = (f32[16,16]{1,0:T(8,128)S(1)}, f32[16,16]{1,0:T(8,128)}, u32[]{:S(2)}) copy-start(f32[16,16]{1,0:T(8,128)} %param.18) | copy-start | bytes 3076
  65.9 2.7 %collective-permute-start.8 = (f32[2,16,16]{2,1,0:T(8,128)S(1)}, f32[2,16,16]{2,1,0:T(8,128)S(1)}, u32[]{:S(2)}, u32[]{:S(2)}) collective-permute-start(f32[2,16,16]{2,1,0:T(8,128)S(1)} %pad_maximum_fusion.5), channel_id=1, source_target_pairs={{0,1},{1,0},{2,3},{3,2},{4,5},{5,4},{6,7},{7,6},{8,9},{9,8},{10,11... | collective-permute-start | bytes 6152 | tf_op jit(solution)/shard_map/ppermute | solution.py:185

commit v2 on v1

--- a/solution.py
+++ b/solution.py
@@ -154,9 +154,10 @@
     turn_y = turning * depth_slope[1][..., None]
     density = spectrum * sea_share[..., None]
 
-    fields = jnp.concatenate([group_speed, turn_x, turn_y], axis=-1)
-    density, fields = [exchange(a, "lon", 1, halo, True) for a in (density, fields)]
-    density, fields = [exchange(a, "lat", 0, halo, False) for a in (density, fields)]
+    stacked = jnp.concatenate([density, group_speed, turn_x, turn_y], axis=-1)
+    stacked = exchange(exchange(stacked, "lon", 1, halo, True), "lat", 0, halo, False)
+    density = stacked[..., :comps_dev]
+    fields = stacked[..., comps_dev:]
 
     total_rows = rows_dev * lax.axis_size("lat")
     first_row = lax.axis_index("lat") * rows_dev - halo

time: 71.5 us -> 65.1 us (0.910)
  starting transfers between devices: 25.8 us -> 15.8 us
  waiting for transfers between devices: 11.1 us -> 13 us
  other arithmetic: 20.6 us -> 21.5 us
  local copies, waits for them, and re-layouts: 8.07 us -> 8.95 us
    ppermute x4 -> x2, starting transfers between devices: 16.3 us -> 8.58 us  [exchange(): lax.ppermute(head, axis, [((i + 1) % count, i) for i in range(ends)])]
    ppermute x4 -> x2, waiting for transfers between devices: 1.09 us -> 6.72 us  [exchange(): lax.ppermute(tail, axis, [(i, (i + 1) % count) for i in range(ends)])]
    ppermute x4 -> x2, waiting for transfers between devices: 8.09 us -> 4.4 us  [exchange(): lax.ppermute(head, axis, [((i + 1) % count, i) for i in range(ends)])]
    ppermute x4 -> x2, starting transfers between devices: 9.07 us -> 6.78 us  [exchange(): lax.ppermute(tail, axis, [(i, (i + 1) % count) for i in range(ends)])]
    mul x1, other arithmetic: 0.1 us -> 1.1 us  [per_device(): density = spectrum * sea_share[..., None]]
    slice x16 -> x17, local copies, waits for them, and re-layouts: 2.15 us -> 2.47 us  [rotate(): outer_roll = jnp.roll(density, NDIR - offset, axis=-1)]
    slice x20 -> x21, local copies, waits for them, and re-layouts: 3.53 us -> 3.59 us  [rotate(): inner_roll = jnp.roll(density, -offset, axis=-1)]
  transfers between devices with their start and end apart: 9 -> 5, of which waited for: 4 -> 4; matrix products, arithmetic and copies ran while one was open for 6% -> 1% of each run, Pallas kernels for 0% -> 0%
where the time goes in v2:
time: 65.1 us; the launch traced here: 64.6 us
  other arithmetic  21.5 us (33%)
  starting transfers between devices  15.8 us (24%)
  waiting for transfers between devices  13 us (20%)
  local copies, waits for them, and re-layouts  8.95 us (14%)
  matrix products  4.71 us (7%)
    mul x12, other arithmetic, quickest(): return courant * face_value  12.8 us
    ppermute x2, starting transfers between devices, exchange(): lax.ppermute(head, axis, [((i + 1) % count, i) for i in range(ends)])  8.58 us
    ppermute x2, starting transfers between devices, exchange(): lax.ppermute(tail, axis, [(i, (i + 1) % count) for i in range(ends)])  6.78 us
    ppermute x2, waiting for transfers between devices, exchange(): lax.ppermute(tail, axis, [(i, (i + 1) % count) for i in range(ends)])  6.72 us
    ppermute x2, waiting for transfers between devices, exchange(): lax.ppermute(head, axis, [((i + 1) % count, i) for i in range(ends)])  4.4 us
    slice x21, local copies, waits for them, and re-layouts, rotate(): inner_roll = jnp.roll(density, -offset, axis=-1)  3.59 us
    dot_general x3, matrix products, expand(): return jnp.dot(per_freq, spread, precision=lax.Precision.HIGHEST)  2.72 us
    slice x17, local copies, waits for them, and re-layouts, rotate(): outer_roll = jnp.roll(density, NDIR - offset, axis=-1)  2.47 us
  transfers between devices with their start and end apart: 5, of which 4 were waited for; matrix products, arithmetic and copies ran while one was open for 1% of the time, Pallas kernels for 0%

profile of v2, /device:TPU:1, one launch (start us, length us, event | category | flops | bytes accessed | tf_op | source)
XLA Modules:
  0.0 64.6 jit_solution(5225477253371550690)
XLA Ops:
  0.0 0.7 %convert_element_type.45 = f32[16,16]{1,0:T(8,128)S(1)} convert(s32[16,16]{1,0:T(8,128)} %param.11) | non-fusion elementwise | flops 256 | bytes 2048 | tf_op jit(solution)/shard_map/convert_element_type | solution.py:147
  0.7 0.7 %slice_bitcast_fusion.3 = (f32[16,16]{1,0:T(8,128)S(1)}, f32[16,16]{1,0:T(8,128)S(1)}) fusion(f32[2,16,16]{2,1,0:T(8,128)} %param.16), kind=kLoop, calls=%fused_computation.172 | loop fusion | bytes 4096 | tf_op jit(solution)/shard_map/mul | solution.py:153
  1.4 1.0 %convolution_multiply_fusion.1 = f32[16,16,8]{1,2,0:T(8,128)S(1)} fusion(f32[16,16]{1,0:T(8,128)S(1)} %convert_element_type.45, s32[16,16]{1,0:T(8,128)} %param.13, f32[8,16]{1,0:T(8,128)} %param.14, s32[]{:T(128)S(6)} %select_n.236), kind=kOutput, calls=%fused_computation.46 | convolution fusion | flops 200704 | bytes 10756 | tf_op jit(solution)/shard_map/dot_general | solution.py:72
  2.5 1.0 %broadcast_multiply_fusion.3 = (f32[16,16,8]{1,2,0:T(8,128)S(1)}, f32[16,16,8]{1,2,0:T(8,128)S(1)}) fusion(f32[16,16]{1,0:T(8,128)S(1)} %get-tuple-element.50, f32[16,16]{1,0:T(8,128)S(1)} %get-tuple-element.51, f32[16,16]{1,0:T(8,128)S(1)} %convert_element_type.45, f32[8,16]{1,0:T(8,128)S(1)} %copy-done, s32[]{:T(128)S(6)} %select_n.236, s32[16,16]{1,0:T(8,128)} %param.13), kind=kOutput, calls=%fused_computation.158 | convolution fusion | flops 204800 | bytes 20996 | tf_op jit(solution)/shard_map/dot_general | solution.py:72
  3.7 1.1 %broadcast_multiply_fusion.1 = f32[16,16,288]{2,1,0:T(8,128)S(1)} fusion(f32[16,16,288]{2,1,0:T(8,128)} %param.10, f32[16,16]{1,0:T(8,128)S(1)} %convert_element_type.45), kind=kLoop, calls=%fused_computation.155 | loop fusion | flops 73728 | bytes 590848 | tf_op jit(solution)/shard_map/mul | solution.py:155
  5.1 2.5 %collective-permute-start = (f32[16,8,312]{2,1,0:T(8,128)S(1)}, f32[16,8,312]{2,1,0:T(8,128)S(1)}, u32[]{:S(2)}, u32[]{:S(2)}) collective-permute-start(f32[16,8,312]{2,1,0:T(8,128)S(1)} %get-tuple-element.44), channel_id=1, source_target_pairs={{0,16},{16,32},{32,48},{48,64},{64,80},{80,96},{96,112},{112,128},... | collective-permute-start | bytes 479240 | tf_op jit(solution)/shard_map/ppermute | solution.py:112
  7.6 6.7 %collective-permute-start.1 = (f32[16,8,312]{2,1,0:T(8,128)S(1)}, f32[16,8,312]{2,1,0:T(8,128)S(1)}, u32[]{:S(2)}, u32[]{:S(2)}) collective-permute-start(f32[16,8,312]{2,1,0:T(8,128)S(1)} %get-tuple-element.45), channel_id=1, source_target_pairs={{16,0},{32,16},{48,32},{64,48},{80,64},{96,80},{112,96},{128,112},... | collective-permute-start | bytes 479240 | tf_op jit(solution)/shard_map/ppermute | solution.py:113
  14.8 4.0 %collective-permute-done = f32[16,8,312]{2,1,0:T(8,128)S(1)} collective-permute-done((f32[16,8,312]{2,1,0:T(8,128)S(1)}, f32[16,8,312]{2,1,0:T(8,128)S(1)}, u32[]{:S(2)}, u32[]{:S(2)}) %collective-permute-start) | collective-permute-done | bytes 159776 | tf_op jit(solution)/shard_map/ppermute | solution.py:112
  19.0 4.2 %collective-permute-start.2 = (f32[8,32,312]{2,1,0:T(8,128)S(1)}, f32[8,32,312]{2,1,0:T(8,128)S(1)}, u32[]{:S(2)}, u32[]{:S(2)}) collective-permute-start(f32[8,32,312]{2,1,0:T(8,128)S(1)} %get-tuple-element.26), channel_id=1, source_target_pairs={{0,2},{2,4},{4,6},{6,8},{8,10},{10,12},{12,14},{1,3},{3,5},{5,7},{... | collective-permute-start | bytes 958472 | tf_op jit(solution)/shard_map/ppermute | solution.py:112
  23.3 1.9 %collective-permute-start.3 = (f32[8,32,312]{2,1,0:T(8,128)S(1)}, f32[8,32,312]{2,1,0:T(8,128)S(1)}, u32[]{:S(2)}, u32[]{:S(2)}) collective-permute-start(f32[8,32,312]{2,1,0:T(8,128)S(1)} %get-tuple-element.27), channel_id=1, source_target_pairs={{2,0},{4,2},{6,4},{8,6},{10,8},{12,10},{14,12},{3,1},{5,3},{7,5},{... | collective-permute-start | bytes 958472 | tf_op jit(solution)/shard_map/ppermute | solution.py:113
  25.3 2.7 %collective-permute-done.2 = f32[8,32,312]{2,1,0:T(8,128)S(1)} collective-permute-done((f32[8,32,312]{2,1,0:T(8,128)S(1)}, f32[8,32,312]{2,1,0:T(8,128)S(1)}, u32[]{:S(2)}, u32[]{:S(2)}) %collective-permute-start.2) | collective-permute-done | bytes 319520 | tf_op jit(solution)/shard_map/ppermute | solution.py:112
  28.0 4.4 %collective-permute-done.3 = f32[8,32,312]{2,1,0:T(8,128)S(1)} collective-permute-done((f32[8,32,312]{2,1,0:T(8,128)S(1)}, f32[8,32,312]{2,1,0:T(8,128)S(1)}, u32[]{:S(2)}, u32[]{:S(2)}) %collective-permute-start.3) | collective-permute-done | bytes 319520 | tf_op jit(solution)/shard_map/ppermute | solution.py:113
  32.6 0.8 %fusion.72 = f32[32,32,288]{2,1,0:T(8,128)S(1)} fusion(f32[32,32,312]{2,1,0:T(8,128)S(1)} %pad_maximum_fusion, s32[288]{0:T(512)S(1)} %add_select_fusion.2), kind=kOutput, calls=%fused_computation.118 | convolution fusion | flops 28313856 | bytes 1705984 | tf_op jit(solution)/shard_map/dot_general | solution.py:67
  33.5 0.9 %broadcast_multiply_fusion = (f32[32,32,288]{2,1,0:T(8,128)S(1)}, f32[32,32,288]{2,1,0:T(8,128)S(1)}) fusion(f32[288]{0:T(512)S(1)} %get-tuple-element.56, f32[32]{0:T(128)S(1)} %cosine_divide_fusion, f32[288]{0:T(512)S(1)} %get-tuple-element.57, s32[288]{0:T(512)S(1)} %add_select_fusion.2, f32[32,32,312]{2,1,0:T(8,128)S(1)} %pad_maximum_fusion), kind=kOutput, calls=%fused_computation.84 | convolution fusion | flops 29198592 | bytes 2890240 | tf_op jit(solution)/shard_map/dot_general | solution.py:67
  34.4 1.6 %fusion.5 = f32[32,29,288]{2,1,0:T(8,128)S(1)} fusion(f32[32,32,312]{2,1,0:T(8,128)S(1)} %pad_maximum_fusion, f32[32,32,288]{2,1,0:T(8,128)S(1)} %get-tuple-element.9), kind=kLoop, calls=%fused_computation.7 | loop fusion | flops 5879808 | bytes 7483392 | tf_op jit(solution)/shard_map/mul | solution.py:29
  36.4 1.0 %fusion.10 = f32[29,28,288]{2,1,0:T(8,128)S(1)} fusion(f32[32,28,288]{2,1,0:T(8,128)S(1)} %fusion, f32[32,32,288]{2,1,0:T(8,128)S(1)} %get-tuple-element.8), kind=kLoop, calls=%fused_computation.18 | loop fusion | flops 5144832 | bytes 6547968 | tf_op jit(solution)/shard_map/mul | solution.py:29
  39.0 0.5 fusion.135
  39.5 1.0 %multiply_subtract_fusion = f32[32,32,288]{2,1,0:T(8,128)S(1)} fusion(f32[32,32,288]{2,1,0:T(8,128)S(1)} %fusion.72, f32[288]{0:T(512)S(1)} %get-tuple-element.54, f32[288]{0:T(512)S(1)} %get-tuple-element.55, f32[32,32,312]{2,1,0:T(8,128)S(1)} %pad_maximum_fusion, s32[288]{0:T(512)S(1)} %add_select_fusion.2), kind=kOutput, calls=%fused_computation.11 | convolution fusion | flops 29198592 | bytes 3282944 | tf_op jit(solution)/shard_map/dot_general | solution.py:67
  41.3 2.5 %fusion.22 = f32[28,28,288]{2,1,0:T(8,128)S(1)} fusion(f32[28,28,35]{2,1,0:T(8,128)S(1)} %get-tuple-element.11, f32[28,28,253]{2,1,0:T(8,128)S(1)} %get-tuple-element.13, f32[28,28,287]{2,1,0:T(8,128)S(1)} %get-tuple-element.15, f32[28,28,1]{2,1,0:T(8,128)S(1)} %get-tuple-element.17, f32[28,28,288]{2,1,0:T(8,128)S(1)} %copy-done.2, ...), kind=kLoop, calls=%fused_computation.38 | loop fusion | flops 6547968 | bytes 8129376 | tf_op jit(solution)/shard_map/mul | solution.py:29
  44.4 0.8 %fusion.26 = f32[28,28,288]{2,1,0:T(8,128)S(1)} fusion(f32[28,28,288]{2,1,0:T(8,128)S(1)} %copy-done.2, f32[28,28,288]{2,1,0:T(8,128)S(1)} %fusion.22, f32[28,28,35]{2,1,0:T(8,128)S(1)} %slice.773, f32[28,28,253]{2,1,0:T(8,128)S(1)} %slice.772, f32[28,28,287]{2,1,0:T(8,128)S(1)} %bitcast.43, f32[28,28,1]{2,1,0:T(8,128)S(1)} %slice.774, ...), kind=kLoop, calls=%fused_computation.44 | loop fusion | flops 1128960 | bytes 4516128 | tf_op jit(solution)/shard_map/sub | solution.py:63
  45.2 1.4 %fusion.15 = f32[28,25,288]{2,1,0:T(8,128)S(1)} fusion(f32[28,28,288]{2,1,0:T(8,128)S(1)} %fusion.26, f32[32,32,288]{2,1,0:T(8,128)S(1)} %get-tuple-element.9), kind=kLoop, calls=%fused_computation.26 | loop fusion | flops 4435200 | bytes 5644800 | tf_op jit(solution)/shard_map/mul | solution.py:29
  46.9 0.6 fusion.32
  49.0 1.2 %fusion.45 = f32[24,24,288]{2,1,0:T(8,128)S(1)} fusion(f32[24,24,35]{2,1,0:T(8,128)S(1)} %get-tuple-element.19, f32[24,24,253]{2,1,0:T(8,128)S(1)} %get-tuple-element.21, f32[24,24,287]{2,1,0:T(8,128)S(1)} %get-tuple-element.23, f32[24,24,1]{2,1,0:T(8,128)S(1)} %get-tuple-element.25, f32[24,24,288]{2,1,0:T(8,128)S(1)} %fusion.40, ...), kind=kLoop, calls=%fused_computation.76 | loop fusion | flops 4810752 | bytes 5972832 | tf_op jit(solution)/shard_map/mul | solution.py:29
  50.6 0.5 fusion.49
  51.1 0.9 %fusion.38 = f32[24,21,288]{2,1,0:T(8,128)S(1)} fusion(f32[24,24,288]{2,1,0:T(8,128)S(1)} %fusion.49, f32[32,32,288]{2,1,0:T(8,128)S(1)} %get-tuple-element.9), kind=kLoop, calls=%fused_computation.64 | loop fusion | flops 3193344 | bytes 4064256 | tf_op jit(solution)/shard_map/mul | solution.py:29
  52.3 0.5 fusion.54
  54.1 1.1 %fusion.66 = f32[20,20,288]{2,1,0:T(8,128)S(1)} fusion(f32[20,20,35]{2,1,0:T(8,128)S(1)} %get-tuple-element.29, f32[20,20,253]{2,1,0:T(8,128)S(1)} %get-tuple-element.31, f32[20,20,287]{2,1,0:T(8,128)S(1)} %get-tuple-element.33, f32[20,20,1]{2,1,0:T(8,128)S(1)} %get-tuple-element.35, f32[20,20,288]{2,1,0:T(8,128)S(1)} %fusion.61, ...), kind=kLoop, calls=%fused_computation.110 | loop fusion | flops 3340800 | bytes 4148064 | tf_op jit(solution)/shard_map/mul | solution.py:29
  56.0 0.7 %fusion.59 = f32[20,17,288]{2,1,0:T(8,128)S(1)} fusion(f32[20,20,288]{2,1,0:T(8,128)S(1)} %fusion.70, f32[32,32,288]{2,1,0:T(8,128)S(1)} %get-tuple-element.9), kind=kLoop, calls=%fused_computation.98 | loop fusion | flops 2154240 | bytes 2741760 | tf_op jit(solution)/shard_map/mul | solution.py:29
  56.8 0.5 fusion.81
  58.3 0.6 fusion.92
  60.4 1.9 %collective-permute-done.4 = f32[2,16,16]{2,1,0:T(8,128)S(1)} collective-permute-done((f32[2,16,16]{2,1,0:T(8,128)S(1)}, f32[2,16,16]{2,1,0:T(8,128)S(1)}, u32[]{:S(2)}, u32[]{:S(2)}) %collective-permute-start.4) | collective-permute-done | bytes 2080 | tf_op jit(solution)/shard_map/ppermute | solution.py:186
  62.3 2.3 %fusion.85 = f32[16,16,288]{2,1,0:T(8,128)} fusion(f32[16,16,288]{2,1,0:T(8,128)S(1)} %get-tuple-element.7, f32[288]{0:T(512)S(1)} %dynamic_slice.11, f32[16,16]{1,0:T(8,128)S(1)} %convert_element_type.49, f32[16,16]{1,0:T(8,128)S(1)} %get-tuple-element.49, f32[16,16]{1,0:T(8,128)S(1)} %get-tuple-element.48, f32[288]{0:T(512)S(1)} %get-tuple-element.52, ...), kind=kLoop, calls=%fused_computation.136 | loop fusion | flops 811008 | bytes 600576 | tf_op jit(solution)/shard_map/mul | solution.py:104
  (99 shorter events, 11.4 us)
Async XLA Ops:
  0.0 2.5 %copy-start = (f32[8,16]{1,0:T(8,128)S(1)}, f32[8,16]{1,0:T(8,128)}, u32[]{:S(2)}) copy-start(f32[8,16]{1,0:T(8,128)} %param.15) | copy-start | bytes 1540
  5.1 13.7 %collective-permute-start = (f32[16,8,312]{2,1,0:T(8,128)S(1)}, f32[16,8,312]{2,1,0:T(8,128)S(1)}, u32[]{:S(2)}, u32[]{:S(2)}) collective-permute-start(f32[16,8,312]{2,1,0:T(8,128)S(1)} %get-tuple-element.44), channel_id=1, source_target_pairs={{0,16},{16,32},{32,48},{48,64},{64,80},{80,96},{96,112},{112,128},... | collective-permute-start | bytes 479240 | tf_op jit(solution)/shard_map/ppermute | solution.py:112
  7.6 11.2 %collective-permute-start.1 = (f32[16,8,312]{2,1,0:T(8,128)S(1)}, f32[16,8,312]{2,1,0:T(8,128)S(1)}, u32[]{:S(2)}, u32[]{:S(2)}) collective-permute-start(f32[16,8,312]{2,1,0:T(8,128)S(1)} %get-tuple-element.45), channel_id=1, source_target_pairs={{16,0},{32,16},{48,32},{64,48},{80,64},{96,80},{112,96},{128,112},... | collective-permute-start | bytes 479240 | tf_op jit(solution)/shard_map/ppermute | solution.py:113
  14.8 10.4 %copy-start.4 = (f32[16,16]{1,0:T(8,128)S(1)}, f32[16,16]{1,0:T(8,128)}, u32[]{:S(2)}) copy-start(f32[16,16]{1,0:T(8,128)} %param.17) | copy-start | bytes 3076
  19.0 8.9 %collective-permute-start.2 = (f32[8,32,312]{2,1,0:T(8,128)S(1)}, f32[8,32,312]{2,1,0:T(8,128)S(1)}, u32[]{:S(2)}, u32[]{:S(2)}) collective-permute-start(f32[8,32,312]{2,1,0:T(8,128)S(1)} %get-tuple-element.26), channel_id=1, source_target_pairs={{0,2},{2,4},{4,6},{6,8},{8,10},{10,12},{12,14},{1,3},{3,5},{5,7},{... | collective-permute-start | bytes 958472 | tf_op jit(solution)/shard_map/ppermute | solution.py:112
  23.3 9.1 %collective-permute-start.3 = (f32[8,32,312]{2,1,0:T(8,128)S(1)}, f32[8,32,312]{2,1,0:T(8,128)S(1)}, u32[]{:S(2)}, u32[]{:S(2)}) collective-permute-start(f32[8,32,312]{2,1,0:T(8,128)S(1)} %get-tuple-element.27), channel_id=1, source_target_pairs={{2,0},{4,2},{6,4},{8,6},{10,8},{12,10},{14,12},{3,1},{5,3},{7,5},{... | collective-permute-start | bytes 958472 | tf_op jit(solution)/shard_map/ppermute | solution.py:113
  37.6 1.4 %copy-start.1 = (f32[28,28,288]{2,1,0:T(8,128)}, f32[28,28,288]{2,1,0:T(8,128)S(1)}, u32[]{:S(2)}) copy-start(f32[28,28,288]{2,1,0:T(8,128)S(1)} %fusion.17) | copy-start | bytes 2709508
  39.5 1.3 %copy-start.2 = (f32[28,28,288]{2,1,0:T(8,128)S(1)}, f32[28,28,288]{2,1,0:T(8,128)}, u32[]{:S(2)}) copy-start(f32[28,28,288]{2,1,0:T(8,128)} %copy-done.1) | copy-start | bytes 2709508
  39.5 1.4 %slice-start = ((f32[28,28,288]{2,1,0:T(8,128)}), f32[28,28,2]{2,1,0:T(8,128)S(1)}, s32[]{:S(2)}) async-start(f32[28,28,288]{2,1,0:T(8,128)} %copy-done.1), calls=%async_computation | async-start | bytes 917504 | tf_op jit(solution)/shard_map/jit(_roll_static)/slice | solution.py:53
  39.5 1.8 %slice-start.1 = ((f32[28,28,288]{2,1,0:T(8,128)}), f32[28,28,254]{2,1,0:T(8,128)S(1)}, s32[]{:S(2)}) async-start(f32[28,28,288]{2,1,0:T(8,128)} %copy-done.1), calls=%async_computation.1 | async-start | bytes 1835008 | tf_op jit(solution)/shard_map/jit(_roll_static)/slice | solution.py:55
  59.0 1.1 %copy-start.5 = (s32[16,16]{1,0:T(8,128)S(1)}, s32[16,16]{1,0:T(8,128)}, u32[]{:S(2)}) copy-start(s32[16,16]{1,0:T(8,128)} %param.12) | copy-start | bytes 3076
  59.0 1.1 %copy-start.6 = (f32[16]{0:T(128)S(1)}, f32[16]{0:T(128)}, u32[]{:S(2)}) copy-start(f32[16]{0:T(128)} %param.19) | copy-start | bytes 196
  59.0 3.2 %copy-start.3 = (f32[16,16]{1,0:T(8,128)S(1)}, f32[16,16]{1,0:T(8,128)}, u32[]{:S(2)}) copy-start(f32[16,16]{1,0:T(8,128)} %param.18) | copy-start | bytes 3076
  59.6 2.7 %collective-permute-start.4 = (f32[2,16,16]{2,1,0:T(8,128)S(1)}, f32[2,16,16]{2,1,0:T(8,128)S(1)}, u32[]{:S(2)}, u32[]{:S(2)}) collective-permute-start(f32[2,16,16]{2,1,0:T(8,128)S(1)} %pad_maximum_fusion.3), channel_id=1, source_target_pairs={{0,1},{1,0},{2,3},{3,2},{4,5},{5,4},{6,7},{7,6},{8,9},{9,8},{10,11... | collective-permute-start | bytes 6152 | tf_op jit(solution)/shard_map/ppermute | solution.py:186

commit v3 on v2

--- a/solution.py
+++ b/solution.py
@@ -1,8 +1,11 @@
+import functools
 import math
 
 import jax
 import jax.numpy as jnp
 from jax import lax
+from jax.experimental import pallas as pl
+from jax.experimental.pallas import tpu as pltpu
 from jax.sharding import PartitionSpec as P
 
 NDIR = 36
@@ -102,6 +105,98 @@
     )
     damping = ice_share[..., None] * ice_loss
     return sea_share[..., None] * density * jnp.exp(growth - breaking - damping)
+
+
+INTERPRET = False
+
+
+def face_flux(behind, center, forward, beyond, courant, weight):
+    curvature = jnp.where(
+        courant >= 0.0, forward - 2.0 * center + behind, beyond - 2.0 * forward + center
+    )
+    face_value = 0.5 * (center + forward) - 0.5 * courant * (forward - center) - weight * curvature
+    return courant * face_value
+
+
+def propagate_kernel(
+    tab_ref, q_ref, gs_ref, tx_ref, ty_ref, st_ref, in_ref, out_ref,
+    kx_ref, wx_ref, ky_ref, wy_ref, kt_ref, wt_ref, f_ref, *, width
+):
+    ndir, _, npos = q_ref.shape
+
+    def pick(x, s):
+        return pltpu.roll(x, (-s) % npos, 1)
+
+    def prev(d):
+        return (d + ndir - 1) % ndir
+
+    def coefficients(d, carry):
+        gs = gs_ref[...]
+        ax = gs * tab_ref[0, d] * st_ref[...]
+        ay = gs * tab_ref[1, d]
+        kx = 0.5 * (ax + pick(ax, 1))
+        ky = 0.5 * (ay + pick(ay, width))
+        kt = tx_ref[...] * tab_ref[2, d] - ty_ref[...] * tab_ref[3, d]
+        kx_ref[d] = kx
+        ky_ref[d] = ky
+        kt_ref[d] = kt
+        wx_ref[d] = (1.0 - kx * kx) / 6.0
+        wy_ref[d] = (1.0 - ky * ky) / 6.0
+        wt_ref[d] = (1.0 - kt * kt) / 6.0
+        return carry
+
+    lax.fori_loop(0, ndir, coefficients, 0)
+    inside = jnp.broadcast_to(in_ref[...] > 0.5, q_ref.shape[1:])
+
+    def sweep(q, step, k, w):
+        flux = face_flux(pick(q, -step), q, pick(q, step), pick(q, 2 * step), k, w)
+        return q - (flux - pick(flux, -step))
+
+    for substep in range(ITERS):
+        source = q_ref if substep == 0 else out_ref
+
+        def spatial(d, carry):
+            q = source[d]
+            if substep > 0:
+                q = q - (f_ref[d] - f_ref[prev(d)])
+            q = sweep(q, 1, kx_ref[d], wx_ref[d])
+            q = sweep(q, width, ky_ref[d], wy_ref[d])
+            out_ref[d] = jnp.where(inside, q, 0.0)
+            return carry
+
+        lax.fori_loop(0, ndir, spatial, 0)
+
+        def directional(d, carry):
+            f_ref[d] = face_flux(
+                out_ref[prev(d)],
+                out_ref[d],
+                out_ref[(d + 1) % ndir],
+                out_ref[(d + 2) % ndir],
+                kt_ref[d],
+                wt_ref[d],
+            )
+            return carry
+
+        lax.fori_loop(0, ndir, directional, 0)
+
+    def finish(d, carry):
+        out_ref[d] = out_ref[d] - (f_ref[d] - f_ref[prev(d)])
+        return carry
+
+    lax.fori_loop(0, ndir, finish, 0)
+
+
+def propagate(tables, q, gs, tx, ty, st, inside, width):
+    vmem = pl.BlockSpec(memory_space=pltpu.VMEM)
+    scratch = [pltpu.VMEM(q.shape, jnp.float32) for _ in range(7)]
+    return pl.pallas_call(
+        functools.partial(propagate_kernel, width=width),
+        out_shape=jax.ShapeDtypeStruct(q.shape, jnp.float32),
+        in_specs=[pl.BlockSpec(memory_space=pltpu.SMEM)] + [vmem] * 6,
+        out_specs=vmem,
+        scratch_shapes=scratch,
+        interpret=INTERPRET,
+    )(tables, q, gs, tx, ty, st, inside)
 
 
 def exchange(cells, axis, dim, width, closed):
@@ -161,24 +256,22 @@
 
     total_rows = rows_dev * lax.axis_size("lat")
     first_row = lax.axis_index("lat") * rows_dev - halo
-    rows_ext = first_row + jnp.arange(rows_dev + 2 * halo)
-    inside = ((rows_ext >= 0) & (rows_ext < total_rows))[:, None, None]
-    stretch_rows = stretch(rows_ext, total_rows)
-    gs_ext = expand(fields[..., :freqs_dev], spread)
-    along_x = gs_ext * cos_head * stretch_rows[:, None, None]
-    along_y = gs_ext * sin_head
-    along_t = (
-        expand(fields[..., freqs_dev : 2 * freqs_dev], spread) * sin_face
-        - expand(fields[..., 2 * freqs_dev :], spread) * cos_face
-    )
-    for substep in range(ITERS):
-        density = advect(density, along_x, 1)
-        along_x, along_y, along_t = [trim(a, 1, 2) for a in (along_x, along_y, along_t)]
-        density = advect(density, along_y, 0)
-        inside = trim(inside, 0, 2)
-        density = jnp.where(inside, density, 0.0)
-        along_x, along_y, along_t = [trim(a, 0, 2) for a in (along_x, along_y, along_t)]
-        density = refract(density, along_t)
+    rows_ext, cols_ext = stacked.shape[:2]
+    rows_at = first_row + jnp.arange(rows_ext)
+    inside = ((rows_at >= 0) & (rows_at < total_rows)).astype(jnp.float32)
+    positions = rows_ext * cols_ext
+    per_pos = lambda v: jnp.repeat(v, cols_ext).reshape(1, positions)
+    tables = jnp.stack([cos_head, sin_head, sin_face, cos_face])[:, :NDIR]
+    by_dir = density.reshape(positions, freqs_dev, NDIR).transpose(2, 1, 0)
+    by_freq = [
+        fields[..., i * freqs_dev : (i + 1) * freqs_dev].reshape(positions, freqs_dev).T
+        for i in range(3)
+    ]
+    moved = propagate(
+        tables, by_dir, *by_freq, per_pos(stretch(rows_at, total_rows)), per_pos(inside), cols_ext
+    )
+    density = moved.transpose(2, 1, 0).reshape(rows_ext, cols_ext, comps_dev)
+    density = density[halo : halo + rows_dev, halo : halo + cols_dev]
 
     levels = jnp.exp(math.log(freq_ratio) * (comp_index // NDIR).astype(jnp.float32))
     ice_loss = lax.dynamic_slice_in_dim(jnp.repeat(ice_rate, NDIR), first_comp, comps_dev, 0)

time: 65.1 us -> 116 us (1.78)
  the two profiles are of different devices: /device:TPU:1 before, /device:TPU:2 now
where the time goes in v3:
time: 116 us; the launch traced here: 114 us
  Pallas kernels  60.8 us (52%)
  local copies, waits for them, and re-layouts  19.8 us (17%)
  starting transfers between devices  15 us (13%)
  waiting for transfers between devices  10.5 us (9%)
  other arithmetic  5.7 us (5%)
  matrix products  1.99 us (2%)
    pallas_call x1, Pallas kernels, propagate(): pl.pallas_call(functools.partial(propagate_kernel, width=width), out_shap...  60.8 us
    ppermute x2, starting transfers between devices, exchange(): lax.ppermute(head, axis, [((i + 1) % count, i) for i in range(ends)])  10.3 us
    reshape x2, local copies, waits for them, and re-layouts, per_device(): by_dir = density.reshape(positions, freqs_dev, NDIR).transpose(2, 1, 0)  6.88 us
    ppermute x2, waiting for transfers between devices, exchange(): lax.ppermute(tail, axis, [(i, (i + 1) % count) for i in range(ends)])  5.99 us
    ppermute x2, starting transfers between devices, exchange(): lax.ppermute(tail, axis, [(i, (i + 1) % count) for i in range(ends)])  3.91 us
    transpose x1, local copies, waits for them, and re-layouts, per_device(): density = moved.transpose(2, 1, 0).reshape(rows_ext, cols_ext, comps_dev)  3.82 us
    reshape x1, local copies, waits for them, and re-layouts, per_device(): density = moved.transpose(2, 1, 0).reshape(rows_ext, cols_ext, comps_dev)  3.5 us
    ppermute x1, waiting for transfers between devices, per_device(): other = lax.ppermute(partial, 'band', [(0, 1), (1, 0)])  2.77 us
  transfers between devices with their start and end apart: 5, of which 4 were waited for; matrix products, arithmetic and copies ran while one was open for 2% of the time, Pallas kernels for 0%

profile of v3, /device:TPU:2, one launch (start us, length us, event | category | flops | bytes accessed | tf_op | source)
XLA Modules:
  0.0 114.1 jit_solution(4396849198079189054)
XLA Ops:
  0.0 0.7 convert_element_type.52
  0.7 0.7 slice_bitcast_fusion.3
  1.4 1.0 convolution_multiply_fusion.1
  2.5 1.0 broadcast_multiply_fusion.2
  3.6 0.1 copy.23
  3.7 1.1 broadcast_multiply_fusion
  4.8 0.2 pad_maximum_fusion.2
  5.1 2.0 %collective-permute-start = (f32[16,8,312]{2,1,0:T(8,128)S(1)}, f32[16,8,312]{2,1,0:T(8,128)S(1)}, u32[]{:S(2)}, u32[]{:S(2)}) collective-permute-start(f32[16,8,312]{2,1,0:T(8,128)S(1)} %get-tuple-element.12), channel_id=1, source_target_pairs={{0,16},{16,32},{32,48},{48,64},{64,80},{80,96},{96,112},{112,128},... | collective-permute-start | bytes 479240 | tf_op jit(solution)/shard_map/ppermute | solution.py:207
  7.1 6.7 %collective-permute-start.1 = (f32[16,8,312]{2,1,0:T(8,128)S(1)}, f32[16,8,312]{2,1,0:T(8,128)S(1)}, u32[]{:S(2)}, u32[]{:S(2)}) collective-permute-start(f32[16,8,312]{2,1,0:T(8,128)S(1)} %get-tuple-element.13), channel_id=1, source_target_pairs={{16,0},{32,16},{48,32},{64,48},{80,64},{96,80},{112,96},{128,112},... | collective-permute-start | bytes 479240 | tf_op jit(solution)/shard_map/ppermute | solution.py:208
  13.9 0.7 reshape_reshape.6.st_ref
  14.7 0.7 reshape_reshape.7.in_ref
  15.5 3.1 %collective-permute-done = f32[16,8,312]{2,1,0:T(8,128)S(1)} collective-permute-done((f32[16,8,312]{2,1,0:T(8,128)S(1)}, f32[16,8,312]{2,1,0:T(8,128)S(1)}, u32[]{:S(2)}, u32[]{:S(2)}) %collective-permute-start) | collective-permute-done | bytes 159776 | tf_op jit(solution)/shard_map/ppermute | solution.py:207
  18.5 0.2 pad_maximum_fusion.1
  18.8 1.9 %collective-permute-start.2 = (f32[8,32,312]{2,1,0:T(8,128)S(1)}, f32[8,32,312]{2,1,0:T(8,128)S(1)}, u32[]{:S(2)}, u32[]{:S(2)}) collective-permute-start(f32[8,32,312]{2,1,0:T(8,128)S(1)} %get-tuple-element.10), channel_id=1, source_target_pairs={{0,2},{2,4},{4,6},{6,8},{8,10},{10,12},{12,14},{1,3},{3,5},{5,7},{... | collective-permute-start | bytes 958472 | tf_op jit(solution)/shard_map/ppermute | solution.py:207
  20.7 3.6 %collective-permute-start.3 = (f32[8,32,312]{2,1,0:T(8,128)S(1)}, f32[8,32,312]{2,1,0:T(8,128)S(1)}, u32[]{:S(2)}, u32[]{:S(2)}) collective-permute-start(f32[8,32,312]{2,1,0:T(8,128)S(1)} %get-tuple-element.11), channel_id=1, source_target_pairs={{2,0},{4,2},{6,4},{8,6},{10,8},{12,10},{14,12},{3,1},{5,3},{7,5},{... | collective-permute-start | bytes 958472 | tf_op jit(solution)/shard_map/ppermute | solution.py:208
  24.3 0.6 pad_maximum_fusion.4.tab_ref
  24.9 2.9 %collective-permute-done.2 = f32[8,32,312]{2,1,0:T(8,128)S(1)} collective-permute-done((f32[8,32,312]{2,1,0:T(8,128)S(1)}, f32[8,32,312]{2,1,0:T(8,128)S(1)}, u32[]{:S(2)}, u32[]{:S(2)}) %collective-permute-start.2) | collective-permute-done | bytes 319520 | tf_op jit(solution)/shard_map/ppermute | solution.py:207
  27.9 1.8 %collective-permute-done.3 = f32[8,32,312]{2,1,0:T(8,128)S(1)} collective-permute-done((f32[8,32,312]{2,1,0:T(8,128)S(1)}, f32[8,32,312]{2,1,0:T(8,128)S(1)}, u32[]{:S(2)}, u32[]{:S(2)}) %collective-permute-start.3) | collective-permute-done | bytes 319520 | tf_op jit(solution)/shard_map/ppermute | solution.py:208
  29.6 0.2 pad_maximum_fusion
  29.9 0.5 fusion.27
  30.3 0.8 copy.31
  31.1 0.8 copy.30
  31.9 0.8 copy.29
  32.7 2.9 %reshape.127 = f32[1024,8,36]{2,1,0:T(8,128)} reshape(f32[32,32,288]{2,1,0:T(8,128)S(1)} %bitcast.41) | data formatting | bytes 2359296 | tf_op jit(solution)/shard_map/reshape | solution.py:265
  35.6 4.0 %copy.24 = f32[1024,8,36]{0,1,2:T(8,128)} copy(f32[1024,8,36]{2,1,0:T(8,128)} %reshape.127) | data formatting | bytes 2359296 | tf_op jit(solution)/shard_map/reshape | solution.py:265
  39.6 60.8 %shard_map.100 = f32[36,8,1024]{2,1,0:T(8,128)} custom-call(f32[4,36]{1,0:T(4,128)} %pad_maximum_fusion.4.tab_ref, f32[36,8,1024]{2,1,0:T(8,128)} %bitcast.42, f32[8,1024]{1,0:T(8,128)} %bitcast.49, f32[8,1024]{1,0:T(8,128)} %bitcast.48, f32[8,1024]{1,0:T(8,128)} %bitcast.47, f32[1,1024]{1,0:T(1,128)} %reshape_reshape.6.st_ref, f32[1,1024]{1,0:T(1,128)} %reshape_reshape.7.in_ref), custom_call_target="tpu_custom_call" | custom-call | tf_op jit(solution)/shard_map/pallas_call | solution.py:192
  100.4 3.8 %copy.28 = f32[1024,8,36]{2,1,0:T(8,128)} copy(f32[1024,8,36]{0,1,2:T(8,128)} %bitcast.43) | data formatting | bytes 2359296 | tf_op jit(solution)/shard_map/transpose | solution.py:273
  104.2 3.5 %reshape.131 = f32[32,32,288]{2,1,0:T(8,128)S(1)} reshape(f32[1024,8,36]{2,1,0:T(8,128)} %copy.28) | data formatting | bytes 2359296 | tf_op jit(solution)/shard_map/reshape | solution.py:273
  107.7 0.1 multiply_reduce_fusion
  107.9 0.8 collective-permute-start.4
  108.9 2.8 %collective-permute-done.4 = f32[2,16,16]{2,1,0:T(8,128)S(1)} collective-permute-done((f32[2,16,16]{2,1,0:T(8,128)S(1)}, f32[2,16,16]{2,1,0:T(8,128)S(1)}, u32[]{:S(2)}, u32[]{:S(2)}) %collective-permute-start.4) | collective-permute-done | bytes 2080 | tf_op jit(solution)/shard_map/ppermute | solution.py:279
  111.7 2.3 %fusion.3 = f32[16,16,288]{2,1,0:T(8,128)} fusion(f32[32,32,288]{2,1,0:T(8,128)S(1)} %reshape.131, f32[288]{0:T(512)S(1)} %dynamic_slice.11, f32[16,16]{1,0:T(8,128)S(1)} %convert_element_type.58, f32[16,16]{1,0:T(8,128)S(1)} %get-tuple-element.17, f32[16,16]{1,0:T(8,128)S(1)} %get-tuple-element.16, f32[288]{0:T(512)S(1)} %get-tuple-element.20, ...), kind=kLoop, calls=%fused_computation.8 | loop fusion | flops 811008 | bytes 600576 | tf_op jit(solution)/shard_map/mul | solution.py:107
  (30 shorter events, 0.9 us)
Async XLA Ops:
  0.0 2.5 %copy-start = (f32[8,16]{1,0:T(8,128)S(1)}, f32[8,16]{1,0:T(8,128)}, u32[]{:S(2)}) copy-start(f32[8,16]{1,0:T(8,128)} %param.15) | copy-start | bytes 1540
  5.1 13.5 %collective-permute-start = (f32[16,8,312]{2,1,0:T(8,128)S(1)}, f32[16,8,312]{2,1,0:T(8,128)S(1)}, u32[]{:S(2)}, u32[]{:S(2)}) collective-permute-start(f32[16,8,312]{2,1,0:T(8,128)S(1)} %get-tuple-element.12), channel_id=1, source_target_pairs={{0,16},{16,32},{32,48},{48,64},{64,80},{80,96},{96,112},{112,128},... | collective-permute-start | bytes 479240 | tf_op jit(solution)/shard_map/ppermute | solution.py:207
  7.1 11.5 %collective-permute-start.1 = (f32[16,8,312]{2,1,0:T(8,128)S(1)}, f32[16,8,312]{2,1,0:T(8,128)S(1)}, u32[]{:S(2)}, u32[]{:S(2)}) collective-permute-start(f32[16,8,312]{2,1,0:T(8,128)S(1)} %get-tuple-element.13), channel_id=1, source_target_pairs={{16,0},{32,16},{48,32},{64,48},{80,64},{96,80},{112,96},{128,112},... | collective-permute-start | bytes 479240 | tf_op jit(solution)/shard_map/ppermute | solution.py:208
  15.5 9.5 %copy-start.2 = (f32[16,16]{1,0:T(8,128)S(1)}, f32[16,16]{1,0:T(8,128)}, u32[]{:S(2)}) copy-start(f32[16,16]{1,0:T(8,128)} %param.17) | copy-start | bytes 3076
  18.8 9.1 %collective-permute-start.2 = (f32[8,32,312]{2,1,0:T(8,128)S(1)}, f32[8,32,312]{2,1,0:T(8,128)S(1)}, u32[]{:S(2)}, u32[]{:S(2)}) collective-permute-start(f32[8,32,312]{2,1,0:T(8,128)S(1)} %get-tuple-element.10), channel_id=1, source_target_pairs={{0,2},{2,4},{4,6},{6,8},{8,10},{10,12},{12,14},{1,3},{3,5},{5,7},{... | collective-permute-start | bytes 958472 | tf_op jit(solution)/shard_map/ppermute | solution.py:207
  20.7 8.9 %collective-permute-start.3 = (f32[8,32,312]{2,1,0:T(8,128)S(1)}, f32[8,32,312]{2,1,0:T(8,128)S(1)}, u32[]{:S(2)}, u32[]{:S(2)}) collective-permute-start(f32[8,32,312]{2,1,0:T(8,128)S(1)} %get-tuple-element.11), channel_id=1, source_target_pairs={{2,0},{4,2},{6,4},{8,6},{10,8},{12,10},{14,12},{3,1},{5,3},{7,5},{... | collective-permute-start | bytes 958472 | tf_op jit(solution)/shard_map/ppermute | solution.py:208
  104.2 4.5 %copy-start.3 = (s32[16,16]{1,0:T(8,128)S(1)}, s32[16,16]{1,0:T(8,128)}, u32[]{:S(2)}) copy-start(s32[16,16]{1,0:T(8,128)} %param.12) | copy-start | bytes 3076
  104.2 4.5 %copy-start.4 = (f32[16]{0:T(128)S(1)}, f32[16]{0:T(128)}, u32[]{:S(2)}) copy-start(f32[16]{0:T(128)} %param.19) | copy-start | bytes 196
  104.2 7.5 %copy-start.1 = (f32[16,16]{1,0:T(8,128)S(1)}, f32[16,16]{1,0:T(8,128)}, u32[]{:S(2)}) copy-start(f32[16,16]{1,0:T(8,128)} %param.18) | copy-start | bytes 3076
  107.9 3.8 %collective-permute-start.4 = (f32[2,16,16]{2,1,0:T(8,128)S(1)}, f32[2,16,16]{2,1,0:T(8,128)S(1)}, u32[]{:S(2)}, u32[]{:S(2)}) collective-permute-start(f32[2,16,16]{2,1,0:T(8,128)S(1)} %pad_maximum_fusion.3), channel_id=1, source_target_pairs={{0,1},{1,0},{2,3},{3,2},{4,5},{5,4},{6,7},{7,6},{8,9},{9,8},{10,11... | collective-permute-start | bytes 6152 | tf_op jit(solution)/shard_map/ppermute | solution.py:279

commit v4 on v2

--- a/solution.py
+++ b/solution.py
@@ -1,8 +1,11 @@
+import functools
 import math
 
 import jax
 import jax.numpy as jnp
 from jax import lax
+from jax.experimental import pallas as pl
+from jax.experimental.pallas import tpu as pltpu
 from jax.sharding import PartitionSpec as P
 
 NDIR = 36
@@ -102,6 +105,87 @@
     )
     damping = ice_share[..., None] * ice_loss
     return sea_share[..., None] * density * jnp.exp(growth - breaking - damping)
+
+
+INTERPRET = False
+MESH_ID = pl.DeviceIdType.MESH
+OFFSETS = [(a, b) for a in (-1, 0, 1) for b in (-1, 0, 1) if (a, b) != (0, 0)]
+
+
+def halo_kernel(in_ref, out_ref, send_sem, recv_sem, *, halo):
+    lon = lax.axis_index("lon")
+    lat = lax.axis_index("lat")
+    nlon = lax.axis_size("lon")
+    nlat = lax.axis_size("lat")
+    rows, cols = in_ref.shape[:2]
+
+    def target(a, b):
+        return {"lon": lax.rem(lon + b + nlon, nlon), "lat": lat + a}
+
+    def has(a):
+        return jnp.logical_and(lat + a >= 0, lat + a < nlat)
+
+    def span(a, size):
+        if a == 1:
+            return pl.ds(size - halo, halo), pl.ds(0, halo)
+        if a == -1:
+            return pl.ds(0, halo), pl.ds(size + halo, halo)
+        return pl.ds(0, size), pl.ds(halo, size)
+
+    barrier = pltpu.get_barrier_semaphore()
+    for a, b in OFFSETS:
+
+        @pl.when(has(a))
+        def _():
+            pl.semaphore_signal(barrier, inc=1, device_id=target(a, b), device_id_type=MESH_ID)
+
+    below = (lat + nlat - 1) // nlat
+    above = 1 - lat // (nlat - 1)
+    pl.semaphore_wait(barrier, 3 * (1 + below + above) - 1)
+
+    copies = []
+    for k, (a, b) in enumerate(OFFSETS):
+        rows_src, rows_dst = span(a, rows)
+        cols_src, cols_dst = span(b, cols)
+        copy = pltpu.make_async_remote_copy(
+            src_ref=in_ref.at[rows_src, cols_src],
+            dst_ref=out_ref.at[rows_dst, cols_dst],
+            send_sem=send_sem.at[k],
+            recv_sem=recv_sem.at[k],
+            device_id=target(a, b),
+            device_id_type=MESH_ID,
+        )
+        pl.when(has(a))(copy.start)
+        copies.append((a, copy))
+
+    out_ref[pl.ds(halo, rows), pl.ds(halo, cols)] = in_ref[...]
+    ghost = jnp.zeros((halo,) + out_ref.shape[1:], out_ref.dtype)
+
+    @pl.when(lat == 0)
+    def _():
+        out_ref[pl.ds(0, halo)] = ghost
+
+    @pl.when(lat == nlat - 1)
+    def _():
+        out_ref[pl.ds(rows + halo, halo)] = ghost
+
+    for a, copy in copies:
+        pl.when(has(a))(copy.wait_send)
+        pl.when(has(-a))(copy.wait_recv)
+
+
+def halo_exchange(cells, halo):
+    rows, cols, chans = cells.shape
+    vmem = pl.BlockSpec(memory_space=pltpu.VMEM)
+    return pl.pallas_call(
+        functools.partial(halo_kernel, halo=halo),
+        out_shape=jax.ShapeDtypeStruct((rows + 2 * halo, cols + 2 * halo, chans), cells.dtype),
+        in_specs=[vmem],
+        out_specs=vmem,
+        scratch_shapes=[pltpu.SemaphoreType.DMA((8,)), pltpu.SemaphoreType.DMA((8,))],
+        compiler_params=pltpu.CompilerParams(collective_id=0, has_side_effects=True),
+        interpret=pltpu.InterpretParams(detect_races=True) if INTERPRET else False,
+    )(cells)
 
 
 def exchange(cells, axis, dim, width, closed):
@@ -155,7 +239,7 @@
     density = spectrum * sea_share[..., None]
 
     stacked = jnp.concatenate([density, group_speed, turn_x, turn_y], axis=-1)
-    stacked = exchange(exchange(stacked, "lon", 1, halo, True), "lat", 0, halo, False)
+    stacked = halo_exchange(stacked, halo)
     density = stacked[..., :comps_dev]
     fields = stacked[..., comps_dev:]
 

time: 65.1 us -> 63.3 us (0.972)
  the two profiles are of different devices: /device:TPU:1 before, /device:TPU:2 now
where the time goes in v4:
time: 63.3 us; the launch traced here: 62.7 us
  Pallas kernels  22.2 us (35%)
  other arithmetic  21.8 us (34%)
  local copies, waits for them, and re-layouts  8.7 us (14%)
  matrix products  5.88 us (9%)
  waiting for transfers between devices  2.76 us (4%)
  starting transfers between devices  0.76 us (1%)
    pallas_call x1, Pallas kernels, halo_exchange(): pl.pallas_call(functools.partial(halo_kernel, halo=halo), out_shape=jax.S...  22.2 us
    mul x12, other arithmetic, quickest(): return courant * face_value  12.8 us
    dot_general x3, matrix products, expand(): return jnp.dot(per_freq, spread, precision=lax.Precision.HIGHEST)  3.88 us
    slice x21, local copies, waits for them, and re-layouts, rotate(): inner_roll = jnp.roll(density, -offset, axis=-1)  3.61 us
    ppermute x1, waiting for transfers between devices, per_device(): other = lax.ppermute(partial, 'band', [(0, 1), (1, 0)])  2.76 us
    slice x17, local copies, waits for them, and re-layouts, rotate(): outer_roll = jnp.roll(density, NDIR - offset, axis=-1)  2.55 us
    mul x1, other arithmetic, sources(): return sea_share[..., None] * density * jnp.exp(growth - breaking - damping)  2.34 us
    dot_general x2, matrix products, lookup(): return jnp.dot(onehot, lookup_table, precision=lax.Precision.HIGHEST)  2 us
  transfers between devices with their start and end apart: 1, of which 1 were waited for; matrix products, arithmetic and copies ran while one was open for 0% of the time, Pallas kernels for 0%

profile of v4, /device:TPU:2, one launch (start us, length us, event | category | flops | bytes accessed | tf_op | source)
XLA Modules:
  0.0 62.7 jit_solution(14106580064661626674)
XLA Ops:
  0.6 0.7 %convert_element_type.45 = f32[16,16]{1,0:T(8,128)S(1)} convert(s32[16,16]{1,0:T(8,128)} %param.11) | non-fusion elementwise | flops 256 | bytes 2048 | tf_op jit(solution)/shard_map/convert_element_type | solution.py:231
  1.3 0.7 %slice_bitcast_fusion.3 = (f32[16,16]{1,0:T(8,128)S(1)}, f32[16,16]{1,0:T(8,128)S(1)}) fusion(f32[2,16,16]{2,1,0:T(8,128)} %param.16), kind=kLoop, calls=%fused_computation.165 | loop fusion | bytes 4096 | tf_op jit(solution)/shard_map/mul | solution.py:237
  2.0 1.1 %broadcast_multiply_fusion.1 = f32[16,16,288]{2,1,0:T(8,128)S(1)} fusion(f32[16,16,288]{2,1,0:T(8,128)} %param.10, f32[16,16]{1,0:T(8,128)S(1)} %convert_element_type.45), kind=kLoop, calls=%fused_computation.147 | loop fusion | flops 73728 | bytes 590848 | tf_op jit(solution)/shard_map/mul | solution.py:239
  3.1 1.0 %convolution_multiply_fusion.1 = f32[16,16,8]{2,1,0:T(8,128)S(1)} fusion(f32[16,16]{1,0:T(8,128)S(1)} %convert_element_type.45, s32[16,16]{1,0:T(8,128)} %param.13, f32[8,16]{1,0:T(8,128)} %param.14, s32[]{:T(128)S(6)} %select_n.236), kind=kOutput, calls=%fused_computation.39 | convolution fusion | flops 202752 | bytes 10756 | tf_op jit(solution)/shard_map/dot_general | solution.py:75
  4.1 1.0 %broadcast_multiply_fusion.3 = (f32[16,16,8]{2,1,0:T(8,128)S(1)}, f32[16,16,8]{2,1,0:T(8,128)S(1)}) fusion(f32[16,16]{1,0:T(8,128)S(1)} %get-tuple-element.46, f32[16,16]{1,0:T(8,128)S(1)} %get-tuple-element.47, f32[16,16]{1,0:T(8,128)S(1)} %convert_element_type.45, f32[8,16]{1,0:T(8,128)S(1)} %copy-done, s32[]{:T(128)S(6)} %select_n.236, s32[16,16]{1,0:T(8,128)} %param.13), kind=kOutput, calls=%fused_computation.149 | convolution fusion | flops 206848 | bytes 20996 | tf_op jit(solution)/shard_map/dot_general | solution.py:75
  5.1 0.9 %pad_maximum_fusion.in_ref = f32[16,16,312]{2,1,0:T(8,128)} fusion(f32[16,16,8]{2,1,0:T(8,128)S(1)} %get-tuple-element.43, f32[16,16,8]{2,1,0:T(8,128)S(1)} %get-tuple-element.42, f32[16,16,8]{2,1,0:T(8,128)S(1)} %convolution_multiply_fusion.1, f32[16,16,288]{2,1,0:T(8,128)S(1)} %broadcast_multiply_fusion.1), kind=kLoop, calls=%fused_computation.132 | loop fusion | flops 239616 | bytes 638976 | tf_op jit(solution)/shard_map/concatenate | solution.py:241
  6.1 22.2 %shard_map.100 = f32[32,32,312]{2,1,0:T(8,128)} custom-call(f32[16,16,312]{2,1,0:T(8,128)} %pad_maximum_fusion.in_ref), custom_call_target="tpu_custom_call" | custom-call | tf_op jit(solution)/shard_map/pallas_call | solution.py:180
  28.3 2.0 %fusion.67 = f32[32,32,288]{2,1,0:T(8,128)S(1)} fusion(f32[32,32,312]{2,1,0:T(8,128)} %shard_map.100, s32[288]{0:T(512)S(1)} %add_select_fusion.2), kind=kOutput, calls=%fused_computation.110 | convolution fusion | flops 28313856 | bytes 1705088 | tf_op jit(solution)/shard_map/dot_general | solution.py:70
  30.3 0.9 %broadcast_multiply_fusion = (f32[32,32,288]{2,1,0:T(8,128)S(1)}, f32[32,32,288]{2,1,0:T(8,128)S(1)}) fusion(f32[288]{0:T(512)S(1)} %get-tuple-element.53, f32[32]{0:T(128)S(1)} %cosine_divide_fusion, f32[288]{0:T(512)S(1)} %fusion.127, s32[288]{0:T(512)S(1)} %add_select_fusion.2, f32[32,32,312]{2,1,0:T(8,128)S(1)} %copy-done.3), kind=kOutput, calls=%fused_computation.76 | convolution fusion | flops 29198592 | bytes 2890240 | tf_op jit(solution)/shard_map/dot_general | solution.py:70
  31.3 1.6 %subtract_multiply_fusion = f32[32,29,288]{2,1,0:T(8,128)S(1)} fusion(f32[32,32,312]{2,1,0:T(8,128)S(1)} %copy-done.3, f32[32,32,288]{2,1,0:T(8,128)S(1)} %get-tuple-element.9), kind=kLoop, calls=%fused_computation.4 | loop fusion | flops 5879808 | bytes 7483392 | tf_op jit(solution)/shard_map/mul | solution.py:32
  33.3 1.0 %fusion.5 = f32[29,28,288]{2,1,0:T(8,128)S(1)} fusion(f32[32,28,288]{2,1,0:T(8,128)S(1)} %fusion, f32[32,32,288]{2,1,0:T(8,128)S(1)} %get-tuple-element.8), kind=kLoop, calls=%fused_computation.11 | loop fusion | flops 5144832 | bytes 6547968 | tf_op jit(solution)/shard_map/mul | solution.py:32
  35.0 0.4 slice.742
  35.8 0.5 fusion.133
  36.3 1.0 %multiply_subtract_fusion = f32[32,32,288]{2,1,0:T(8,128)S(1)} fusion(f32[32,32,288]{2,1,0:T(8,128)S(1)} %fusion.67, f32[288]{0:T(512)S(1)} %get-tuple-element.51, f32[288]{0:T(512)S(1)} %get-tuple-element.52, f32[32,32,312]{2,1,0:T(8,128)S(1)} %copy-done.3, s32[288]{0:T(512)S(1)} %add_select_fusion.2), kind=kOutput, calls=%fused_computation.3 | convolution fusion | flops 29198592 | bytes 3282944 | tf_op jit(solution)/shard_map/dot_general | solution.py:70
  37.8 0.5 slice-done.1
  38.2 2.5 %fusion.17 = f32[28,28,288]{2,1,0:T(8,128)S(1)} fusion(f32[28,28,35]{2,1,0:T(8,128)S(1)} %get-tuple-element.11, f32[28,28,253]{2,1,0:T(8,128)S(1)} %get-tuple-element.13, f32[28,28,287]{2,1,0:T(8,128)S(1)} %get-tuple-element.15, f32[28,28,1]{2,1,0:T(8,128)S(1)} %get-tuple-element.17, f32[28,28,288]{2,1,0:T(8,128)S(1)} %copy-done.2, ...), kind=kLoop, calls=%fused_computation.31 | loop fusion | flops 6547968 | bytes 8129376 | tf_op jit(solution)/shard_map/mul | solution.py:32
  41.3 0.8 %fusion.21 = f32[28,28,288]{2,1,0:T(8,128)S(1)} fusion(f32[28,28,288]{2,1,0:T(8,128)S(1)} %copy-done.2, f32[28,28,288]{2,1,0:T(8,128)S(1)} %fusion.17, f32[28,28,35]{2,1,0:T(8,128)S(1)} %slice.745, f32[28,28,253]{2,1,0:T(8,128)S(1)} %slice.744, f32[28,28,287]{2,1,0:T(8,128)S(1)} %bitcast.43, f32[28,28,1]{2,1,0:T(8,128)S(1)} %slice.746, ...), kind=kLoop, calls=%fused_computation.37 | loop fusion | flops 1128960 | bytes 4516128 | tf_op jit(solution)/shard_map/sub | solution.py:66
  42.1 1.4 %fusion.10 = f32[28,25,288]{2,1,0:T(8,128)S(1)} fusion(f32[28,28,288]{2,1,0:T(8,128)S(1)} %fusion.21, f32[32,32,288]{2,1,0:T(8,128)S(1)} %get-tuple-element.9), kind=kLoop, calls=%fused_computation.19 | loop fusion | flops 4435200 | bytes 5644800 | tf_op jit(solution)/shard_map/mul | solution.py:32
  43.8 0.6 %fusion.27 = f32[25,24,288]{2,1,0:T(8,128)S(1)} fusion(f32[28,24,288]{2,1,0:T(8,128)S(1)} %fusion.22, f32[32,32,288]{2,1,0:T(8,128)S(1)} %get-tuple-element.8), kind=kLoop, calls=%fused_computation.47 | loop fusion | flops 3801600 | bytes 4838400 | tf_op jit(solution)/shard_map/mul | solution.py:32
  45.9 1.2 %fusion.40 = f32[24,24,288]{2,1,0:T(8,128)S(1)} fusion(f32[24,24,35]{2,1,0:T(8,128)S(1)} %get-tuple-element.19, f32[24,24,253]{2,1,0:T(8,128)S(1)} %get-tuple-element.21, f32[24,24,287]{2,1,0:T(8,128)S(1)} %get-tuple-element.23, f32[24,24,1]{2,1,0:T(8,128)S(1)} %get-tuple-element.25, f32[24,24,288]{2,1,0:T(8,128)S(1)} %fusion.35, ...), kind=kLoop, calls=%fused_computation.69 | loop fusion | flops 4810752 | bytes 5972832 | tf_op jit(solution)/shard_map/mul | solution.py:32
  47.6 0.5 fusion.44
  48.1 0.9 %fusion.33 = f32[24,21,288]{2,1,0:T(8,128)S(1)} fusion(f32[24,24,288]{2,1,0:T(8,128)S(1)} %fusion.44, f32[32,32,288]{2,1,0:T(8,128)S(1)} %get-tuple-element.9), kind=kLoop, calls=%fused_computation.57 | loop fusion | flops 3193344 | bytes 4064256 | tf_op jit(solution)/shard_map/mul | solution.py:32
  49.2 0.5 fusion.49
  51.1 1.1 %fusion.61 = f32[20,20,288]{2,1,0:T(8,128)S(1)} fusion(f32[20,20,35]{2,1,0:T(8,128)S(1)} %get-tuple-element.27, f32[20,20,253]{2,1,0:T(8,128)S(1)} %get-tuple-element.29, f32[20,20,287]{2,1,0:T(8,128)S(1)} %get-tuple-element.31, f32[20,20,1]{2,1,0:T(8,128)S(1)} %get-tuple-element.33, f32[20,20,288]{2,1,0:T(8,128)S(1)} %fusion.56, ...), kind=kLoop, calls=%fused_computation.102 | loop fusion | flops 3340800 | bytes 4148064 | tf_op jit(solution)/shard_map/mul | solution.py:32
  52.5 0.4 fusion.65
  52.9 0.7 %fusion.54 = f32[20,17,288]{2,1,0:T(8,128)S(1)} fusion(f32[20,20,288]{2,1,0:T(8,128)S(1)} %fusion.65, f32[32,32,288]{2,1,0:T(8,128)S(1)} %get-tuple-element.9), kind=kLoop, calls=%fused_computation.90 | loop fusion | flops 2154240 | bytes 2741760 | tf_op jit(solution)/shard_map/mul | solution.py:32
  53.8 0.5 fusion.76
  55.2 0.6 fusion.87
  56.1 0.4 multiply_reduce_fusion
  56.5 0.8 %collective-permute-start = (f32[2,16,16]{2,1,0:T(8,128)S(1)}, f32[2,16,16]{2,1,0:T(8,128)S(1)}, u32[]{:S(2)}, u32[]{:S(2)}) collective-permute-start(f32[2,16,16]{2,1,0:T(8,128)S(1)} %pad_maximum_fusion.1), channel_id=1, source_target_pairs={{0,1},{1,0},{2,3},{3,2},{4,5},{5,4},{6,7},{7,6},{8,9},{9,8},{10,11... | collective-permute-start | bytes 6152 | tf_op jit(solution)/shard_map/ppermute | solution.py:270
  57.6 2.8 %collective-permute-done = f32[2,16,16]{2,1,0:T(8,128)S(1)} collective-permute-done((f32[2,16,16]{2,1,0:T(8,128)S(1)}, f32[2,16,16]{2,1,0:T(8,128)S(1)}, u32[]{:S(2)}, u32[]{:S(2)}) %collective-permute-start) | collective-permute-done | bytes 2080 | tf_op jit(solution)/shard_map/ppermute | solution.py:270
  60.4 2.3 %fusion.80 = f32[16,16,288]{2,1,0:T(8,128)} fusion(f32[16,16,288]{2,1,0:T(8,128)S(1)} %get-tuple-element.7, f32[288]{0:T(512)S(1)} %dynamic_slice.11, f32[16,16]{1,0:T(8,128)S(1)} %convert_element_type.49, f32[16,16]{1,0:T(8,128)S(1)} %get-tuple-element.45, f32[16,16]{1,0:T(8,128)S(1)} %get-tuple-element.44, f32[288]{0:T(512)S(1)} %get-tuple-element.48, ...), kind=kLoop, calls=%fused_computation.128 | loop fusion | flops 811008 | bytes 600576 | tf_op jit(solution)/shard_map/mul | solution.py:107
  (87 shorter events, 8.5 us)
Async XLA Ops:
  0.0 4.1 %copy-start = (f32[8,16]{1,0:T(8,128)S(1)}, f32[8,16]{1,0:T(8,128)}, u32[]{:S(2)}) copy-start(f32[8,16]{1,0:T(8,128)} %param.15) | copy-start | bytes 1540
  28.3 2.0 %copy-start.3 = (f32[32,32,312]{2,1,0:T(8,128)S(1)}, f32[32,32,312]{2,1,0:T(8,128)}, u32[]{:S(2)}) copy-start(f32[32,32,312]{2,1,0:T(8,128)} %shard_map.100) | copy-start | bytes 3833860
  34.5 1.4 %copy-start.1 = (f32[28,28,288]{2,1,0:T(8,128)}, f32[28,28,288]{2,1,0:T(8,128)S(1)}, u32[]{:S(2)}) copy-start(f32[28,28,288]{2,1,0:T(8,128)S(1)} %fusion.12) | copy-start | bytes 2709508
  36.3 1.3 %copy-start.2 = (f32[28,28,288]{2,1,0:T(8,128)S(1)}, f32[28,28,288]{2,1,0:T(8,128)}, u32[]{:S(2)}) copy-start(f32[28,28,288]{2,1,0:T(8,128)} %copy-done.1) | copy-start | bytes 2709508
  36.3 1.4 %slice-start = ((f32[28,28,288]{2,1,0:T(8,128)}), f32[28,28,2]{2,1,0:T(8,128)S(1)}, s32[]{:S(2)}) async-start(f32[28,28,288]{2,1,0:T(8,128)} %copy-done.1), calls=%async_computation | async-start | bytes 917504 | tf_op jit(solution)/shard_map/jit(_roll_static)/slice | solution.py:56
  36.3 1.9 %slice-start.1 = ((f32[28,28,288]{2,1,0:T(8,128)}), f32[28,28,254]{2,1,0:T(8,128)S(1)}, s32[]{:S(2)}) async-start(f32[28,28,288]{2,1,0:T(8,128)} %copy-done.1), calls=%async_computation.1 | async-start | bytes 1835008 | tf_op jit(solution)/shard_map/jit(_roll_static)/slice | solution.py:58
  55.9 1.4 %copy-start.5 = (f32[16,16]{1,0:T(8,128)S(1)}, f32[16,16]{1,0:T(8,128)}, u32[]{:S(2)}) copy-start(f32[16,16]{1,0:T(8,128)} %param.17) | copy-start | bytes 3076
  55.9 1.4 %copy-start.6 = (s32[16,16]{1,0:T(8,128)S(1)}, s32[16,16]{1,0:T(8,128)}, u32[]{:S(2)}) copy-start(s32[16,16]{1,0:T(8,128)} %param.12) | copy-start | bytes 3076
  56.0 1.4 %copy-start.7 = (f32[16]{0:T(128)S(1)}, f32[16]{0:T(128)}, u32[]{:S(2)}) copy-start(f32[16]{0:T(128)} %param.19) | copy-start | bytes 196
  56.0 4.4 %copy-start.4 = (f32[16,16]{1,0:T(8,128)S(1)}, f32[16,16]{1,0:T(8,128)}, u32[]{:S(2)}) copy-start(f32[16,16]{1,0:T(8,128)} %param.18) | copy-start | bytes 3076
  56.5 3.8 %collective-permute-start = (f32[2,16,16]{2,1,0:T(8,128)S(1)}, f32[2,16,16]{2,1,0:T(8,128)S(1)}, u32[]{:S(2)}, u32[]{:S(2)}) collective-permute-start(f32[2,16,16]{2,1,0:T(8,128)S(1)} %pad_maximum_fusion.1), channel_id=1, source_target_pairs={{0,1},{1,0},{2,3},{3,2},{4,5},{5,4},{6,7},{7,6},{8,9},{9,8},{10,11... | collective-permute-start | bytes 6152 | tf_op jit(solution)/shard_map/ppermute | solution.py:270

commit v5 on v4

--- a/solution.py
+++ b/solution.py
@@ -232,8 +232,9 @@
     ice_share = ice_mask.astype(jnp.float32)
     speed_local = lax.dynamic_slice_in_dim(speed_table, band_index * freqs_dev, freqs_dev, 1)
     refr_local = lax.dynamic_slice_in_dim(refraction_table, band_index * freqs_dev, freqs_dev, 1)
-    group_speed = lookup(depth_class, speed_local) * sea_share[..., None]
-    turning = lookup(depth_class, refr_local) * sea_share[..., None]
+    chosen = (depth_class[..., None] == jnp.arange(speed_table.shape[0]))[..., None]
+    group_speed = jnp.sum(jnp.where(chosen, speed_local, 0.0), axis=2) * sea_share[..., None]
+    turning = jnp.sum(jnp.where(chosen, refr_local, 0.0), axis=2) * sea_share[..., None]
     turn_x = turning * depth_slope[0][..., None]
     turn_y = turning * depth_slope[1][..., None]
     density = spectrum * sea_share[..., None]

time: 63.3 us -> 63.2 us (level)
  matrix products: 5.88 us -> 3.88 us
  other arithmetic: 21.8 us -> 22.9 us
  local copies, waits for them, and re-layouts: 8.7 us -> 9.53 us
    dot_general x2 -> x0, matrix products: 2 us -> none  [lookup(): return jnp.dot(onehot, lookup_table, precision=lax.Precision.HIGHEST)]
    dynamic_slice x0 -> x1, local copies, waits for them, and re-layouts: none -> 0.77 us  [per_device(): lax.dynamic_slice_in_dim(refraction_table, band_index * freqs_dev, freqs_...]
    eq x0 -> x1, other arithmetic: none -> 0.71 us  [per_device(): depth_class[..., None] == jnp.arange(speed_table.shape[0])]
where the time goes in v5:
time: 63.2 us; the launch traced here: 62.7 us
  other arithmetic  22.9 us (36%)
  Pallas kernels  22.2 us (35%)
  local copies, waits for them, and re-layouts  9.53 us (15%)
  matrix products  3.88 us (6%)
  waiting for transfers between devices  2.76 us (4%)
  starting transfers between devices  0.76 us (1%)
    pallas_call x1, Pallas kernels, halo_exchange(): pl.pallas_call(functools.partial(halo_kernel, halo=halo), out_shape=jax.S...  22.2 us
    mul x12, other arithmetic, quickest(): return courant * face_value  12.8 us
    dot_general x3, matrix products, expand(): return jnp.dot(per_freq, spread, precision=lax.Precision.HIGHEST)  3.88 us
    slice x21, local copies, waits for them, and re-layouts, rotate(): inner_roll = jnp.roll(density, -offset, axis=-1)  3.59 us
    ppermute x1, waiting for transfers between devices, per_device(): other = lax.ppermute(partial, 'band', [(0, 1), (1, 0)])  2.76 us
    slice x17, local copies, waits for them, and re-layouts, rotate(): outer_roll = jnp.roll(density, NDIR - offset, axis=-1)  2.45 us
    mul x1, other arithmetic, sources(): return sea_share[..., None] * density * jnp.exp(growth - breaking - damping)  2.33 us
    sub x3, other arithmetic, refract(): return density - (fluxes - rotate(fluxes, -1))  1.67 us
  transfers between devices with their start and end apart: 1, of which 1 were waited for; matrix products, arithmetic and copies ran while one was open for 0% of the time, Pallas kernels for 0%

profile of v5, /device:TPU:2, one launch (start us, length us, event | category | flops | bytes accessed | tf_op | source)
XLA Modules:
  0.0 62.7 jit_solution(17662201641405968269)
XLA Ops:
  0.6 0.7 %convert_element_type.43 = f32[16,16]{1,0:T(8,128)S(1)} convert(s32[16,16]{1,0:T(8,128)} %param.11) | non-fusion elementwise | flops 256 | bytes 2048 | tf_op jit(solution)/shard_map/convert_element_type | solution.py:231
  1.3 0.7 %iota_compare_fusion = pred[16,16,8]{1,2,0:T(8,128)(4,1)S(1)} fusion(s32[16,16]{1,0:T(8,128)} %param.13), kind=kLoop, calls=%fused_computation.151 | loop fusion | flops 2048 | bytes 3072 | tf_op jit(solution)/shard_map/eq | solution.py:235
  2.0 0.7 %slice_bitcast_fusion.3 = (f32[16,16]{1,0:T(8,128)S(1)}, f32[16,16]{1,0:T(8,128)S(1)}) fusion(f32[2,16,16]{2,1,0:T(8,128)} %param.16), kind=kLoop, calls=%fused_computation.163 | loop fusion | bytes 4096 | tf_op jit(solution)/shard_map/mul | solution.py:238
  2.7 0.8 %constant_dynamic-slice_fusion = (f32[8,8]{1,0:T(8,128)S(1)}, f32[8,8]{1,0:T(8,128)S(1)}) fusion(f32[8,16]{1,0:T(8,128)} %param.15, s32[]{:T(128)S(6)} %select_n.243, f32[8,16]{1,0:T(8,128)} %param.14), kind=kLoop, calls=%fused_computation.201 | loop fusion | bytes 1028 | tf_op jit(solution)/shard_map/dynamic_slice | solution.py:234
  4.0 1.1 %broadcast_multiply_fusion.1 = f32[16,16,288]{2,1,0:T(8,128)S(1)} fusion(f32[16,16,288]{2,1,0:T(8,128)} %param.10, f32[16,16]{1,0:T(8,128)S(1)} %convert_element_type.43), kind=kLoop, calls=%fused_computation.147 | loop fusion | flops 73728 | bytes 590848 | tf_op jit(solution)/shard_map/mul | solution.py:240
  5.2 0.9 %pad_maximum_fusion.in_ref = f32[16,16,312]{2,1,0:T(8,128)} fusion(f32[16,16,8]{2,1,0:T(8,128)S(1)} %get-tuple-element.45, f32[16,16,8]{2,1,0:T(8,128)S(1)} %get-tuple-element.44, f32[16,16,8]{2,1,0:T(8,128)S(1)} %get-tuple-element.50, f32[16,16,288]{2,1,0:T(8,128)S(1)} %broadcast_multiply_fusion.1), kind=kLoop, calls=%fused_computation.132 | loop fusion | flops 239616 | bytes 638976 | tf_op jit(solution)/shard_map/concatenate | solution.py:242
  6.2 22.2 %shard_map.100 = f32[32,32,312]{2,1,0:T(8,128)} custom-call(f32[16,16,312]{2,1,0:T(8,128)} %pad_maximum_fusion.in_ref), custom_call_target="tpu_custom_call" | custom-call | tf_op jit(solution)/shard_map/pallas_call | solution.py:180
  28.4 2.0 %fusion.67 = f32[32,32,288]{2,1,0:T(8,128)S(1)} fusion(f32[32,32,312]{2,1,0:T(8,128)} %shard_map.100, s32[288]{0:T(512)S(1)} %add_select_fusion.2), kind=kOutput, calls=%fused_computation.108 | convolution fusion | flops 28313856 | bytes 1705088 | tf_op jit(solution)/shard_map/dot_general | solution.py:70
  30.4 0.9 %broadcast_multiply_fusion = (f32[32,32,288]{2,1,0:T(8,128)S(1)}, f32[32,32,288]{2,1,0:T(8,128)S(1)}) fusion(f32[288]{0:T(512)S(1)} %get-tuple-element.58, f32[32]{0:T(128)S(1)} %cosine_divide_fusion, f32[288]{0:T(512)S(1)} %fusion.118, s32[288]{0:T(512)S(1)} %add_select_fusion.2, f32[32,32,312]{2,1,0:T(8,128)S(1)} %copy-done.2), kind=kOutput, calls=%fused_computation.74 | convolution fusion | flops 29198592 | bytes 2890240 | tf_op jit(solution)/shard_map/dot_general | solution.py:70
  31.3 1.6 %subtract_multiply_fusion = f32[32,29,288]{2,1,0:T(8,128)S(1)} fusion(f32[32,32,312]{2,1,0:T(8,128)S(1)} %copy-done.2, f32[32,32,288]{2,1,0:T(8,128)S(1)} %get-tuple-element.11), kind=kLoop, calls=%fused_computation.4 | loop fusion | flops 5879808 | bytes 7483392 | tf_op jit(solution)/shard_map/mul | solution.py:32
  33.0 0.4 fusion
  33.3 1.0 %fusion.5 = f32[29,28,288]{2,1,0:T(8,128)S(1)} fusion(f32[32,28,288]{2,1,0:T(8,128)S(1)} %fusion, f32[32,32,288]{2,1,0:T(8,128)S(1)} %get-tuple-element.10), kind=kLoop, calls=%fused_computation.11 | loop fusion | flops 5144832 | bytes 6547968 | tf_op jit(solution)/shard_map/mul | solution.py:32
  35.1 0.4 slice.742
  35.9 0.5 fusion.122
  36.4 1.0 %multiply_subtract_fusion = f32[32,32,288]{2,1,0:T(8,128)S(1)} fusion(f32[32,32,288]{2,1,0:T(8,128)S(1)} %fusion.67, f32[288]{0:T(512)S(1)} %get-tuple-element.56, f32[288]{0:T(512)S(1)} %get-tuple-element.57, f32[32,32,312]{2,1,0:T(8,128)S(1)} %copy-done.2, s32[288]{0:T(512)S(1)} %add_select_fusion.2), kind=kOutput, calls=%fused_computation.3 | convolution fusion | flops 29198592 | bytes 3282944 | tf_op jit(solution)/shard_map/dot_general | solution.py:70
  38.2 2.5 %fusion.17 = f32[28,28,288]{2,1,0:T(8,128)S(1)} fusion(f32[28,28,35]{2,1,0:T(8,128)S(1)} %get-tuple-element.13, f32[28,28,253]{2,1,0:T(8,128)S(1)} %get-tuple-element.15, f32[28,28,287]{2,1,0:T(8,128)S(1)} %get-tuple-element.17, f32[28,28,1]{2,1,0:T(8,128)S(1)} %get-tuple-element.19, f32[28,28,288]{2,1,0:T(8,128)S(1)} %copy-done.1, ...), kind=kLoop, calls=%fused_computation.31 | loop fusion | flops 6547968 | bytes 8129376 | tf_op jit(solution)/shard_map/mul | solution.py:32
  41.3 0.8 %fusion.21 = f32[28,28,288]{2,1,0:T(8,128)S(1)} fusion(f32[28,28,288]{2,1,0:T(8,128)S(1)} %copy-done.1, f32[28,28,288]{2,1,0:T(8,128)S(1)} %fusion.17, f32[28,28,35]{2,1,0:T(8,128)S(1)} %slice.745, f32[28,28,253]{2,1,0:T(8,128)S(1)} %slice.744, f32[28,28,287]{2,1,0:T(8,128)S(1)} %bitcast.33, f32[28,28,1]{2,1,0:T(8,128)S(1)} %slice.746, ...), kind=kLoop, calls=%fused_computation.37 | loop fusion | flops 1128960 | bytes 4516128 | tf_op jit(solution)/shard_map/sub | solution.py:66
  42.1 1.4 %fusion.10 = f32[28,25,288]{2,1,0:T(8,128)S(1)} fusion(f32[28,28,288]{2,1,0:T(8,128)S(1)} %fusion.21, f32[32,32,288]{2,1,0:T(8,128)S(1)} %get-tuple-element.11), kind=kLoop, calls=%fused_computation.19 | loop fusion | flops 4435200 | bytes 5644800 | tf_op jit(solution)/shard_map/mul | solution.py:32
  43.8 0.6 %fusion.27 = f32[25,24,288]{2,1,0:T(8,128)S(1)} fusion(f32[28,24,288]{2,1,0:T(8,128)S(1)} %fusion.22, f32[32,32,288]{2,1,0:T(8,128)S(1)} %get-tuple-element.10), kind=kLoop, calls=%fused_computation.45 | loop fusion | flops 3801600 | bytes 4838400 | tf_op jit(solution)/shard_map/mul | solution.py:32
  45.9 1.2 %fusion.40 = f32[24,24,288]{2,1,0:T(8,128)S(1)} fusion(f32[24,24,35]{2,1,0:T(8,128)S(1)} %get-tuple-element.21, f32[24,24,253]{2,1,0:T(8,128)S(1)} %get-tuple-element.23, f32[24,24,287]{2,1,0:T(8,128)S(1)} %get-tuple-element.25, f32[24,24,1]{2,1,0:T(8,128)S(1)} %get-tuple-element.27, f32[24,24,288]{2,1,0:T(8,128)S(1)} %fusion.35, ...), kind=kLoop, calls=%fused_computation.67 | loop fusion | flops 4810752 | bytes 5972832 | tf_op jit(solution)/shard_map/mul | solution.py:32
  47.5 0.5 fusion.44
  48.0 0.9 %fusion.33 = f32[24,21,288]{2,1,0:T(8,128)S(1)} fusion(f32[24,24,288]{2,1,0:T(8,128)S(1)} %fusion.44, f32[32,32,288]{2,1,0:T(8,128)S(1)} %get-tuple-element.11), kind=kLoop, calls=%fused_computation.55 | loop fusion | flops 3193344 | bytes 4064256 | tf_op jit(solution)/shard_map/mul | solution.py:32
  49.2 0.5 fusion.49
  51.0 1.1 %fusion.61 = f32[20,20,288]{2,1,0:T(8,128)S(1)} fusion(f32[20,20,35]{2,1,0:T(8,128)S(1)} %get-tuple-element.29, f32[20,20,253]{2,1,0:T(8,128)S(1)} %get-tuple-element.31, f32[20,20,287]{2,1,0:T(8,128)S(1)} %get-tuple-element.33, f32[20,20,1]{2,1,0:T(8,128)S(1)} %get-tuple-element.35, f32[20,20,288]{2,1,0:T(8,128)S(1)} %fusion.56, ...), kind=kLoop, calls=%fused_computation.100 | loop fusion | flops 3340800 | bytes 4148064 | tf_op jit(solution)/shard_map/mul | solution.py:32
  52.5 0.4 fusion.65
  52.9 0.7 %fusion.54 = f32[20,17,288]{2,1,0:T(8,128)S(1)} fusion(f32[20,20,288]{2,1,0:T(8,128)S(1)} %fusion.65, f32[32,32,288]{2,1,0:T(8,128)S(1)} %get-tuple-element.11), kind=kLoop, calls=%fused_computation.88 | loop fusion | flops 2154240 | bytes 2741760 | tf_op jit(solution)/shard_map/mul | solution.py:32
  53.7 0.5 fusion.76
  55.2 0.6 fusion.87
  56.1 0.4 multiply_reduce_fusion
  56.5 0.8 %collective-permute-start = (f32[2,16,16]{2,1,0:T(8,128)S(1)}, f32[2,16,16]{2,1,0:T(8,128)S(1)}, u32[]{:S(2)}, u32[]{:S(2)}) collective-permute-start(f32[2,16,16]{2,1,0:T(8,128)S(1)} %pad_maximum_fusion.1), channel_id=1, source_target_pairs={{0,1},{1,0},{2,3},{3,2},{4,5},{5,4},{6,7},{7,6},{8,9},{9,8},{10,11... | collective-permute-start | bytes 6152 | tf_op jit(solution)/shard_map/ppermute | solution.py:271
  57.6 2.8 %collective-permute-done = f32[2,16,16]{2,1,0:T(8,128)S(1)} collective-permute-done((f32[2,16,16]{2,1,0:T(8,128)S(1)}, f32[2,16,16]{2,1,0:T(8,128)S(1)}, u32[]{:S(2)}, u32[]{:S(2)}) %collective-permute-start) | collective-permute-done | bytes 2080 | tf_op jit(solution)/shard_map/ppermute | solution.py:271
  60.4 2.3 %fusion.80 = f32[16,16,288]{2,1,0:T(8,128)} fusion(f32[16,16,288]{2,1,0:T(8,128)S(1)} %get-tuple-element.9, f32[288]{0:T(512)S(1)} %dynamic_slice.11, f32[16,16]{1,0:T(8,128)S(1)} %convert_element_type.47, f32[16,16]{1,0:T(8,128)S(1)} %get-tuple-element.47, f32[16,16]{1,0:T(8,128)S(1)} %get-tuple-element.46, f32[288]{0:T(512)S(1)} %get-tuple-element.53, ...), kind=kLoop, calls=%fused_computation.128 | loop fusion | flops 811008 | bytes 600576 | tf_op jit(solution)/shard_map/mul | solution.py:107
  (89 shorter events, 9.1 us)
Async XLA Ops:
  28.4 2.0 %copy-start.2 = (f32[32,32,312]{2,1,0:T(8,128)S(1)}, f32[32,32,312]{2,1,0:T(8,128)}, u32[]{:S(2)}) copy-start(f32[32,32,312]{2,1,0:T(8,128)} %shard_map.100) | copy-start | bytes 3833860
  34.5 1.4 %copy-start = (f32[28,28,288]{2,1,0:T(8,128)}, f32[28,28,288]{2,1,0:T(8,128)S(1)}, u32[]{:S(2)}) copy-start(f32[28,28,288]{2,1,0:T(8,128)S(1)} %fusion.12) | copy-start | bytes 2709508
  36.4 1.3 %copy-start.1 = (f32[28,28,288]{2,1,0:T(8,128)S(1)}, f32[28,28,288]{2,1,0:T(8,128)}, u32[]{:S(2)}) copy-start(f32[28,28,288]{2,1,0:T(8,128)} %copy-done) | copy-start | bytes 2709508
  36.4 1.4 %slice-start = ((f32[28,28,288]{2,1,0:T(8,128)}), f32[28,28,2]{2,1,0:T(8,128)S(1)}, s32[]{:S(2)}) async-start(f32[28,28,288]{2,1,0:T(8,128)} %copy-done), calls=%async_computation | async-start | bytes 917504 | tf_op jit(solution)/shard_map/jit(_roll_static)/slice | solution.py:56
  36.4 1.8 %slice-start.1 = ((f32[28,28,288]{2,1,0:T(8,128)}), f32[28,28,254]{2,1,0:T(8,128)S(1)}, s32[]{:S(2)}) async-start(f32[28,28,288]{2,1,0:T(8,128)} %copy-done), calls=%async_computation.1 | async-start | bytes 1835008 | tf_op jit(solution)/shard_map/jit(_roll_static)/slice | solution.py:58
  55.9 1.4 %copy-start.4 = (f32[16,16]{1,0:T(8,128)S(1)}, f32[16,16]{1,0:T(8,128)}, u32[]{:S(2)}) copy-start(f32[16,16]{1,0:T(8,128)} %param.17) | copy-start | bytes 3076
  55.9 1.4 %copy-start.5 = (s32[16,16]{1,0:T(8,128)S(1)}, s32[16,16]{1,0:T(8,128)}, u32[]{:S(2)}) copy-start(s32[16,16]{1,0:T(8,128)} %param.12) | copy-start | bytes 3076
  55.9 1.4 %copy-start.6 = (f32[16]{0:T(128)S(1)}, f32[16]{0:T(128)}, u32[]{:S(2)}) copy-start(f32[16]{0:T(128)} %param.19) | copy-start | bytes 196
  56.0 4.4 %copy-start.3 = (f32[16,16]{1,0:T(8,128)S(1)}, f32[16,16]{1,0:T(8,128)}, u32[]{:S(2)}) copy-start(f32[16,16]{1,0:T(8,128)} %param.18) | copy-start | bytes 3076
  56.5 3.8 %collective-permute-start = (f32[2,16,16]{2,1,0:T(8,128)S(1)}, f32[2,16,16]{2,1,0:T(8,128)S(1)}, u32[]{:S(2)}, u32[]{:S(2)}) collective-permute-start(f32[2,16,16]{2,1,0:T(8,128)S(1)} %pad_maximum_fusion.1), channel_id=1, source_target_pairs={{0,1},{1,0},{2,3},{3,2},{4,5},{5,4},{6,7},{7,6},{8,9},{9,8},{10,11... | collective-permute-start | bytes 6152 | tf_op jit(solution)/shard_map/ppermute | solution.py:271

commit v6 on v5

--- a/solution.py
+++ b/solution.py
@@ -186,6 +186,36 @@
         compiler_params=pltpu.CompilerParams(collective_id=0, has_side_effects=True),
         interpret=pltpu.InterpretParams(detect_races=True) if INTERPRET else False,
     )(cells)
+
+
+def swap_kernel(in_ref, out_ref, send_sem, recv_sem):
+    peer = {"band": 1 - lax.axis_index("band")}
+    barrier = pltpu.get_barrier_semaphore()
+    pl.semaphore_signal(barrier, inc=1, device_id=peer, device_id_type=MESH_ID)
+    pl.semaphore_wait(barrier, 1)
+    copy = pltpu.make_async_remote_copy(
+        src_ref=in_ref,
+        dst_ref=out_ref,
+        send_sem=send_sem,
+        recv_sem=recv_sem,
+        device_id=peer,
+        device_id_type=MESH_ID,
+    )
+    copy.start()
+    copy.wait()
+
+
+def band_swap(values):
+    vmem = pl.BlockSpec(memory_space=pltpu.VMEM)
+    return pl.pallas_call(
+        swap_kernel,
+        out_shape=jax.ShapeDtypeStruct(values.shape, values.dtype),
+        in_specs=[vmem],
+        out_specs=vmem,
+        scratch_shapes=[pltpu.SemaphoreType.DMA(()), pltpu.SemaphoreType.DMA(())],
+        compiler_params=pltpu.CompilerParams(collective_id=1, has_side_effects=True),
+        interpret=pltpu.InterpretParams(detect_races=True) if INTERPRET else False,
+    )(values)
 
 
 def exchange(cells, axis, dim, width, closed):
@@ -268,7 +298,7 @@
     levels = jnp.exp(math.log(freq_ratio) * (comp_index // NDIR).astype(jnp.float32))
     ice_loss = lax.dynamic_slice_in_dim(jnp.repeat(ice_rate, NDIR), first_comp, comps_dev, 0)
     partial = jnp.stack([jnp.sum(density, axis=-1), jnp.sum(density * levels, axis=-1)])
-    other = lax.ppermute(partial, "band", [(0, 1), (1, 0)])
+    other = band_swap(partial)
     energy_sum = partial[0] + other[0]
     moment = partial[1] + other[1]
     return sources(

time: 63.2 us -> 66.5 us (1.052)
  Pallas kernels: 22.2 us -> 27.3 us
  waiting for transfers between devices: 2.76 us -> 0 us
  other arithmetic: 22.9 us -> 24.7 us
  starting transfers between devices: 0.76 us -> 0 us
    pallas_call x0 -> x1, Pallas kernels: none -> 5.07 us  [band_swap(): pl.pallas_call(swap_kernel, out_shape=jax.ShapeDtypeStruct(values.shape,...]
    ppermute x1 -> x0, waiting for transfers between devices: 2.76 us -> none  [per_device(): other = lax.ppermute(partial, 'band', [(0, 1), (1, 0)])]
    mul x1, other arithmetic: 1.1 us -> 0.1 us  [per_device(): density = spectrum * sea_share[..., None]]
    ppermute x1 -> x0, starting transfers between devices: 0.76 us -> none  [per_device(): other = lax.ppermute(partial, 'band', [(0, 1), (1, 0)])]
    div x1, other arithmetic: 0.01 us -> 0.73 us  [sources(): mean_level = jnp.maximum(moment, 1.0) / jnp.maximum(energy_sum, 1.0)]
    mul x1, other arithmetic: 0.01 us -> 0.7 us  [sources(): wind_gain * wind_speed[..., None] * levels]
    convert_element_type x1, other arithmetic: 0.01 us -> 0.7 us  [per_device(): ice_share = ice_mask.astype(jnp.float32)]
    slice x17 -> x16, local copies, waits for them, and re-layouts: 2.45 us -> 2.14 us  [rotate(): outer_roll = jnp.roll(density, NDIR - offset, axis=-1)]
  transfers between devices with their start and end apart: 1 -> 0, of which waited for: 1 -> 0; matrix products, arithmetic and copies ran while one was open for 0% -> 0% of each run, Pallas kernels for 0% -> 0%
where the time goes in v6:
time: 66.5 us; the launch traced here: 65.8 us
  Pallas kernels  27.3 us (41%)
  other arithmetic  24.7 us (37%)
  local copies, waits for them, and re-layouts  9.47 us (14%)
  matrix products  3.88 us (6%)
    pallas_call x1, Pallas kernels, halo_exchange(): pl.pallas_call(functools.partial(halo_kernel, halo=halo), out_shape=jax.S...  22.2 us
    mul x12, other arithmetic, quickest(): return courant * face_value  12.8 us
    pallas_call x1, Pallas kernels, band_swap(): pl.pallas_call(swap_kernel, out_shape=jax.ShapeDtypeStruct(values.shape,...  5.07 us
    dot_general x3, matrix products, expand(): return jnp.dot(per_freq, spread, precision=lax.Precision.HIGHEST)  3.88 us
    slice x20, local copies, waits for them, and re-layouts, rotate(): inner_roll = jnp.roll(density, -offset, axis=-1)  3.53 us
    mul x1, other arithmetic, sources(): return sea_share[..., None] * density * jnp.exp(growth - breaking - damping)  2.33 us
    slice x16, local copies, waits for them, and re-layouts, rotate(): outer_roll = jnp.roll(density, NDIR - offset, axis=-1)  2.14 us
    sub x3, other arithmetic, refract(): return density - (fluxes - rotate(fluxes, -1))  1.67 us

profile of v6, /device:TPU:2, one launch (start us, length us, event | category | flops | bytes accessed | tf_op | source)
XLA Modules:
  0.0 65.8 jit_solution(9691037193915458289)
XLA Ops:
  0.6 0.8 %constant_dynamic-slice_fusion = (f32[8,8]{1,0:T(8,128)S(1)}, f32[8,8]{1,0:T(8,128)S(1)}) fusion(f32[8,16]{1,0:T(8,128)} %param.15, s32[]{:T(128)S(6)} %select_n.243, f32[8,16]{1,0:T(8,128)} %param.14), kind=kLoop, calls=%fused_computation.199 | loop fusion | bytes 1028 | tf_op jit(solution)/shard_map/dynamic_slice | solution.py:264
  1.4 0.7 %convert_element_type.43 = f32[16,16]{1,0:T(8,128)S(1)} convert(s32[16,16]{1,0:T(8,128)} %param.11) | non-fusion elementwise | flops 256 | bytes 2048 | tf_op jit(solution)/shard_map/convert_element_type | solution.py:261
  2.1 0.7 %convert_element_type.47 = f32[16,16]{1,0:T(8,128)S(1)} convert(s32[16,16]{1,0:T(8,128)} %param.12) | non-fusion elementwise | flops 256 | bytes 2048 | tf_op jit(solution)/shard_map/convert_element_type | solution.py:262
  2.8 0.7 %broadcast_multiply_fusion.3 = f32[16,16]{1,0:T(8,128)S(1)} fusion(f32[16,16]{1,0:T(8,128)} %param.17), kind=kLoop, calls=%fused_computation.165 | loop fusion | flops 256 | bytes 2048 | tf_op jit(solution)/shard_map/mul | solution.py:101
  3.5 0.7 %broadcast_in_dim.175 = f32[16,36]{1,0:T(8,128)S(1)} broadcast(f32[16]{0:T(128)} %param.19), dimensions={0} | broadcast | bytes 2368 | tf_op jit(solution)/shard_map/broadcast_in_dim | solution.py:299
  4.4 0.7 %iota_compare_fusion = pred[16,16,8]{1,2,0:T(8,128)(4,1)S(1)} fusion(s32[16,16]{1,0:T(8,128)} %param.13), kind=kLoop, calls=%fused_computation.151 | loop fusion | flops 2048 | bytes 3072 | tf_op jit(solution)/shard_map/eq | solution.py:265
  5.1 0.7 %slice_bitcast_fusion.1 = (f32[16,16]{1,0:T(8,128)S(1)}, f32[16,16]{1,0:T(8,128)S(1)}) fusion(f32[2,16,16]{2,1,0:T(8,128)} %param.16), kind=kLoop, calls=%fused_computation.161 | loop fusion | bytes 4096 | tf_op jit(solution)/shard_map/mul | solution.py:268
  6.6 0.9 %pad_maximum_fusion.in_ref = f32[16,16,312]{2,1,0:T(8,128)} fusion(f32[16,16,8]{2,1,0:T(8,128)S(1)} %get-tuple-element.45, f32[16,16,8]{2,1,0:T(8,128)S(1)} %get-tuple-element.44, f32[16,16,8]{2,1,0:T(8,128)S(1)} %get-tuple-element.50, f32[16,16,288]{2,1,0:T(8,128)S(1)} %broadcast_multiply_fusion.1), kind=kLoop, calls=%fused_computation.132 | loop fusion | flops 239616 | bytes 638976 | tf_op jit(solution)/shard_map/concatenate | solution.py:272
  7.5 22.2 %shard_map.100 = f32[32,32,312]{2,1,0:T(8,128)} custom-call(f32[16,16,312]{2,1,0:T(8,128)} %pad_maximum_fusion.in_ref), custom_call_target="tpu_custom_call" | custom-call | tf_op jit(solution)/shard_map/pallas_call | solution.py:180
  29.7 2.0 %fusion.67 = f32[32,32,288]{2,1,0:T(8,128)S(1)} fusion(f32[32,32,312]{2,1,0:T(8,128)} %shard_map.100, s32[288]{0:T(512)S(1)} %add_select_fusion.2), kind=kOutput, calls=%fused_computation.108 | convolution fusion | flops 28313856 | bytes 1705088 | tf_op jit(solution)/shard_map/dot_general | solution.py:70
  31.7 1.0 %multiply_subtract_fusion = f32[32,32,288]{2,1,0:T(8,128)S(1)} fusion(f32[32,32,288]{2,1,0:T(8,128)S(1)} %fusion.67, f32[288]{0:T(512)S(1)} %get-tuple-element.56, f32[288]{0:T(512)S(1)} %get-tuple-element.57, f32[32,32,312]{2,1,0:T(8,128)S(1)} %copy-done, s32[288]{0:T(512)S(1)} %add_select_fusion.2), kind=kOutput, calls=%fused_computation.3 | convolution fusion | flops 29198592 | bytes 3282944 | tf_op jit(solution)/shard_map/dot_general | solution.py:70
  32.7 0.9 %broadcast_multiply_fusion = (f32[32,32,288]{2,1,0:T(8,128)S(1)}, f32[32,32,288]{2,1,0:T(8,128)S(1)}) fusion(f32[288]{0:T(512)S(1)} %get-tuple-element.58, f32[32]{0:T(128)S(1)} %cosine_divide_fusion, f32[288]{0:T(512)S(1)} %fusion.116, s32[288]{0:T(512)S(1)} %add_select_fusion.2, f32[32,32,312]{2,1,0:T(8,128)S(1)} %copy-done), kind=kOutput, calls=%fused_computation.74 | convolution fusion | flops 29198592 | bytes 2890240 | tf_op jit(solution)/shard_map/dot_general | solution.py:70
  33.6 1.6 %subtract_multiply_fusion = f32[32,29,288]{2,1,0:T(8,128)S(1)} fusion(f32[32,32,312]{2,1,0:T(8,128)S(1)} %copy-done, f32[32,32,288]{2,1,0:T(8,128)S(1)} %get-tuple-element.11), kind=kLoop, calls=%fused_computation.4 | loop fusion | flops 5879808 | bytes 7483392 | tf_op jit(solution)/shard_map/mul | solution.py:32
  35.6 1.0 %fusion.5 = f32[29,28,288]{2,1,0:T(8,128)S(1)} fusion(f32[32,28,288]{2,1,0:T(8,128)S(1)} %fusion, f32[32,32,288]{2,1,0:T(8,128)S(1)} %get-tuple-element.10), kind=kLoop, calls=%fused_computation.11 | loop fusion | flops 5144832 | bytes 6547968 | tf_op jit(solution)/shard_map/mul | solution.py:32
  37.5 0.4 slice.742
  38.3 0.5 fusion.120
  38.8 2.5 %fusion.17 = f32[28,28,288]{2,1,0:T(8,128)S(1)} fusion(f32[28,28,35]{2,1,0:T(8,128)S(1)} %get-tuple-element.13, f32[28,28,253]{2,1,0:T(8,128)S(1)} %get-tuple-element.15, f32[28,28,287]{2,1,0:T(8,128)S(1)} %get-tuple-element.17, f32[28,28,1]{2,1,0:T(8,128)S(1)} %get-tuple-element.19, f32[28,28,288]{2,1,0:T(8,128)S(1)} %fusion.12, ...), kind=kLoop, calls=%fused_computation.31 | loop fusion | flops 6547968 | bytes 8129376 | tf_op jit(solution)/shard_map/mul | solution.py:32
  41.9 0.8 %fusion.21 = f32[28,28,288]{2,1,0:T(8,128)S(1)} fusion(f32[28,28,288]{2,1,0:T(8,128)S(1)} %fusion.12, f32[28,28,288]{2,1,0:T(8,128)S(1)} %fusion.17, f32[28,28,35]{2,1,0:T(8,128)S(1)} %slice.745, f32[28,28,253]{2,1,0:T(8,128)S(1)} %slice.744, f32[28,28,287]{2,1,0:T(8,128)S(1)} %bitcast.29, f32[28,28,1]{2,1,0:T(8,128)S(1)} %slice.746, ...), kind=kLoop, calls=%fused_computation.37 | loop fusion | flops 1128960 | bytes 4516128 | tf_op jit(solution)/shard_map/sub | solution.py:66
  42.6 1.4 %fusion.10 = f32[28,25,288]{2,1,0:T(8,128)S(1)} fusion(f32[28,28,288]{2,1,0:T(8,128)S(1)} %fusion.21, f32[32,32,288]{2,1,0:T(8,128)S(1)} %get-tuple-element.11), kind=kLoop, calls=%fused_computation.19 | loop fusion | flops 4435200 | bytes 5644800 | tf_op jit(solution)/shard_map/mul | solution.py:32
  44.4 0.6 fusion.27
  46.5 1.2 %fusion.40 = f32[24,24,288]{2,1,0:T(8,128)S(1)} fusion(f32[24,24,35]{2,1,0:T(8,128)S(1)} %get-tuple-element.21, f32[24,24,253]{2,1,0:T(8,128)S(1)} %get-tuple-element.23, f32[24,24,287]{2,1,0:T(8,128)S(1)} %get-tuple-element.25, f32[24,24,1]{2,1,0:T(8,128)S(1)} %get-tuple-element.27, f32[24,24,288]{2,1,0:T(8,128)S(1)} %fusion.35, ...), kind=kLoop, calls=%fused_computation.67 | loop fusion | flops 4810752 | bytes 5972832 | tf_op jit(solution)/shard_map/mul | solution.py:32
  48.1 0.5 fusion.44
  48.6 0.9 %fusion.33 = f32[24,21,288]{2,1,0:T(8,128)S(1)} fusion(f32[24,24,288]{2,1,0:T(8,128)S(1)} %fusion.44, f32[32,32,288]{2,1,0:T(8,128)S(1)} %get-tuple-element.11), kind=kLoop, calls=%fused_computation.55 | loop fusion | flops 3193344 | bytes 4064256 | tf_op jit(solution)/shard_map/mul | solution.py:32
  49.8 0.5 fusion.49
  51.6 1.1 %fusion.61 = f32[20,20,288]{2,1,0:T(8,128)S(1)} fusion(f32[20,20,35]{2,1,0:T(8,128)S(1)} %get-tuple-element.29, f32[20,20,253]{2,1,0:T(8,128)S(1)} %get-tuple-element.31, f32[20,20,287]{2,1,0:T(8,128)S(1)} %get-tuple-element.33, f32[20,20,1]{2,1,0:T(8,128)S(1)} %get-tuple-element.35, f32[20,20,288]{2,1,0:T(8,128)S(1)} %fusion.56, ...), kind=kLoop, calls=%fused_computation.100 | loop fusion | flops 3340800 | bytes 4148064 | tf_op jit(solution)/shard_map/mul | solution.py:32
  53.5 0.7 %fusion.54 = f32[20,17,288]{2,1,0:T(8,128)S(1)} fusion(f32[20,20,288]{2,1,0:T(8,128)S(1)} %fusion.65, f32[32,32,288]{2,1,0:T(8,128)S(1)} %get-tuple-element.11), kind=kLoop, calls=%fused_computation.88 | loop fusion | flops 2154240 | bytes 2741760 | tf_op jit(solution)/shard_map/mul | solution.py:32
  54.3 0.5 fusion.76
  55.8 0.6 fusion.87
  57.0 0.6 pad_maximum_fusion.1.in_ref
  57.7 5.1 %shard_map.101 = f32[2,16,16]{2,1,0:T(8,128)} custom-call(f32[2,16,16]{2,1,0:T(8,128)} %pad_maximum_fusion.1.in_ref), custom_call_target="tpu_custom_call" | custom-call | tf_op jit(solution)/shard_map/pallas_call | solution.py:210
  62.7 0.7 %fusion.97 = (f32[16,16]{1,0:T(8,128)S(1)}, f32[16,16]{1,0:T(8,128)S(1)}) fusion(f32[16,16]{1,0:T(8,128)S(1)} %get-tuple-element.5, f32[2,16,16]{2,1,0:T(8,128)} %shard_map.101, f32[16,16]{1,0:T(8,128)S(1)} %get-tuple-element.6), kind=kLoop, calls=%fused_computation.158 | loop fusion | flops 1792 | bytes 6144 | tf_op jit(solution)/shard_map/div | solution.py:97
  63.5 2.3 %fusion.80 = f32[16,16,288]{2,1,0:T(8,128)} fusion(f32[16,16,288]{2,1,0:T(8,128)S(1)} %get-tuple-element.9, f32[288]{0:T(512)S(1)} %dynamic_slice.11, f32[16,16]{1,0:T(8,128)S(1)} %convert_element_type.47, f32[16,16]{1,0:T(8,128)S(1)} %get-tuple-element.47, f32[16,16]{1,0:T(8,128)S(1)} %get-tuple-element.46, f32[288]{0:T(512)S(1)} %get-tuple-element.53, ...), kind=kLoop, calls=%fused_computation.128 | loop fusion | flops 811008 | bytes 600576 | tf_op jit(solution)/shard_map/mul | solution.py:107
  (78 shorter events, 9.5 us)
Async XLA Ops:
  0.0 6.5 %copy-start.1 = (f32[16,16,288]{2,1,0:T(8,128)S(1)}, f32[16,16,288]{2,1,0:T(8,128)}, u32[]{:S(2)}) copy-start(f32[16,16,288]{2,1,0:T(8,128)} %param.10) | copy-start | bytes 884740
  29.7 2.0 %copy-start = (f32[32,32,312]{2,1,0:T(8,128)S(1)}, f32[32,32,312]{2,1,0:T(8,128)}, u32[]{:S(2)}) copy-start(f32[32,32,312]{2,1,0:T(8,128)} %shard_map.100) | copy-start | bytes 3833860
  56.5 7.0 %copy-start.2 = (f32[16,16]{1,0:T(8,128)S(1)}, f32[16,16]{1,0:T(8,128)}, u32[]{:S(2)}) copy-start(f32[16,16]{1,0:T(8,128)} %param.18) | copy-start | bytes 3076

commit v7 on v4

--- a/solution.py
+++ b/solution.py
@@ -232,16 +232,18 @@
     ice_share = ice_mask.astype(jnp.float32)
     speed_local = lax.dynamic_slice_in_dim(speed_table, band_index * freqs_dev, freqs_dev, 1)
     refr_local = lax.dynamic_slice_in_dim(refraction_table, band_index * freqs_dev, freqs_dev, 1)
-    group_speed = lookup(depth_class, speed_local) * sea_share[..., None]
-    turning = lookup(depth_class, refr_local) * sea_share[..., None]
-    turn_x = turning * depth_slope[0][..., None]
-    turn_y = turning * depth_slope[1][..., None]
-    density = spectrum * sea_share[..., None]
-
-    stacked = jnp.concatenate([density, group_speed, turn_x, turn_y], axis=-1)
+    point_inputs = [sea_share, depth_class.astype(jnp.float32), depth_slope[0], depth_slope[1]]
+    stacked = jnp.concatenate([spectrum] + [v[..., None] for v in point_inputs], axis=-1)
     stacked = halo_exchange(stacked, halo)
-    density = stacked[..., :comps_dev]
-    fields = stacked[..., comps_dev:]
+    sea_ext, class_ext, slope_x, slope_y = [stacked[..., comps_dev + i] for i in range(4)]
+    classes = jnp.arange(speed_table.shape[0]).astype(jnp.float32)
+    chosen = (class_ext[..., None] == classes)[..., None]
+    group_speed = jnp.sum(jnp.where(chosen, speed_local, 0.0), axis=2) * sea_ext[..., None]
+    turning = jnp.sum(jnp.where(chosen, refr_local, 0.0), axis=2) * sea_ext[..., None]
+    turn_x = turning * slope_x[..., None]
+    turn_y = turning * slope_y[..., None]
+    density = stacked[..., :comps_dev] * sea_ext[..., None]
+    fields = jnp.concatenate([group_speed, turn_x, turn_y], axis=-1)
 
     total_rows = rows_dev * lax.axis_size("lat")
     first_row = lax.axis_index("lat") * rows_dev - halo

time: 63.3 us -> 65.7 us (1.038)
  local copies, waits for them, and re-layouts: 8.7 us -> 14.7 us
  matrix products: 5.88 us -> 2.82 us
    slice x0 -> x1, local copies, waits for them, and re-layouts: none -> 3.07 us  [per_device(): stacked[..., comps_dev + i]]
    dot_general x2 -> x0, matrix products: 2 us -> none  [lookup(): return jnp.dot(onehot, lookup_table, precision=lax.Precision.HIGHEST)]
    concatenate x0 -> x1, local copies, waits for them, and re-layouts: none -> 1.94 us  [per_device(): jnp.concatenate([spectrum] + [v[..., None] for v in point_inputs], axis=-1)]
    another operation x0 -> x3, local copies, waits for them, and re-layouts: none -> 1.06 us  [per_device(): v[..., None]]
    dot_general x3, matrix products: 3.88 us -> 2.82 us  [expand(): return jnp.dot(per_freq, spread, precision=lax.Precision.HIGHEST)]
    concatenate x1 -> x0, other arithmetic: 0.92 us -> none  [per_device(): stacked = jnp.concatenate([density, group_speed, turn_x, turn_y], axis=-1)]
    mul x1, other arithmetic: 1.09 us -> 0.21 us  [per_device(): density = stacked[..., :comps_dev] * sea_ext[..., None]]
    mul x1 -> x0, local copies, waits for them, and re-layouts: 0.72 us -> none  [per_device(): turn_x = turning * depth_slope[0][..., None]]
where the time goes in v7:
time: 65.7 us; the launch traced here: 65.1 us
  Pallas kernels  22.2 us (34%)
  other arithmetic  21.2 us (32%)
  local copies, waits for them, and re-layouts  14.7 us (22%)
  matrix products  2.82 us (4%)
  waiting for transfers between devices  2.76 us (4%)
  starting transfers between devices  0.76 us (1%)
    pallas_call x1, Pallas kernels, halo_exchange(): pl.pallas_call(functools.partial(halo_kernel, halo=halo), out_shape=jax.S...  22.2 us
    mul x12, other arithmetic, quickest(): return courant * face_value  12.7 us
    slice x21, local copies, waits for them, and re-layouts, rotate(): inner_roll = jnp.roll(density, -offset, axis=-1)  3.76 us
    slice x1, local copies, waits for them, and re-layouts, per_device(): stacked[..., comps_dev + i]  3.07 us
    dot_general x3, matrix products, expand(): return jnp.dot(per_freq, spread, precision=lax.Precision.HIGHEST)  2.82 us
    ppermute x1, waiting for transfers between devices, per_device(): other = lax.ppermute(partial, 'band', [(0, 1), (1, 0)])  2.76 us
    slice x17, local copies, waits for them, and re-layouts, rotate(): outer_roll = jnp.roll(density, NDIR - offset, axis=-1)  2.34 us
    mul x1, other arithmetic, sources(): return sea_share[..., None] * density * jnp.exp(growth - breaking - damping)  2.33 us
  transfers between devices with their start and end apart: 1, of which 1 were waited for; matrix products, arithmetic and copies ran while one was open for 0% of the time, Pallas kernels for 0%

profile of v7, /device:TPU:2, one launch (start us, length us, event | category | flops | bytes accessed | tf_op | source)
XLA Modules:
  0.0 65.1 jit_solution(2663973378015613618)
XLA Ops:
  0.3 0.7 %fusion.148 = (f32[16,16]{1,0:T(8,128)S(1)}, f32[16,16,1]{1,0,2:T(8,128)S(1)}) fusion(s32[16,16]{1,0:T(8,128)} %param.11), kind=kLoop, calls=%fused_computation.236 | loop fusion | flops 256 | bytes 3072 | tf_op jit(solution)/shard_map/convert_element_type | solution.py:231
  1.1 0.7 %convert_bitcast_fusion = f32[16,16,1]{1,0,2:T(8,128)S(1)} fusion(s32[16,16]{1,0:T(8,128)} %param.13), kind=kLoop, calls=%fused_computation.177 | loop fusion | flops 256 | bytes 2048 | tf_op jit(solution)/shard_map/broadcast_in_dim | solution.py:236
  2.0 0.7 %slice_bitcast_fusion.2 = (f32[16,16,1]{1,0,2:T(8,128)S(1)}, f32[16,16,1]{1,0,2:T(8,128)S(1)}) fusion(f32[2,16,16]{2,1,0:T(8,128)} %param.16), kind=kLoop, calls=%fused_computation.175 | loop fusion | bytes 4096 | tf_op jit(solution)/shard_map/broadcast_in_dim;squeeze | solution.py:236
  3.1 1.9 %concatenate.123.in_ref = f32[16,16,292]{2,1,0:T(8,128)} concatenate(f32[16,16,288]{2,1,0:T(8,128)} %param.10, f32[16,16,1]{2,1,0:T(8,128)S(1)} %copy.15, f32[16,16,1]{2,1,0:T(8,128)S(1)} %copy.16, f32[16,16,1]{2,1,0:T(8,128)S(1)} %copy.17, f32[16,16,1]{2,1,0:T(8,128)S(1)} %copy.18), dimensions={2} | concatenate | bytes 598016 | tf_op jit(solution)/shard_map/concatenate | solution.py:236
  5.0 22.2 %shard_map.100 = f32[32,32,292]{2,1,0:T(8,128)} custom-call(f32[16,16,292]{2,1,0:T(8,128)} %concatenate.123.in_ref), custom_call_target="tpu_custom_call" | custom-call | tf_op jit(solution)/shard_map/pallas_call | solution.py:180
  27.2 3.1 %slice_reduce_fusion = (f32[32,32]{1,0:T(8,128)S(1)}, f32[32,32]{1,0:T(8,128)S(1)}, f32[32,32]{1,0:T(8,128)S(1)}, f32[32,32]{1,0:T(8,128)S(1)}) fusion(f32[32,32,292]{2,1,0:T(8,128)} %shard_map.100), kind=kLoop, calls=%fused_computation.116 | loop fusion | bytes 32768 | tf_op jit(solution)/shard_map/slice | solution.py:238
  30.7 0.4 copy-done.6
  31.1 0.4 select_reduce_fusion
  31.5 1.0 %broadcast_multiply_fusion = (f32[32,32,288]{2,1,0:T(8,128)S(1)}, f32[32,32,288]{2,1,0:T(8,128)S(1)}) fusion(f32[288]{0:T(512)S(1)} %get-tuple-element.59, f32[32]{0:T(128)S(1)} %cosine_divide_fusion, f32[288]{0:T(512)S(1)} %fusion.130, s32[288]{0:T(512)S(1)} %add_select_fusion.2, f32[32,32,8]{1,2,0:T(8,128)S(1)} %get-tuple-element.12, ...), kind=kOutput, calls=%fused_computation.83 | convolution fusion | flops 29206784 | bytes 2399744 | tf_op jit(solution)/shard_map/dot_general | solution.py:70
  32.5 1.7 %fusion.5 = f32[32,29,288]{2,1,0:T(8,128)S(1)} fusion(f32[32,32,288]{2,1,0:T(8,128)S(1)} %slice_multiply_fusion, f32[32,32,288]{2,1,0:T(8,128)S(1)} %get-tuple-element.15), kind=kLoop, calls=%fused_computation.7 | loop fusion | flops 5879808 | bytes 7483392 | tf_op jit(solution)/shard_map/mul | solution.py:32
  34.2 0.4 fusion
  34.6 1.0 %fusion.10 = f32[29,28,288]{2,1,0:T(8,128)S(1)} fusion(f32[32,28,288]{2,1,0:T(8,128)S(1)} %fusion, f32[32,32,288]{2,1,0:T(8,128)S(1)} %get-tuple-element.14), kind=kLoop, calls=%fused_computation.18 | loop fusion | flops 5144832 | bytes 6547968 | tf_op jit(solution)/shard_map/mul | solution.py:32
  36.4 0.5 fusion.134
  37.3 0.4 slice.745
  37.7 0.9 %fusion.93 = f32[32,32,288]{2,1,0:T(8,128)S(1)} fusion(f32[32,32,8]{1,2,0:T(8,128)S(1)} %get-tuple-element.11, f32[32,32]{1,0:T(8,128)S(1)} %get-tuple-element.6, f32[32,32]{1,0:T(8,128)S(1)} %get-tuple-element.8, s32[288]{0:T(512)S(1)} %add_select_fusion.2), kind=kOutput, calls=%fused_computation.153 | convolution fusion | flops 28330240 | bytes 1221760 | tf_op jit(solution)/shard_map/dot_general | solution.py:70
  38.6 1.0 %multiply_subtract_fusion = f32[32,32,288]{2,1,0:T(8,128)S(1)} fusion(f32[32,32,288]{2,1,0:T(8,128)S(1)} %fusion.93, f32[288]{0:T(512)S(1)} %get-tuple-element.57, f32[288]{0:T(512)S(1)} %get-tuple-element.58, f32[32,32,8]{1,2,0:T(8,128)S(1)} %get-tuple-element.11, f32[32,32]{1,0:T(8,128)S(1)} %get-tuple-element.5, f32[32,32]{1,0:T(8,128)S(1)} %get-tuple-element.8, ...), kind=kOutput, calls=%fused_computation.10 | convolution fusion | flops 29214976 | bytes 2403712 | tf_op jit(solution)/shard_map/dot_general | solution.py:70
  40.4 2.5 %fusion.22 = f32[28,28,288]{2,1,0:T(8,128)S(1)} fusion(f32[28,28,35]{2,1,0:T(8,128)S(1)} %get-tuple-element.17, f32[28,28,253]{2,1,0:T(8,128)S(1)} %get-tuple-element.19, f32[28,28,287]{2,1,0:T(8,128)S(1)} %get-tuple-element.21, f32[28,28,1]{2,1,0:T(8,128)S(1)} %get-tuple-element.23, f32[28,28,288]{2,1,0:T(8,128)S(1)} %copy-done.1, ...), kind=kLoop, calls=%fused_computation.38 | loop fusion | flops 6547968 | bytes 8129376 | tf_op jit(solution)/shard_map/mul | solution.py:32
  43.6 0.7 %fusion.26 = f32[28,28,288]{2,1,0:T(8,128)S(1)} fusion(f32[28,28,288]{2,1,0:T(8,128)S(1)} %copy-done.1, f32[28,28,288]{2,1,0:T(8,128)S(1)} %fusion.22, f32[28,28,35]{2,1,0:T(8,128)S(1)} %slice.748, f32[28,28,253]{2,1,0:T(8,128)S(1)} %slice.747, f32[28,28,287]{2,1,0:T(8,128)S(1)} %bitcast.37, f32[28,28,1]{2,1,0:T(8,128)S(1)} %slice.749, ...), kind=kLoop, calls=%fused_computation.44 | loop fusion | flops 1128960 | bytes 4516128 | tf_op jit(solution)/shard_map/sub | solution.py:66
  44.3 1.4 %fusion.15 = f32[28,25,288]{2,1,0:T(8,128)S(1)} fusion(f32[28,28,288]{2,1,0:T(8,128)S(1)} %fusion.26, f32[32,32,288]{2,1,0:T(8,128)S(1)} %get-tuple-element.15), kind=kLoop, calls=%fused_computation.26 | loop fusion | flops 4435200 | bytes 5644800 | tf_op jit(solution)/shard_map/mul | solution.py:32
  46.0 0.6 fusion.32
  48.1 1.2 %fusion.45 = f32[24,24,288]{2,1,0:T(8,128)S(1)} fusion(f32[24,24,35]{2,1,0:T(8,128)S(1)} %get-tuple-element.25, f32[24,24,253]{2,1,0:T(8,128)S(1)} %get-tuple-element.27, f32[24,24,287]{2,1,0:T(8,128)S(1)} %get-tuple-element.29, f32[24,24,1]{2,1,0:T(8,128)S(1)} %get-tuple-element.31, f32[24,24,288]{2,1,0:T(8,128)S(1)} %fusion.40, ...), kind=kLoop, calls=%fused_computation.76 | loop fusion | flops 4810752 | bytes 5972832 | tf_op jit(solution)/shard_map/mul | solution.py:32
  49.8 0.5 fusion.49
  50.3 0.9 %fusion.38 = f32[24,21,288]{2,1,0:T(8,128)S(1)} fusion(f32[24,24,288]{2,1,0:T(8,128)S(1)} %fusion.49, f32[32,32,288]{2,1,0:T(8,128)S(1)} %get-tuple-element.15), kind=kLoop, calls=%fused_computation.64 | loop fusion | flops 3193344 | bytes 4064256 | tf_op jit(solution)/shard_map/mul | solution.py:32
  51.5 0.5 fusion.54
  53.3 1.1 %fusion.66 = f32[20,20,288]{2,1,0:T(8,128)S(1)} fusion(f32[20,20,35]{2,1,0:T(8,128)S(1)} %get-tuple-element.33, f32[20,20,253]{2,1,0:T(8,128)S(1)} %get-tuple-element.35, f32[20,20,287]{2,1,0:T(8,128)S(1)} %get-tuple-element.37, f32[20,20,1]{2,1,0:T(8,128)S(1)} %get-tuple-element.39, f32[20,20,288]{2,1,0:T(8,128)S(1)} %fusion.61, ...), kind=kLoop, calls=%fused_computation.109 | loop fusion | flops 3340800 | bytes 4148064 | tf_op jit(solution)/shard_map/mul | solution.py:32
  54.9 0.4 fusion.70
  55.3 0.7 %fusion.59 = f32[20,17,288]{2,1,0:T(8,128)S(1)} fusion(f32[20,20,288]{2,1,0:T(8,128)S(1)} %fusion.70, f32[32,32,288]{2,1,0:T(8,128)S(1)} %get-tuple-element.15), kind=kLoop, calls=%fused_computation.97 | loop fusion | flops 2154240 | bytes 2741760 | tf_op jit(solution)/shard_map/mul | solution.py:32
  57.6 0.6 fusion.87
  58.5 0.4 multiply_reduce_fusion
  58.9 0.8 %collective-permute-start = (f32[2,16,16]{2,1,0:T(8,128)S(1)}, f32[2,16,16]{2,1,0:T(8,128)S(1)}, u32[]{:S(2)}, u32[]{:S(2)}) collective-permute-start(f32[2,16,16]{2,1,0:T(8,128)S(1)} %pad_maximum_fusion), channel_id=1, source_target_pairs={{0,1},{1,0},{2,3},{3,2},{4,5},{5,4},{6,7},{7,6},{8,9},{9,8},{10,11... | collective-permute-start | bytes 6152 | tf_op jit(solution)/shard_map/ppermute | solution.py:272
  60.0 2.8 %collective-permute-done = f32[2,16,16]{2,1,0:T(8,128)S(1)} collective-permute-done((f32[2,16,16]{2,1,0:T(8,128)S(1)}, f32[2,16,16]{2,1,0:T(8,128)S(1)}, u32[]{:S(2)}, u32[]{:S(2)}) %collective-permute-start) | collective-permute-done | bytes 2080 | tf_op jit(solution)/shard_map/ppermute | solution.py:272
  62.8 2.3 %fusion.80 = f32[16,16,288]{2,1,0:T(8,128)} fusion(f32[16,16,288]{2,1,0:T(8,128)S(1)} %get-tuple-element.13, f32[288]{0:T(512)S(1)} %dynamic_slice.11, f32[16,16]{1,0:T(8,128)S(1)} %convert_element_type.59, f32[16,16]{1,0:T(8,128)S(1)} %get-tuple-element.49, f32[16,16]{1,0:T(8,128)S(1)} %get-tuple-element.48, f32[288]{0:T(512)S(1)} %get-tuple-element.54, ...), kind=kLoop, calls=%fused_computation.134 | loop fusion | flops 811008 | bytes 600576 | tf_op jit(solution)/shard_map/mul | solution.py:107
  (97 shorter events, 10.0 us)
Async XLA Ops:
  27.2 3.1 %copy-start.2 = (f32[32,32,292]{2,1,0:T(8,128)S(1)}, f32[32,32,292]{2,1,0:T(8,128)}, u32[]{:S(2)}) copy-start(f32[32,32,292]{2,1,0:T(8,128)} %shard_map.100) | copy-start | bytes 3588100
  30.3 0.7 %copy-start.6 = (f32[8,16]{1,0:T(8,128)S(1)}, f32[8,16]{1,0:T(8,128)}, u32[]{:S(2)}) copy-start(f32[8,16]{1,0:T(8,128)} %param.15) | copy-start | bytes 1540
  30.3 0.7 %copy-start.7 = (f32[8,16]{1,0:T(8,128)S(1)}, f32[8,16]{1,0:T(8,128)}, u32[]{:S(2)}) copy-start(f32[8,16]{1,0:T(8,128)} %param.14) | copy-start | bytes 1540
  35.8 1.4 %copy-start = (f32[28,28,288]{2,1,0:T(8,128)}, f32[28,28,288]{2,1,0:T(8,128)S(1)}, u32[]{:S(2)}) copy-start(f32[28,28,288]{2,1,0:T(8,128)S(1)} %fusion.17) | copy-start | bytes 2709508
  38.6 1.3 %copy-start.1 = (f32[28,28,288]{2,1,0:T(8,128)S(1)}, f32[28,28,288]{2,1,0:T(8,128)}, u32[]{:S(2)}) copy-start(f32[28,28,288]{2,1,0:T(8,128)} %copy-done) | copy-start | bytes 2709508
  38.6 1.6 %slice-start = ((f32[28,28,288]{2,1,0:T(8,128)}), f32[28,28,254]{2,1,0:T(8,128)S(1)}, s32[]{:S(2)}) async-start(f32[28,28,288]{2,1,0:T(8,128)} %copy-done), calls=%async_computation | async-start | bytes 1835008 | tf_op jit(solution)/shard_map/jit(_roll_static)/slice | solution.py:58
  38.6 1.8 %slice-start.1 = ((f32[28,28,288]{2,1,0:T(8,128)}), f32[28,28,2]{2,1,0:T(8,128)S(1)}, s32[]{:S(2)}) async-start(f32[28,28,288]{2,1,0:T(8,128)} %copy-done), calls=%async_computation.1 | async-start | bytes 917504 | tf_op jit(solution)/shard_map/jit(_roll_static)/slice | solution.py:56
  58.3 1.4 %copy-start.4 = (f32[16,16]{1,0:T(8,128)S(1)}, f32[16,16]{1,0:T(8,128)}, u32[]{:S(2)}) copy-start(f32[16,16]{1,0:T(8,128)} %param.17) | copy-start | bytes 3076
  58.3 1.4 %copy-start.8 = (f32[16]{0:T(128)S(1)}, f32[16]{0:T(128)}, u32[]{:S(2)}) copy-start(f32[16]{0:T(128)} %param.19) | copy-start | bytes 196
  58.4 1.5 %copy-start.5 = (s32[16,16]{1,0:T(8,128)S(1)}, s32[16,16]{1,0:T(8,128)}, u32[]{:S(2)}) copy-start(s32[16,16]{1,0:T(8,128)} %param.12) | copy-start | bytes 3076
  58.4 4.4 %copy-start.3 = (f32[16,16]{1,0:T(8,128)S(1)}, f32[16,16]{1,0:T(8,128)}, u32[]{:S(2)}) copy-start(f32[16,16]{1,0:T(8,128)} %param.18) | copy-start | bytes 3076
  58.9 3.8 %collective-permute-start = (f32[2,16,16]{2,1,0:T(8,128)S(1)}, f32[2,16,16]{2,1,0:T(8,128)S(1)}, u32[]{:S(2)}, u32[]{:S(2)}) collective-permute-start(f32[2,16,16]{2,1,0:T(8,128)S(1)} %pad_maximum_fusion), channel_id=1, source_target_pairs={{0,1},{1,0},{2,3},{3,2},{4,5},{5,4},{6,7},{7,6},{8,9},{9,8},{10,11... | collective-permute-start | bytes 6152 | tf_op jit(solution)/shard_map/ppermute | solution.py:272

commit v8 on v5

--- a/solution.py
+++ b/solution.py
@@ -50,15 +50,18 @@
     return piece(density, 2, length - 2) - (piece(fluxes, 1, faces) - piece(fluxes, 0, faces - 1))
 
 
+def shifted(density, offset):
+    edges = [(0, 0, 0)] * (density.ndim - 1) + [(-offset, offset, 0)]
+    return lax.pad(density, jnp.zeros((), density.dtype), edges)
+
+
 def rotate(density, offset):
     dir_index = jnp.arange(density.shape[-1]) % NDIR
     target = dir_index + offset
-    inner_roll = jnp.roll(density, -offset, axis=-1)
+    inner = shifted(density, offset)
     if offset > 0:
-        outer_roll = jnp.roll(density, NDIR - offset, axis=-1)
-        return jnp.where(target >= NDIR, outer_roll, inner_roll)
-    outer_roll = jnp.roll(density, -(offset + NDIR), axis=-1)
-    return jnp.where(target < 0, outer_roll, inner_roll)
+        return jnp.where(target >= NDIR, shifted(density, offset - NDIR), inner)
+    return jnp.where(target < 0, shifted(density, offset + NDIR), inner)
 
 
 def refract(density, courant):

time: 63.2 us -> 55.9 us (0.88)
  local copies, waits for them, and re-layouts: 9.53 us -> 2.24 us
    slice x46 -> x0, local copies, waits for them, and re-layouts: 6.95 us -> none  [the longest x21 3.59 us: rotate(): inner_roll = jnp.roll(density, -offset, axis=-1)]
where the time goes in v8:
time: 55.9 us; the launch traced here: 55.4 us
  other arithmetic  23.2 us (42%)
  Pallas kernels  22.2 us (40%)
  matrix products  3.88 us (7%)
  waiting for transfers between devices  2.76 us (5%)
  local copies, waits for them, and re-layouts  2.24 us (4%)
  starting transfers between devices  0.77 us (1%)
    pallas_call x1, Pallas kernels, halo_exchange(): pl.pallas_call(functools.partial(halo_kernel, halo=halo), out_shape=jax.S...  22.2 us
    mul x12, other arithmetic, quickest(): return courant * face_value  13 us
    dot_general x3, matrix products, expand(): return jnp.dot(per_freq, spread, precision=lax.Precision.HIGHEST)  3.88 us
    ppermute x1, waiting for transfers between devices, per_device(): other = lax.ppermute(partial, 'band', [(0, 1), (1, 0)])  2.76 us
    mul x1, other arithmetic, sources(): return sea_share[..., None] * density * jnp.exp(growth - breaking - damping)  2.34 us
    sub x3, other arithmetic, refract(): return density - (fluxes - rotate(fluxes, -1))  1.81 us
  transfers between devices with their start and end apart: 1, of which 1 were waited for; matrix products, arithmetic and copies ran while one was open for 0% of the time, Pallas kernels for 0%

profile of v8, /device:TPU:2, one launch (start us, length us, event | category | flops | bytes accessed | tf_op | source)
XLA Modules:
  0.0 55.4 jit_solution(5203779938975665822)
XLA Ops:
  0.6 0.7 %iota_compare_fusion = pred[16,16,8]{1,2,0:T(8,128)(4,1)S(1)} fusion(s32[16,16]{1,0:T(8,128)} %param.13), kind=kLoop, calls=%fused_computation.107 | loop fusion | flops 2048 | bytes 3072 | tf_op jit(solution)/shard_map/eq | solution.py:238
  1.3 0.8 %constant_dynamic-slice_fusion = (f32[8,8]{1,0:T(8,128)S(1)}, f32[8,8]{1,0:T(8,128)S(1)}) fusion(f32[8,16]{1,0:T(8,128)} %param.15, s32[]{:T(128)S(6)} %select_n.243, f32[8,16]{1,0:T(8,128)} %param.14), kind=kLoop, calls=%fused_computation.157 | loop fusion | bytes 1028 | tf_op jit(solution)/shard_map/dynamic_slice | solution.py:237
  2.1 0.3 select_reduce_fusion.1
  2.5 0.7 %convert_element_type.43 = f32[16,16]{1,0:T(8,128)S(1)} convert(s32[16,16]{1,0:T(8,128)} %param.11) | non-fusion elementwise | flops 256 | bytes 2048 | tf_op jit(solution)/shard_map/convert_element_type | solution.py:234
  3.2 0.7 %slice_bitcast_fusion.3 = (f32[16,16]{1,0:T(8,128)S(1)}, f32[16,16]{1,0:T(8,128)S(1)}) fusion(f32[2,16,16]{2,1,0:T(8,128)} %param.16), kind=kLoop, calls=%fused_computation.119 | loop fusion | bytes 4096 | tf_op jit(solution)/shard_map/mul | solution.py:241
  4.0 1.1 %broadcast_multiply_fusion.1 = f32[16,16,288]{2,1,0:T(8,128)S(1)} fusion(f32[16,16,288]{2,1,0:T(8,128)} %param.10, f32[16,16]{1,0:T(8,128)S(1)} %convert_element_type.43), kind=kLoop, calls=%fused_computation.103 | loop fusion | flops 73728 | bytes 590848 | tf_op jit(solution)/shard_map/mul | solution.py:243
  5.2 0.9 %pad_maximum_fusion.in_ref = f32[16,16,312]{2,1,0:T(8,128)} fusion(f32[16,16,8]{2,1,0:T(8,128)S(1)} %get-tuple-element.13, f32[16,16,8]{2,1,0:T(8,128)S(1)} %get-tuple-element.12, f32[16,16,8]{2,1,0:T(8,128)S(1)} %get-tuple-element.18, f32[16,16,288]{2,1,0:T(8,128)S(1)} %broadcast_multiply_fusion.1), kind=kLoop, calls=%fused_computation.99 | loop fusion | flops 239616 | bytes 638976 | tf_op jit(solution)/shard_map/concatenate | solution.py:245
  6.2 22.2 %shard_map.100 = f32[32,32,312]{2,1,0:T(8,128)} custom-call(f32[16,16,312]{2,1,0:T(8,128)} %pad_maximum_fusion.in_ref), custom_call_target="tpu_custom_call" | custom-call | tf_op jit(solution)/shard_map/pallas_call | solution.py:183
  28.4 2.0 %fusion.40 = f32[32,32,288]{2,1,0:T(8,128)S(1)} fusion(f32[32,32,312]{2,1,0:T(8,128)} %shard_map.100, s32[288]{0:T(512)S(1)} %add_select_fusion.2), kind=kOutput, calls=%fused_computation.75 | convolution fusion | flops 28313856 | bytes 1705088 | tf_op jit(solution)/shard_map/dot_general | solution.py:73
  30.4 0.9 %broadcast_multiply_fusion = (f32[32,32,288]{2,1,0:T(8,128)S(1)}, f32[32,32,288]{2,1,0:T(8,128)S(1)}) fusion(f32[288]{0:T(512)S(1)} %get-tuple-element.24, f32[32]{0:T(128)S(1)} %cosine_divide_fusion, f32[288]{0:T(512)S(1)} %fusion.82, s32[288]{0:T(512)S(1)} %add_select_fusion.2, f32[32,32,312]{2,1,0:T(8,128)S(1)} %copy-done), kind=kOutput, calls=%fused_computation.52 | convolution fusion | flops 29198592 | bytes 2890240 | tf_op jit(solution)/shard_map/dot_general | solution.py:73
  31.3 1.6 %subtract_multiply_fusion = f32[32,29,288]{2,1,0:T(8,128)S(1)} fusion(f32[32,32,312]{2,1,0:T(8,128)S(1)} %copy-done, f32[32,32,288]{2,1,0:T(8,128)S(1)} %get-tuple-element.11), kind=kLoop, calls=%fused_computation.4 | loop fusion | flops 5879808 | bytes 7483392 | tf_op jit(solution)/shard_map/mul | solution.py:32
  32.9 0.4 fusion
  33.3 1.0 %fusion.5 = f32[29,28,288]{2,1,0:T(8,128)S(1)} fusion(f32[32,28,288]{2,1,0:T(8,128)S(1)} %fusion, f32[32,32,288]{2,1,0:T(8,128)S(1)} %get-tuple-element.10), kind=kLoop, calls=%fused_computation.11 | loop fusion | flops 5144832 | bytes 6547968 | tf_op jit(solution)/shard_map/mul | solution.py:32
  34.5 1.0 %multiply_subtract_fusion = f32[32,32,288]{2,1,0:T(8,128)S(1)} fusion(f32[32,32,288]{2,1,0:T(8,128)S(1)} %fusion.40, f32[288]{0:T(512)S(1)} %get-tuple-element.22, f32[288]{0:T(512)S(1)} %get-tuple-element.23, f32[32,32,312]{2,1,0:T(8,128)S(1)} %copy-done, s32[288]{0:T(512)S(1)} %add_select_fusion.2), kind=kOutput, calls=%fused_computation.3 | convolution fusion | flops 29198592 | bytes 3282944 | tf_op jit(solution)/shard_map/dot_general | solution.py:73
  35.5 2.5 %subtract_multiply_fusion.1 = f32[28,28,288]{2,1,0:T(8,128)S(1)} fusion(f32[28,28,288]{2,1,0:T(8,128)S(1)} %fusion.12, f32[32,32,288]{2,1,0:T(8,128)S(1)} %multiply_subtract_fusion, pred[288]{0:T(512)(128)(4,1)S(1)} %get-tuple-element.27, pred[288]{0:T(512)(128)(4,1)S(1)} %get-tuple-element.28, pred[288]{0:T(512)(128)(4,1)S(1)} %add_compare_fusion.2), kind=kLoop, calls=%fused_computation.26 | loop fusion | flops 5193216 | bytes 2710368 | tf_op jit(solution)/shard_map/mul | solution.py:32
  38.0 0.8 %subtract_subtract_fusion = f32[28,28,288]{2,1,0:T(8,128)S(1)} fusion(f32[28,28,288]{2,1,0:T(8,128)S(1)} %fusion.12, f32[28,28,288]{2,1,0:T(8,128)S(1)} %subtract_multiply_fusion.1, pred[288]{0:T(512)(128)(4,1)S(1)} %get-tuple-element.28), kind=kLoop, calls=%fused_computation.25 | loop fusion | flops 677376 | bytes 2709792 | tf_op jit(solution)/shard_map/sub | solution.py:69
  38.8 1.4 %fusion.10 = f32[28,25,288]{2,1,0:T(8,128)S(1)} fusion(f32[28,28,288]{2,1,0:T(8,128)S(1)} %subtract_subtract_fusion, f32[32,32,288]{2,1,0:T(8,128)S(1)} %get-tuple-element.11), kind=kLoop, calls=%fused_computation.19 | loop fusion | flops 4435200 | bytes 5644800 | tf_op jit(solution)/shard_map/mul | solution.py:32
  40.3 0.3 fusion.13
  40.5 0.6 %fusion.18 = f32[25,24,288]{2,1,0:T(8,128)S(1)} fusion(f32[28,24,288]{2,1,0:T(8,128)S(1)} %fusion.13, f32[32,32,288]{2,1,0:T(8,128)S(1)} %get-tuple-element.10), kind=kLoop, calls=%fused_computation.34 | loop fusion | flops 3801600 | bytes 4838400 | tf_op jit(solution)/shard_map/mul | solution.py:32
  41.4 1.5 %subtract_multiply_fusion.2 = f32[24,24,288]{2,1,0:T(8,128)S(1)} fusion(f32[24,24,288]{2,1,0:T(8,128)S(1)} %fusion.26, f32[32,32,288]{2,1,0:T(8,128)S(1)} %multiply_subtract_fusion, pred[288]{0:T(512)(128)(4,1)S(1)} %get-tuple-element.27, pred[288]{0:T(512)(128)(4,1)S(1)} %get-tuple-element.28, pred[288]{0:T(512)(128)(4,1)S(1)} %add_compare_fusion.2), kind=kLoop, calls=%fused_computation.51 | loop fusion | flops 3815424 | bytes 1991520 | tf_op jit(solution)/shard_map/mul | solution.py:32
  42.8 0.5 subtract_subtract_fusion.1
  43.4 0.9 %fusion.24 = f32[24,21,288]{2,1,0:T(8,128)S(1)} fusion(f32[24,24,288]{2,1,0:T(8,128)S(1)} %subtract_subtract_fusion.1, f32[32,32,288]{2,1,0:T(8,128)S(1)} %get-tuple-element.11), kind=kLoop, calls=%fused_computation.44 | loop fusion | flops 3193344 | bytes 4064256 | tf_op jit(solution)/shard_map/mul | solution.py:32
  44.5 0.5 fusion.31
  45.2 1.2 %subtract_multiply_fusion.3 = f32[20,20,288]{2,1,0:T(8,128)S(1)} fusion(f32[20,20,288]{2,1,0:T(8,128)S(1)} %fusion.38, f32[32,32,288]{2,1,0:T(8,128)S(1)} %multiply_subtract_fusion, pred[288]{0:T(512)(128)(4,1)S(1)} %get-tuple-element.27, pred[288]{0:T(512)(128)(4,1)S(1)} %get-tuple-element.28, pred[288]{0:T(512)(128)(4,1)S(1)} %add_compare_fusion.2), kind=kLoop, calls=%fused_computation.73 | loop fusion | flops 2649600 | bytes 1383264 | tf_op jit(solution)/shard_map/mul | solution.py:32
  46.4 0.5 subtract_subtract_fusion.2
  46.8 0.7 %fusion.36 = f32[20,17,288]{2,1,0:T(8,128)S(1)} fusion(f32[20,20,288]{2,1,0:T(8,128)S(1)} %subtract_subtract_fusion.2, f32[32,32,288]{2,1,0:T(8,128)S(1)} %get-tuple-element.11), kind=kLoop, calls=%fused_computation.66 | loop fusion | flops 2154240 | bytes 2741760 | tf_op jit(solution)/shard_map/mul | solution.py:32
  47.7 0.3 fusion.49
  48.1 0.7 %subtract_multiply_fusion.4 = f32[16,16,288]{2,1,0:T(8,128)S(1)} fusion(f32[16,16,288]{2,1,0:T(8,128)S(1)} %fusion.55, f32[32,32,288]{2,1,0:T(8,128)S(1)} %multiply_subtract_fusion, pred[288]{0:T(512)(128)(4,1)S(1)} %get-tuple-element.27, pred[288]{0:T(512)(128)(4,1)S(1)} %get-tuple-element.28, pred[288]{0:T(512)(128)(4,1)S(1)} %add_compare_fusion.2), kind=kLoop, calls=%fused_computation.102 | loop fusion | flops 1695744 | bytes 885600 | tf_op jit(solution)/shard_map/mul | solution.py:32
  48.8 0.4 multiply_reduce_fusion
  49.2 0.8 %collective-permute-start = (f32[2,16,16]{2,1,0:T(8,128)S(1)}, f32[2,16,16]{2,1,0:T(8,128)S(1)}, u32[]{:S(2)}, u32[]{:S(2)}) collective-permute-start(f32[2,16,16]{2,1,0:T(8,128)S(1)} %pad_maximum_fusion.1), channel_id=1, source_target_pairs={{0,1},{1,0},{2,3},{3,2},{4,5},{5,4},{6,7},{7,6},{8,9},{9,8},{10,11... | collective-permute-start | bytes 6152 | tf_op jit(solution)/shard_map/ppermute | solution.py:274
  50.3 2.8 %collective-permute-done = f32[2,16,16]{2,1,0:T(8,128)S(1)} collective-permute-done((f32[2,16,16]{2,1,0:T(8,128)S(1)}, f32[2,16,16]{2,1,0:T(8,128)S(1)}, u32[]{:S(2)}, u32[]{:S(2)}) %collective-permute-start) | collective-permute-done | bytes 2080 | tf_op jit(solution)/shard_map/ppermute | solution.py:274
  53.0 2.3 %fusion.53 = f32[16,16,288]{2,1,0:T(8,128)} fusion(f32[16,16,288]{2,1,0:T(8,128)S(1)} %get-tuple-element.9, f32[288]{0:T(512)S(1)} %dynamic_slice.11, f32[16,16]{1,0:T(8,128)S(1)} %convert_element_type.47, f32[16,16]{1,0:T(8,128)S(1)} %get-tuple-element.15, f32[16,16]{1,0:T(8,128)S(1)} %get-tuple-element.14, f32[288]{0:T(512)S(1)} %get-tuple-element.19, ...), kind=kLoop, calls=%fused_computation.95 | loop fusion | flops 811008 | bytes 600576 | tf_op jit(solution)/shard_map/mul | solution.py:110
  (39 shorter events, 2.1 us)
Async XLA Ops:
  28.4 2.0 %copy-start = (f32[32,32,312]{2,1,0:T(8,128)S(1)}, f32[32,32,312]{2,1,0:T(8,128)}, u32[]{:S(2)}) copy-start(f32[32,32,312]{2,1,0:T(8,128)} %shard_map.100) | copy-start | bytes 3833860
  48.1 1.9 %copy-start.2 = (f32[16,16]{1,0:T(8,128)S(1)}, f32[16,16]{1,0:T(8,128)}, u32[]{:S(2)}) copy-start(f32[16,16]{1,0:T(8,128)} %param.17) | copy-start | bytes 3076
  48.1 1.9 %copy-start.4 = (f32[16]{0:T(128)S(1)}, f32[16]{0:T(128)}, u32[]{:S(2)}) copy-start(f32[16]{0:T(128)} %param.19) | copy-start | bytes 196
  48.1 2.1 %copy-start.3 = (s32[16,16]{1,0:T(8,128)S(1)}, s32[16,16]{1,0:T(8,128)}, u32[]{:S(2)}) copy-start(s32[16,16]{1,0:T(8,128)} %param.12) | copy-start | bytes 3076
  48.1 4.9 %copy-start.1 = (f32[16,16]{1,0:T(8,128)S(1)}, f32[16,16]{1,0:T(8,128)}, u32[]{:S(2)}) copy-start(f32[16,16]{1,0:T(8,128)} %param.18) | copy-start | bytes 3076
  49.2 3.8 %collective-permute-start = (f32[2,16,16]{2,1,0:T(8,128)S(1)}, f32[2,16,16]{2,1,0:T(8,128)S(1)}, u32[]{:S(2)}, u32[]{:S(2)}) collective-permute-start(f32[2,16,16]{2,1,0:T(8,128)S(1)} %pad_maximum_fusion.1), channel_id=1, source_target_pairs={{0,1},{1,0},{2,3},{3,2},{4,5},{5,4},{6,7},{7,6},{8,9},{9,8},{10,11... | collective-permute-start | bytes 6152 | tf_op jit(solution)/shard_map/ppermute | solution.py:274

commit v9 on v8

--- a/solution.py
+++ b/solution.py
@@ -35,19 +35,14 @@
 def advect(density, cell_speed, axis_dim):
     length = density.shape[axis_dim]
 
-    def piece(array, low, high):
-        return lax.slice_in_dim(array, low, high, axis=axis_dim)
-
-    courant = 0.5 * (piece(cell_speed, 1, length - 2) + piece(cell_speed, 2, length - 1))
-    fluxes = quickest(
-        piece(density, 0, length - 3),
-        piece(density, 1, length - 2),
-        piece(density, 2, length - 1),
-        piece(density, 3, length),
-        courant,
-    )
-    faces = fluxes.shape[axis_dim]
-    return piece(density, 2, length - 2) - (piece(fluxes, 1, faces) - piece(fluxes, 0, faces - 1))
+    def piece(array, low):
+        return lax.slice_in_dim(array, low, low + length - 4, axis=axis_dim)
+
+    def face(low):
+        courant = 0.5 * (piece(cell_speed, low + 1) + piece(cell_speed, low + 2))
+        return quickest(*[piece(density, low + i) for i in range(4)], courant)
+
+    return piece(density, 2) - (face(1) - face(0))
 
 
 def shifted(density, offset):
@@ -64,9 +59,12 @@
     return jnp.where(target < 0, shifted(density, offset + NDIR), inner)
 
 
-def refract(density, courant):
-    fluxes = quickest(rotate(density, -1), density, rotate(density, 1), rotate(density, 2), courant)
-    return density - (fluxes - rotate(fluxes, -1))
+def refract(density, courant, courant_behind):
+    behind = rotate(density, -1)
+    forward = rotate(density, 1)
+    fluxes = quickest(behind, density, forward, rotate(density, 2), courant)
+    behind_fluxes = quickest(rotate(density, -2), behind, density, forward, courant_behind)
+    return density - (fluxes - behind_fluxes)
 
 
 def expand(per_freq, spread):
@@ -259,14 +257,19 @@
         expand(fields[..., freqs_dev : 2 * freqs_dev], spread) * sin_face
         - expand(fields[..., 2 * freqs_dev :], spread) * cos_face
     )
+    along_t_behind = rotate(along_t, -1)
     for substep in range(ITERS):
         density = advect(density, along_x, 1)
-        along_x, along_y, along_t = [trim(a, 1, 2) for a in (along_x, along_y, along_t)]
+        along_x, along_y, along_t, along_t_behind = [
+            trim(a, 1, 2) for a in (along_x, along_y, along_t, along_t_behind)
+        ]
         density = advect(density, along_y, 0)
         inside = trim(inside, 0, 2)
         density = jnp.where(inside, density, 0.0)
-        along_x, along_y, along_t = [trim(a, 0, 2) for a in (along_x, along_y, along_t)]
-        density = refract(density, along_t)
+        along_x, along_y, along_t, along_t_behind = [
+            trim(a, 0, 2) for a in (along_x, along_y, along_t, along_t_behind)
+        ]
+        density = refract(density, along_t, along_t_behind)
 
     levels = jnp.exp(math.log(freq_ratio) * (comp_index // NDIR).astype(jnp.float32))
     ice_loss = lax.dynamic_slice_in_dim(jnp.repeat(ice_rate, NDIR), first_comp, comps_dev, 0)

time: 55.9 us -> 59.8 us (1.070)
  other arithmetic: 23.2 us -> 27.2 us
    mul x12 -> x0, other arithmetic: 13 us -> none  [quickest(): return courant * face_value]
    sub x7, other arithmetic: 2.74 us -> 14.3 us  [the longest x4 7.41 us: advect(): return piece(density, 2) - (face(1) - face(0))]
    select_n x4, other arithmetic: 0.6 us -> 4.54 us  [per_device(): density = jnp.where(inside, density, 0.0)]
    select_n x0 -> x1, other arithmetic: none -> 0.88 us  [rotate(): return jnp.where(target < 0, shifted(density, offset + NDIR), inner)]
    reduce_sum x1, other arithmetic: 0.38 us -> 1 us  [per_device(): jnp.sum(density * levels, axis=-1)]
where the time goes in v9:
time: 59.8 us; the launch traced here: 59.3 us
  other arithmetic  27.2 us (45%)
  Pallas kernels  22.2 us (37%)
  matrix products  3.9 us (7%)
  waiting for transfers between devices  2.76 us (5%)
  local copies, waits for them, and re-layouts  2.24 us (4%)
  starting transfers between devices  0.77 us (1%)
    pallas_call x1, Pallas kernels, halo_exchange(): pl.pallas_call(functools.partial(halo_kernel, halo=halo), out_shape=jax.S...  22.2 us
    sub x4, other arithmetic, advect(): return piece(density, 2) - (face(1) - face(0))  7.41 us
    sub x3, other arithmetic, refract(): return density - (fluxes - behind_fluxes)  6.86 us
    select_n x4, other arithmetic, per_device(): density = jnp.where(inside, density, 0.0)  4.54 us
    dot_general x3, matrix products, expand(): return jnp.dot(per_freq, spread, precision=lax.Precision.HIGHEST)  3.9 us
    ppermute x1, waiting for transfers between devices, per_device(): other = lax.ppermute(partial, 'band', [(0, 1), (1, 0)])  2.76 us
    mul x1, other arithmetic, sources(): return sea_share[..., None] * density * jnp.exp(growth - breaking - damping)  2.34 us
  transfers between devices with their start and end apart: 1, of which 1 were waited for; matrix products, arithmetic and copies ran while one was open for 0% of the time, Pallas kernels for 0%

profile of v9, /device:TPU:2, one launch (start us, length us, event | category | flops | bytes accessed | tf_op | source)
XLA Modules:
  0.0 59.3 jit_solution(1383247831803444607)
XLA Ops:
  0.6 0.7 %iota_compare_fusion = pred[16,16,8]{1,2,0:T(8,128)(4,1)S(1)} fusion(s32[16,16]{1,0:T(8,128)} %param.13), kind=kLoop, calls=%fused_computation.138 | loop fusion | flops 2048 | bytes 3072 | tf_op jit(solution)/shard_map/eq | solution.py:236
  1.3 0.8 %constant_dynamic-slice_fusion = (f32[8,8]{1,0:T(8,128)S(1)}, f32[8,8]{1,0:T(8,128)S(1)}) fusion(f32[8,16]{1,0:T(8,128)} %param.15, s32[]{:T(128)S(6)} %select_n.283, f32[8,16]{1,0:T(8,128)} %param.14), kind=kLoop, calls=%fused_computation.189 | loop fusion | bytes 1028 | tf_op jit(solution)/shard_map/dynamic_slice | solution.py:235
  2.1 0.3 select_reduce_fusion.1
  2.3 0.1 copy.15
  2.4 0.7 %slice_bitcast_fusion.3 = (f32[16,16]{1,0:T(8,128)S(1)}, f32[16,16]{1,0:T(8,128)S(1)}) fusion(f32[2,16,16]{2,1,0:T(8,128)} %param.16), kind=kLoop, calls=%fused_computation.150 | loop fusion | bytes 4096 | tf_op jit(solution)/shard_map/mul | solution.py:239
  3.2 0.7 %convert_element_type.43 = f32[16,16]{1,0:T(8,128)S(1)} convert(s32[16,16]{1,0:T(8,128)} %param.11) | non-fusion elementwise | flops 256 | bytes 2048 | tf_op jit(solution)/shard_map/convert_element_type | solution.py:232
  3.9 0.1 copy.14
  4.0 1.1 %broadcast_multiply_fusion.1 = f32[16,16,288]{2,1,0:T(8,128)S(1)} fusion(f32[16,16,288]{2,1,0:T(8,128)} %param.10, f32[16,16]{1,0:T(8,128)S(1)} %convert_element_type.43), kind=kLoop, calls=%fused_computation.134 | loop fusion | flops 73728 | bytes 590848 | tf_op jit(solution)/shard_map/mul | solution.py:241
  5.1 0.2 multiply_multiply_fusion.2
  5.2 0.9 %pad_maximum_fusion.in_ref = f32[16,16,312]{2,1,0:T(8,128)} fusion(f32[16,16,8]{2,1,0:T(8,128)S(1)} %get-tuple-element.13, f32[16,16,8]{2,1,0:T(8,128)S(1)} %get-tuple-element.12, f32[16,16,8]{2,1,0:T(8,128)S(1)} %get-tuple-element.18, f32[16,16,288]{2,1,0:T(8,128)S(1)} %broadcast_multiply_fusion.1), kind=kLoop, calls=%fused_computation.131 | loop fusion | flops 239616 | bytes 638976 | tf_op jit(solution)/shard_map/concatenate | solution.py:243
  6.2 22.2 %shard_map.100 = f32[32,32,312]{2,1,0:T(8,128)} custom-call(f32[16,16,312]{2,1,0:T(8,128)} %pad_maximum_fusion.in_ref), custom_call_target="tpu_custom_call" | custom-call | tf_op jit(solution)/shard_map/pallas_call | solution.py:181
  28.4 2.0 %fusion.59 = f32[32,32,288]{2,1,0:T(8,128)S(1)} fusion(f32[32,32,312]{2,1,0:T(8,128)} %shard_map.100, s32[288]{0:T(512)S(1)} %add_select_fusion.2), kind=kOutput, calls=%fused_computation.89 | convolution fusion | flops 28313856 | bytes 1705088 | tf_op jit(solution)/shard_map/dot_general | solution.py:71
  30.4 0.9 %broadcast_multiply_fusion = (f32[32,32,288]{2,1,0:T(8,128)S(1)}, f32[32,32,288]{2,1,0:T(8,128)S(1)}) fusion(f32[288]{0:T(512)S(1)} %get-tuple-element.24, f32[32]{0:T(128)S(1)} %cosine_divide_fusion, f32[288]{0:T(512)S(1)} %fusion.116, s32[288]{0:T(512)S(1)} %add_select_fusion.2, f32[32,32,312]{2,1,0:T(8,128)S(1)} %copy-done), kind=kOutput, calls=%fused_computation.70 | convolution fusion | flops 29198592 | bytes 2890240 | tf_op jit(solution)/shard_map/dot_general | solution.py:71
  31.3 3.0 %subtract_subtract_fusion = f32[32,28,288]{2,1,0:T(8,128)S(1)} fusion(f32[32,32,312]{2,1,0:T(8,128)S(1)} %copy-done, f32[32,32,288]{2,1,0:T(8,128)S(1)} %get-tuple-element.11), kind=kLoop, calls=%fused_computation.4 | loop fusion | flops 11096064 | bytes 9289728 | tf_op jit(solution)/shard_map/sub | solution.py:45
  34.3 1.0 %multiply_subtract_fusion = f32[32,32,288]{2,1,0:T(8,128)S(1)} fusion(f32[32,32,288]{2,1,0:T(8,128)S(1)} %fusion.59, f32[288]{0:T(512)S(1)} %get-tuple-element.22, f32[288]{0:T(512)S(1)} %get-tuple-element.23, f32[32,32,312]{2,1,0:T(8,128)S(1)} %copy-done, s32[288]{0:T(512)S(1)} %add_select_fusion.2), kind=kOutput, calls=%fused_computation.3 | convolution fusion | flops 29198592 | bytes 3282944 | tf_op jit(solution)/shard_map/dot_general | solution.py:71
  35.3 0.9 %slice_select_fusion = f32[32,32,288]{2,1,0:T(8,128)S(1)} fusion(f32[32,32,288]{2,1,0:T(8,128)S(1)} %multiply_subtract_fusion, pred[288]{0:T(512)(128)(4,1)S(1)} %get-tuple-element.29), kind=kLoop, calls=%fused_computation.2 | loop fusion | flops 294912 | bytes 2359584 | tf_op jit(solution)/shard_map/jit(_where)/select_n | solution.py:59
  36.1 2.4 %fusion.6 = f32[28,28,288]{2,1,0:T(8,128)S(1)} fusion(f32[32,28,288]{2,1,0:T(8,128)S(1)} %subtract_subtract_fusion, f32[32,32,288]{2,1,0:T(8,128)S(1)} %get-tuple-element.10, pred[28]{0:T(512)(128)(4,1)S(1)} %slice.405), kind=kLoop, calls=%fused_computation.13 | loop fusion | flops 9934848 | bytes 8128540 | tf_op jit(solution)/shard_map/jit(_where)/select_n | solution.py:268
  38.6 3.0 %subtract_subtract_fusion.1 = f32[28,28,288]{2,1,0:T(8,128)S(1)} fusion(f32[28,28,288]{2,1,0:T(8,128)S(1)} %fusion.6, f32[32,32,288]{2,1,0:T(8,128)S(1)} %slice_select_fusion, f32[32,32,288]{2,1,0:T(8,128)S(1)} %multiply_subtract_fusion, pred[288]{0:T(512)(128)(4,1)S(1)} %get-tuple-element.27, pred[288]{0:T(512)(128)(4,1)S(1)} %get-tuple-element.28, ...), kind=kLoop, calls=%fused_computation.22 | loop fusion | flops 9709056 | bytes 3613824 | tf_op jit(solution)/shard_map/sub | solution.py:67
  41.6 1.9 %fusion.17 = f32[28,24,288]{2,1,0:T(8,128)S(1)} fusion(f32[28,28,288]{2,1,0:T(8,128)S(1)} %subtract_subtract_fusion.1, f32[32,32,288]{2,1,0:T(8,128)S(1)} %get-tuple-element.11), kind=kLoop, calls=%fused_computation.29 | loop fusion | flops 8322048 | bytes 6967296 | tf_op jit(solution)/shard_map/sub | solution.py:45
  43.5 1.0 %fusion.40 = f32[24,24,288]{2,1,0:T(8,128)S(1)} fusion(f32[28,24,288]{2,1,0:T(8,128)S(1)} %fusion.17, f32[32,32,288]{2,1,0:T(8,128)S(1)} %get-tuple-element.10, pred[24]{0:T(512)(128)(4,1)S(1)} %slice.404), kind=kLoop, calls=%fused_computation.60 | loop fusion | flops 7299072 | bytes 5971992 | tf_op jit(solution)/shard_map/jit(_where)/select_n | solution.py:268
  44.5 2.2 %subtract_subtract_fusion.2 = f32[24,24,288]{2,1,0:T(8,128)S(1)} fusion(f32[24,24,288]{2,1,0:T(8,128)S(1)} %fusion.40, f32[32,32,288]{2,1,0:T(8,128)S(1)} %slice_select_fusion, f32[32,32,288]{2,1,0:T(8,128)S(1)} %multiply_subtract_fusion, pred[288]{0:T(512)(128)(4,1)S(1)} %get-tuple-element.27, pred[288]{0:T(512)(128)(4,1)S(1)} %get-tuple-element.28, ...), kind=kLoop, calls=%fused_computation.69 | loop fusion | flops 7133184 | bytes 2655360 | tf_op jit(solution)/shard_map/sub | solution.py:67
  46.7 1.7 %fusion.28 = f32[24,20,288]{2,1,0:T(8,128)S(1)} fusion(f32[24,24,288]{2,1,0:T(8,128)S(1)} %subtract_subtract_fusion.2, f32[32,32,288]{2,1,0:T(8,128)S(1)} %get-tuple-element.11), kind=kLoop, calls=%fused_computation.44 | loop fusion | flops 5944320 | bytes 4976640 | tf_op jit(solution)/shard_map/sub | solution.py:45
  48.4 0.8 %fusion.52 = f32[20,20,288]{2,1,0:T(8,128)S(1)} fusion(f32[24,20,288]{2,1,0:T(8,128)S(1)} %fusion.28, f32[32,32,288]{2,1,0:T(8,128)S(1)} %get-tuple-element.10, pred[20]{0:T(512)(128)(4,1)S(1)} %slice.403), kind=kLoop, calls=%fused_computation.78 | loop fusion | flops 5068800 | bytes 4147220 | tf_op jit(solution)/shard_map/jit(_where)/select_n | solution.py:268
  49.2 1.6 %subtract_subtract_fusion.3 = f32[20,20,288]{2,1,0:T(8,128)S(1)} fusion(f32[20,20,288]{2,1,0:T(8,128)S(1)} %fusion.52, f32[32,32,288]{2,1,0:T(8,128)S(1)} %slice_select_fusion, f32[32,32,288]{2,1,0:T(8,128)S(1)} %multiply_subtract_fusion, pred[288]{0:T(512)(128)(4,1)S(1)} %get-tuple-element.27, pred[288]{0:T(512)(128)(4,1)S(1)} %get-tuple-element.28, ...), kind=kLoop, calls=%fused_computation.87 | loop fusion | flops 4953600 | bytes 1844352 | tf_op jit(solution)/shard_map/sub | solution.py:67
  50.8 0.9 %fusion.68 = f32[20,16,288]{2,1,0:T(8,128)S(1)} fusion(f32[20,20,288]{2,1,0:T(8,128)S(1)} %subtract_subtract_fusion.3, f32[32,32,288]{2,1,0:T(8,128)S(1)} %get-tuple-element.11), kind=kLoop, calls=%fused_computation.101 | loop fusion | flops 3962880 | bytes 3317760 | tf_op jit(solution)/shard_map/sub | solution.py:45
  51.7 0.4 fusion.84
  52.1 1.0 %multiply_reduce_fusion = (f32[16,16]{1,0:T(8,128)S(1)}, f32[16,16]{1,0:T(8,128)S(1)}, f32[16,16,288]{2,1,0:T(8,128)S(1)}) fusion(f32[288]{0:T(512)S(1)} %get-tuple-element.21, f32[16,16,288]{2,1,0:T(8,128)S(1)} %fusion.84, pred[288]{0:T(512)(128)(4,1)S(1)} %get-tuple-element.27, f32[32,32,288]{2,1,0:T(8,128)S(1)} %slice_select_fusion, ...), kind=kLoop, calls=%fused_computation.132 | loop fusion | flops 3390976 | bytes 1184000 | tf_op jit(solution)/shard_map/reduce_sum | solution.py:276
  53.1 0.8 %collective-permute-start = (f32[2,16,16]{2,1,0:T(8,128)S(1)}, f32[2,16,16]{2,1,0:T(8,128)S(1)}, u32[]{:S(2)}, u32[]{:S(2)}) collective-permute-start(f32[2,16,16]{2,1,0:T(8,128)S(1)} %pad_maximum_fusion.1), channel_id=1, source_target_pairs={{0,1},{1,0},{2,3},{3,2},{4,5},{5,4},{6,7},{7,6},{8,9},{9,8},{10,11... | collective-permute-start | bytes 6152 | tf_op jit(solution)/shard_map/ppermute | solution.py:277
  54.0 0.1 reshape.121
  54.1 0.1 dynamic_slice.11
  54.2 2.8 %collective-permute-done = f32[2,16,16]{2,1,0:T(8,128)S(1)} collective-permute-done((f32[2,16,16]{2,1,0:T(8,128)S(1)}, f32[2,16,16]{2,1,0:T(8,128)S(1)}, u32[]{:S(2)}, u32[]{:S(2)}) %collective-permute-start) | collective-permute-done | bytes 2080 | tf_op jit(solution)/shard_map/ppermute | solution.py:277
  57.0 2.3 %fusion.77 = f32[16,16,288]{2,1,0:T(8,128)} fusion(f32[16,16,288]{2,1,0:T(8,128)S(1)} %get-tuple-element.9, f32[288]{0:T(512)S(1)} %dynamic_slice.11, f32[16,16]{1,0:T(8,128)S(1)} %convert_element_type.47, f32[16,16]{1,0:T(8,128)S(1)} %get-tuple-element.15, f32[16,16]{1,0:T(8,128)S(1)} %get-tuple-element.14, f32[288]{0:T(512)S(1)} %get-tuple-element.19, ...), kind=kLoop, calls=%fused_computation.114 | loop fusion | flops 811008 | bytes 600576 | tf_op jit(solution)/shard_map/mul | solution.py:108
  (28 shorter events, 0.7 us)
Async XLA Ops:
  28.4 2.0 %copy-start = (f32[32,32,312]{2,1,0:T(8,128)S(1)}, f32[32,32,312]{2,1,0:T(8,128)}, u32[]{:S(2)}) copy-start(f32[32,32,312]{2,1,0:T(8,128)} %shard_map.100) | copy-start | bytes 3833860
  52.0 1.8 %copy-start.2 = (f32[16,16]{1,0:T(8,128)S(1)}, f32[16,16]{1,0:T(8,128)}, u32[]{:S(2)}) copy-start(f32[16,16]{1,0:T(8,128)} %param.17) | copy-start | bytes 3076
  52.0 1.9 %copy-start.4 = (f32[16]{0:T(128)S(1)}, f32[16]{0:T(128)}, u32[]{:S(2)}) copy-start(f32[16]{0:T(128)} %param.19) | copy-start | bytes 196
  52.1 2.0 %copy-start.3 = (s32[16,16]{1,0:T(8,128)S(1)}, s32[16,16]{1,0:T(8,128)}, u32[]{:S(2)}) copy-start(s32[16,16]{1,0:T(8,128)} %param.12) | copy-start | bytes 3076
  52.1 4.9 %copy-start.1 = (f32[16,16]{1,0:T(8,128)S(1)}, f32[16,16]{1,0:T(8,128)}, u32[]{:S(2)}) copy-start(f32[16,16]{1,0:T(8,128)} %param.18) | copy-start | bytes 3076
  53.1 3.8 %collective-permute-start = (f32[2,16,16]{2,1,0:T(8,128)S(1)}, f32[2,16,16]{2,1,0:T(8,128)S(1)}, u32[]{:S(2)}, u32[]{:S(2)}) collective-permute-start(f32[2,16,16]{2,1,0:T(8,128)S(1)} %pad_maximum_fusion.1), channel_id=1, source_target_pairs={{0,1},{1,0},{2,3},{3,2},{4,5},{5,4},{6,7},{7,6},{8,9},{9,8},{10,11... | collective-permute-start | bytes 6152 | tf_op jit(solution)/shard_map/ppermute | solution.py:277

commit v10 on v8

--- a/solution.py
+++ b/solution.py
@@ -35,19 +35,14 @@
 def advect(density, cell_speed, axis_dim):
     length = density.shape[axis_dim]
 
-    def piece(array, low, high):
-        return lax.slice_in_dim(array, low, high, axis=axis_dim)
-
-    courant = 0.5 * (piece(cell_speed, 1, length - 2) + piece(cell_speed, 2, length - 1))
-    fluxes = quickest(
-        piece(density, 0, length - 3),
-        piece(density, 1, length - 2),
-        piece(density, 2, length - 1),
-        piece(density, 3, length),
-        courant,
-    )
-    faces = fluxes.shape[axis_dim]
-    return piece(density, 2, length - 2) - (piece(fluxes, 1, faces) - piece(fluxes, 0, faces - 1))
+    def piece(array, low):
+        return lax.slice_in_dim(array, low, low + length - 4, axis=axis_dim)
+
+    def face(low):
+        courant = 0.5 * (piece(cell_speed, low + 1) + piece(cell_speed, low + 2))
+        return quickest(*[piece(density, low + i) for i in range(4)], courant)
+
+    return piece(density, 2) - (face(1) - face(0))
 
 
 def shifted(density, offset):

time: 55.9 us -> 59.1 us (1.057)
  other arithmetic: 23.2 us -> 26.5 us
    mul x12 -> x4, other arithmetic: 13 us -> 5.86 us  [quickest(): return courant * face_value]
    sub x4, other arithmetic: 0.93 us -> 7.39 us  [advect(): return piece(density, 2) - (face(1) - face(0))]
    select_n x4, other arithmetic: 0.6 us -> 4.54 us  [per_device(): density = jnp.where(inside, density, 0.0)]
where the time goes in v10:
time: 59.1 us; the launch traced here: 58.6 us
  other arithmetic  26.5 us (45%)
  Pallas kernels  22.2 us (38%)
  matrix products  3.9 us (7%)
  waiting for transfers between devices  2.76 us (5%)
  local copies, waits for them, and re-layouts  2.24 us (4%)
  starting transfers between devices  0.76 us (1%)
    pallas_call x1, Pallas kernels, halo_exchange(): pl.pallas_call(functools.partial(halo_kernel, halo=halo), out_shape=jax.S...  22.2 us
    sub x4, other arithmetic, advect(): return piece(density, 2) - (face(1) - face(0))  7.39 us
    mul x4, other arithmetic, quickest(): return courant * face_value  5.86 us
    select_n x4, other arithmetic, per_device(): density = jnp.where(inside, density, 0.0)  4.54 us
    dot_general x3, matrix products, expand(): return jnp.dot(per_freq, spread, precision=lax.Precision.HIGHEST)  3.9 us
    ppermute x1, waiting for transfers between devices, per_device(): other = lax.ppermute(partial, 'band', [(0, 1), (1, 0)])  2.76 us
    mul x1, other arithmetic, sources(): return sea_share[..., None] * density * jnp.exp(growth - breaking - damping)  2.34 us
    sub x3, other arithmetic, refract(): return density - (fluxes - rotate(fluxes, -1))  1.79 us
  transfers between devices with their start and end apart: 1, of which 1 were waited for; matrix products, arithmetic and copies ran while one was open for 0% of the time, Pallas kernels for 0%

profile of v10, /device:TPU:2, one launch (start us, length us, event | category | flops | bytes accessed | tf_op | source)
XLA Modules:
  0.0 58.6 jit_solution(17447040654383994159)
XLA Ops:
  0.6 0.7 %iota_compare_fusion = pred[16,16,8]{1,2,0:T(8,128)(4,1)S(1)} fusion(s32[16,16]{1,0:T(8,128)} %param.13), kind=kLoop, calls=%fused_computation.141 | loop fusion | flops 2048 | bytes 3072 | tf_op jit(solution)/shard_map/eq | solution.py:233
  1.3 0.8 %constant_dynamic-slice_fusion = (f32[8,8]{1,0:T(8,128)S(1)}, f32[8,8]{1,0:T(8,128)S(1)}) fusion(f32[8,16]{1,0:T(8,128)} %param.15, s32[]{:T(128)S(6)} %select_n.263, f32[8,16]{1,0:T(8,128)} %param.14), kind=kLoop, calls=%fused_computation.191 | loop fusion | bytes 1028 | tf_op jit(solution)/shard_map/dynamic_slice | solution.py:232
  2.1 0.3 select_reduce_fusion.1
  2.3 0.1 copy.15
  2.4 0.7 %slice_bitcast_fusion.3 = (f32[16,16]{1,0:T(8,128)S(1)}, f32[16,16]{1,0:T(8,128)S(1)}) fusion(f32[2,16,16]{2,1,0:T(8,128)} %param.16), kind=kLoop, calls=%fused_computation.153 | loop fusion | bytes 4096 | tf_op jit(solution)/shard_map/mul | solution.py:236
  3.2 0.7 %convert_element_type.43 = f32[16,16]{1,0:T(8,128)S(1)} convert(s32[16,16]{1,0:T(8,128)} %param.11) | non-fusion elementwise | flops 256 | bytes 2048 | tf_op jit(solution)/shard_map/convert_element_type | solution.py:229
  4.0 1.1 %broadcast_multiply_fusion.1 = f32[16,16,288]{2,1,0:T(8,128)S(1)} fusion(f32[16,16,288]{2,1,0:T(8,128)} %param.10, f32[16,16]{1,0:T(8,128)S(1)} %convert_element_type.43), kind=kLoop, calls=%fused_computation.137 | loop fusion | flops 73728 | bytes 590848 | tf_op jit(solution)/shard_map/mul | solution.py:238
  5.1 0.2 multiply_multiply_fusion.2
  5.2 0.9 %pad_maximum_fusion.in_ref = f32[16,16,312]{2,1,0:T(8,128)} fusion(f32[16,16,8]{2,1,0:T(8,128)S(1)} %get-tuple-element.13, f32[16,16,8]{2,1,0:T(8,128)S(1)} %get-tuple-element.12, f32[16,16,8]{2,1,0:T(8,128)S(1)} %get-tuple-element.18, f32[16,16,288]{2,1,0:T(8,128)S(1)} %broadcast_multiply_fusion.1), kind=kLoop, calls=%fused_computation.133 | loop fusion | flops 239616 | bytes 638976 | tf_op jit(solution)/shard_map/concatenate | solution.py:240
  6.2 22.2 %shard_map.100 = f32[32,32,312]{2,1,0:T(8,128)} custom-call(f32[16,16,312]{2,1,0:T(8,128)} %pad_maximum_fusion.in_ref), custom_call_target="tpu_custom_call" | custom-call | tf_op jit(solution)/shard_map/pallas_call | solution.py:178
  28.4 2.0 %fusion.59 = f32[32,32,288]{2,1,0:T(8,128)S(1)} fusion(f32[32,32,312]{2,1,0:T(8,128)} %shard_map.100, s32[288]{0:T(512)S(1)} %add_select_fusion.2), kind=kOutput, calls=%fused_computation.91 | convolution fusion | flops 28313856 | bytes 1705088 | tf_op jit(solution)/shard_map/dot_general | solution.py:68
  30.4 0.9 %broadcast_multiply_fusion = (f32[32,32,288]{2,1,0:T(8,128)S(1)}, f32[32,32,288]{2,1,0:T(8,128)S(1)}) fusion(f32[288]{0:T(512)S(1)} %get-tuple-element.24, f32[32]{0:T(128)S(1)} %cosine_divide_fusion, f32[288]{0:T(512)S(1)} %fusion.116, s32[288]{0:T(512)S(1)} %add_select_fusion.2, f32[32,32,312]{2,1,0:T(8,128)S(1)} %copy-done), kind=kOutput, calls=%fused_computation.71 | convolution fusion | flops 29198592 | bytes 2890240 | tf_op jit(solution)/shard_map/dot_general | solution.py:68
  31.3 3.0 %subtract_subtract_fusion = f32[32,28,288]{2,1,0:T(8,128)S(1)} fusion(f32[32,32,312]{2,1,0:T(8,128)S(1)} %copy-done, f32[32,32,288]{2,1,0:T(8,128)S(1)} %get-tuple-element.11), kind=kLoop, calls=%fused_computation.3 | loop fusion | flops 11096064 | bytes 9289728 | tf_op jit(solution)/shard_map/sub | solution.py:45
  34.3 2.4 %fusion.6 = f32[28,28,288]{2,1,0:T(8,128)S(1)} fusion(f32[32,28,288]{2,1,0:T(8,128)S(1)} %subtract_subtract_fusion, f32[32,32,288]{2,1,0:T(8,128)S(1)} %get-tuple-element.10, pred[28]{0:T(512)(128)(4,1)S(1)} %slice.380), kind=kLoop, calls=%fused_computation.12 | loop fusion | flops 9934848 | bytes 8128540 | tf_op jit(solution)/shard_map/jit(_where)/select_n | solution.py:262
  36.7 1.0 %multiply_subtract_fusion = f32[32,32,288]{2,1,0:T(8,128)S(1)} fusion(f32[32,32,288]{2,1,0:T(8,128)S(1)} %fusion.59, f32[288]{0:T(512)S(1)} %get-tuple-element.22, f32[288]{0:T(512)S(1)} %get-tuple-element.23, f32[32,32,312]{2,1,0:T(8,128)S(1)} %copy-done, s32[288]{0:T(512)S(1)} %add_select_fusion.2), kind=kOutput, calls=%fused_computation.2 | convolution fusion | flops 29198592 | bytes 3282944 | tf_op jit(solution)/shard_map/dot_general | solution.py:68
  37.7 2.5 %subtract_multiply_fusion = f32[28,28,288]{2,1,0:T(8,128)S(1)} fusion(f32[28,28,288]{2,1,0:T(8,128)S(1)} %fusion.6, f32[32,32,288]{2,1,0:T(8,128)S(1)} %multiply_subtract_fusion, pred[288]{0:T(512)(128)(4,1)S(1)} %get-tuple-element.27, pred[288]{0:T(512)(128)(4,1)S(1)} %get-tuple-element.28, pred[288]{0:T(512)(128)(4,1)S(1)} %add_compare_fusion.2), kind=kLoop, calls=%fused_computation.22 | loop fusion | flops 5193216 | bytes 2710368 | tf_op jit(solution)/shard_map/mul | solution.py:32
  40.2 0.8 %subtract_subtract_fusion.1 = f32[28,28,288]{2,1,0:T(8,128)S(1)} fusion(f32[28,28,288]{2,1,0:T(8,128)S(1)} %fusion.6, f32[28,28,288]{2,1,0:T(8,128)S(1)} %subtract_multiply_fusion, pred[288]{0:T(512)(128)(4,1)S(1)} %get-tuple-element.28), kind=kLoop, calls=%fused_computation.21 | loop fusion | flops 677376 | bytes 2709792 | tf_op jit(solution)/shard_map/sub | solution.py:64
  41.0 1.9 %fusion.17 = f32[28,24,288]{2,1,0:T(8,128)S(1)} fusion(f32[28,28,288]{2,1,0:T(8,128)S(1)} %subtract_subtract_fusion.1, f32[32,32,288]{2,1,0:T(8,128)S(1)} %get-tuple-element.11), kind=kLoop, calls=%fused_computation.29 | loop fusion | flops 8322048 | bytes 6967296 | tf_op jit(solution)/shard_map/sub | solution.py:45
  42.9 1.0 %fusion.40 = f32[24,24,288]{2,1,0:T(8,128)S(1)} fusion(f32[28,24,288]{2,1,0:T(8,128)S(1)} %fusion.17, f32[32,32,288]{2,1,0:T(8,128)S(1)} %get-tuple-element.10, pred[24]{0:T(512)(128)(4,1)S(1)} %slice.379), kind=kLoop, calls=%fused_computation.60 | loop fusion | flops 7299072 | bytes 5971992 | tf_op jit(solution)/shard_map/jit(_where)/select_n | solution.py:262
  43.9 1.4 %subtract_multiply_fusion.1 = f32[24,24,288]{2,1,0:T(8,128)S(1)} fusion(f32[24,24,288]{2,1,0:T(8,128)S(1)} %fusion.40, f32[32,32,288]{2,1,0:T(8,128)S(1)} %multiply_subtract_fusion, pred[288]{0:T(512)(128)(4,1)S(1)} %get-tuple-element.27, pred[288]{0:T(512)(128)(4,1)S(1)} %get-tuple-element.28, pred[288]{0:T(512)(128)(4,1)S(1)} %add_compare_fusion.2), kind=kLoop, calls=%fused_computation.70 | loop fusion | flops 3815424 | bytes 1991520 | tf_op jit(solution)/shard_map/mul | solution.py:32
  45.4 0.5 subtract_subtract_fusion.2
  45.9 1.7 %fusion.28 = f32[24,20,288]{2,1,0:T(8,128)S(1)} fusion(f32[24,24,288]{2,1,0:T(8,128)S(1)} %subtract_subtract_fusion.2, f32[32,32,288]{2,1,0:T(8,128)S(1)} %get-tuple-element.11), kind=kLoop, calls=%fused_computation.44 | loop fusion | flops 5944320 | bytes 4976640 | tf_op jit(solution)/shard_map/sub | solution.py:45
  47.6 0.8 %fusion.52 = f32[20,20,288]{2,1,0:T(8,128)S(1)} fusion(f32[24,20,288]{2,1,0:T(8,128)S(1)} %fusion.28, f32[32,32,288]{2,1,0:T(8,128)S(1)} %get-tuple-element.10, pred[20]{0:T(512)(128)(4,1)S(1)} %slice.378), kind=kLoop, calls=%fused_computation.79 | loop fusion | flops 5068800 | bytes 4147220 | tf_op jit(solution)/shard_map/jit(_where)/select_n | solution.py:262
  48.4 1.2 %subtract_multiply_fusion.2 = f32[20,20,288]{2,1,0:T(8,128)S(1)} fusion(f32[20,20,288]{2,1,0:T(8,128)S(1)} %fusion.52, f32[32,32,288]{2,1,0:T(8,128)S(1)} %multiply_subtract_fusion, pred[288]{0:T(512)(128)(4,1)S(1)} %get-tuple-element.27, pred[288]{0:T(512)(128)(4,1)S(1)} %get-tuple-element.28, pred[288]{0:T(512)(128)(4,1)S(1)} %add_compare_fusion.2), kind=kLoop, calls=%fused_computation.89 | loop fusion | flops 2649600 | bytes 1383264 | tf_op jit(solution)/shard_map/mul | solution.py:32
  49.6 0.5 subtract_subtract_fusion.3
  50.0 0.9 %fusion.68 = f32[20,16,288]{2,1,0:T(8,128)S(1)} fusion(f32[20,20,288]{2,1,0:T(8,128)S(1)} %subtract_subtract_fusion.3, f32[32,32,288]{2,1,0:T(8,128)S(1)} %get-tuple-element.11), kind=kLoop, calls=%fused_computation.103 | loop fusion | flops 3962880 | bytes 3317760 | tf_op jit(solution)/shard_map/sub | solution.py:45
  50.9 0.3 fusion.84
  51.3 0.7 %subtract_multiply_fusion.3 = f32[16,16,288]{2,1,0:T(8,128)S(1)} fusion(f32[16,16,288]{2,1,0:T(8,128)S(1)} %fusion.84, f32[32,32,288]{2,1,0:T(8,128)S(1)} %multiply_subtract_fusion, pred[288]{0:T(512)(128)(4,1)S(1)} %get-tuple-element.27, pred[288]{0:T(512)(128)(4,1)S(1)} %get-tuple-element.28, pred[288]{0:T(512)(128)(4,1)S(1)} %add_compare_fusion.2), kind=kLoop, calls=%fused_computation.136 | loop fusion | flops 1695744 | bytes 885600 | tf_op jit(solution)/shard_map/mul | solution.py:32
  52.0 0.4 multiply_reduce_fusion
  52.4 0.8 %collective-permute-start = (f32[2,16,16]{2,1,0:T(8,128)S(1)}, f32[2,16,16]{2,1,0:T(8,128)S(1)}, u32[]{:S(2)}, u32[]{:S(2)}) collective-permute-start(f32[2,16,16]{2,1,0:T(8,128)S(1)} %pad_maximum_fusion.1), channel_id=1, source_target_pairs={{0,1},{1,0},{2,3},{3,2},{4,5},{5,4},{6,7},{7,6},{8,9},{9,8},{10,11... | collective-permute-start | bytes 6152 | tf_op jit(solution)/shard_map/ppermute | solution.py:269
  53.5 2.8 %collective-permute-done = f32[2,16,16]{2,1,0:T(8,128)S(1)} collective-permute-done((f32[2,16,16]{2,1,0:T(8,128)S(1)}, f32[2,16,16]{2,1,0:T(8,128)S(1)}, u32[]{:S(2)}, u32[]{:S(2)}) %collective-permute-start) | collective-permute-done | bytes 2080 | tf_op jit(solution)/shard_map/ppermute | solution.py:269
  56.3 2.3 %fusion.77 = f32[16,16,288]{2,1,0:T(8,128)} fusion(f32[16,16,288]{2,1,0:T(8,128)S(1)} %get-tuple-element.9, f32[288]{0:T(512)S(1)} %dynamic_slice.11, f32[16,16]{1,0:T(8,128)S(1)} %convert_element_type.47, f32[16,16]{1,0:T(8,128)S(1)} %get-tuple-element.15, f32[16,16]{1,0:T(8,128)S(1)} %get-tuple-element.14, f32[288]{0:T(512)S(1)} %get-tuple-element.19, ...), kind=kLoop, calls=%fused_computation.116 | loop fusion | flops 811008 | bytes 600576 | tf_op jit(solution)/shard_map/mul | solution.py:105
  (31 shorter events, 1.0 us)
Async XLA Ops:
  28.4 2.0 %copy-start = (f32[32,32,312]{2,1,0:T(8,128)S(1)}, f32[32,32,312]{2,1,0:T(8,128)}, u32[]{:S(2)}) copy-start(f32[32,32,312]{2,1,0:T(8,128)} %shard_map.100) | copy-start | bytes 3833860
  51.3 1.9 %copy-start.2 = (f32[16,16]{1,0:T(8,128)S(1)}, f32[16,16]{1,0:T(8,128)}, u32[]{:S(2)}) copy-start(f32[16,16]{1,0:T(8,128)} %param.17) | copy-start | bytes 3076
  51.3 1.9 %copy-start.4 = (f32[16]{0:T(128)S(1)}, f32[16]{0:T(128)}, u32[]{:S(2)}) copy-start(f32[16]{0:T(128)} %param.19) | copy-start | bytes 196
  51.3 2.1 %copy-start.3 = (s32[16,16]{1,0:T(8,128)S(1)}, s32[16,16]{1,0:T(8,128)}, u32[]{:S(2)}) copy-start(s32[16,16]{1,0:T(8,128)} %param.12) | copy-start | bytes 3076
  51.3 4.9 %copy-start.1 = (f32[16,16]{1,0:T(8,128)S(1)}, f32[16,16]{1,0:T(8,128)}, u32[]{:S(2)}) copy-start(f32[16,16]{1,0:T(8,128)} %param.18) | copy-start | bytes 3076
  52.4 3.8 %collective-permute-start = (f32[2,16,16]{2,1,0:T(8,128)S(1)}, f32[2,16,16]{2,1,0:T(8,128)S(1)}, u32[]{:S(2)}, u32[]{:S(2)}) collective-permute-start(f32[2,16,16]{2,1,0:T(8,128)S(1)} %pad_maximum_fusion.1), channel_id=1, source_target_pairs={{0,1},{1,0},{2,3},{3,2},{4,5},{5,4},{6,7},{7,6},{8,9},{9,8},{10,11... | collective-permute-start | bytes 6152 | tf_op jit(solution)/shard_map/ppermute | solution.py:269

commit v11 on v8

--- a/solution.py
+++ b/solution.py
@@ -70,7 +70,10 @@
 
 
 def expand(per_freq, spread):
-    return jnp.dot(per_freq, spread, precision=lax.Precision.HIGHEST)
+    total = jnp.where(spread[0] > 0.5, per_freq[..., 0:1], 0.0)
+    for freq in range(1, spread.shape[0]):
+        total = total + jnp.where(spread[freq] > 0.5, per_freq[..., freq : freq + 1], 0.0)
+    return total
 
 
 def lookup(classes, lookup_table):

time: 55.9 us -> 69.7 us (1.25)
  local copies, waits for them, and re-layouts: 2.24 us -> 16.2 us
  matrix products: 3.88 us -> 0 us
  other arithmetic: 23.2 us -> 26.9 us
    slice x0 -> x2, local copies, waits for them, and re-layouts: none -> 14 us  [expand(): total = jnp.where(spread[0] > 0.5, per_freq[..., 0:1], 0.0)]
    dot_general x3 -> x0, matrix products: 3.88 us -> none  [expand(): return jnp.dot(per_freq, spread, precision=lax.Precision.HIGHEST)]
    sub x0 -> x1, other arithmetic: none -> 2.54 us  [per_device(): expand(fields[..., freqs_dev:2 * freqs_dev], spread) * sin_face]
    mul x0 -> x1, other arithmetic: none -> 1.23 us  [per_device(): along_y = gs_ext * sin_head]
where the time goes in v11:
time: 69.7 us; the launch traced here: 69.2 us
  other arithmetic  26.9 us (39%)
  Pallas kernels  22.2 us (32%)
  local copies, waits for them, and re-layouts  16.2 us (23%)
  waiting for transfers between devices  2.76 us (4%)
  starting transfers between devices  0.77 us (1%)
    pallas_call x1, Pallas kernels, halo_exchange(): pl.pallas_call(functools.partial(halo_kernel, halo=halo), out_shape=jax.S...  22.2 us
    slice x2, local copies, waits for them, and re-layouts, expand(): total = jnp.where(spread[0] > 0.5, per_freq[..., 0:1], 0.0)  14 us
    mul x12, other arithmetic, quickest(): return courant * face_value  12.9 us
    ppermute x1, waiting for transfers between devices, per_device(): other = lax.ppermute(partial, 'band', [(0, 1), (1, 0)])  2.76 us
    sub x1, other arithmetic, per_device(): expand(fields[..., freqs_dev:2 * freqs_dev], spread) * sin_face  2.54 us
    mul x1, other arithmetic, sources(): return sea_share[..., None] * density * jnp.exp(growth - breaking - damping)  2.33 us
    sub x3, other arithmetic, refract(): return density - (fluxes - rotate(fluxes, -1))  1.78 us
  transfers between devices with their start and end apart: 1, of which 1 were waited for; matrix products, arithmetic and copies ran while one was open for 0% of the time, Pallas kernels for 0%

profile of v11, /device:TPU:2, one launch (start us, length us, event | category | flops | bytes accessed | tf_op | source)
XLA Modules:
  0.0 69.2 jit_solution(2257168576466443339)
XLA Ops:
  0.1 0.7 %iota_compare_fusion = pred[16,16,8]{1,2,0:T(8,128)(4,1)S(1)} fusion(s32[16,16]{1,0:T(8,128)} %param.13), kind=kLoop, calls=%fused_computation.127 | loop fusion | flops 2048 | bytes 3072 | tf_op jit(solution)/shard_map/eq | solution.py:241
  0.8 0.8 %constant_dynamic-slice_fusion = (f32[8,8]{1,0:T(8,128)S(1)}, f32[8,8]{1,0:T(8,128)S(1)}) fusion(f32[8,16]{1,0:T(8,128)} %param.15, s32[]{:T(128)S(6)} %select_n.358, f32[8,16]{1,0:T(8,128)} %param.14), kind=kLoop, calls=%fused_computation.182 | loop fusion | bytes 1028 | tf_op jit(solution)/shard_map/dynamic_slice | solution.py:240
  2.0 0.7 %slice_bitcast_fusion.3 = (f32[16,16]{1,0:T(8,128)S(1)}, f32[16,16]{1,0:T(8,128)S(1)}) fusion(f32[2,16,16]{2,1,0:T(8,128)} %param.16), kind=kLoop, calls=%fused_computation.139 | loop fusion | bytes 4096 | tf_op jit(solution)/shard_map/mul | solution.py:244
  2.7 0.7 %convert_element_type.91 = f32[16,16]{1,0:T(8,128)S(1)} convert(s32[16,16]{1,0:T(8,128)} %param.11) | non-fusion elementwise | flops 256 | bytes 2048 | tf_op jit(solution)/shard_map/convert_element_type | solution.py:237
  3.5 1.1 %broadcast_multiply_fusion = f32[16,16,288]{2,1,0:T(8,128)S(1)} fusion(f32[16,16,288]{2,1,0:T(8,128)} %param.10, f32[16,16]{1,0:T(8,128)S(1)} %convert_element_type.91), kind=kLoop, calls=%fused_computation.123 | loop fusion | flops 73728 | bytes 590848 | tf_op jit(solution)/shard_map/mul | solution.py:246
  4.8 0.9 %pad_maximum_fusion.in_ref = f32[16,16,312]{2,1,0:T(8,128)} fusion(f32[16,16,8]{2,1,0:T(8,128)S(1)} %get-tuple-element.43, f32[16,16,8]{2,1,0:T(8,128)S(1)} %get-tuple-element.42, f32[16,16,8]{2,1,0:T(8,128)S(1)} %get-tuple-element.50, f32[16,16,288]{2,1,0:T(8,128)S(1)} %broadcast_multiply_fusion), kind=kLoop, calls=%fused_computation.119 | loop fusion | flops 239616 | bytes 638976 | tf_op jit(solution)/shard_map/concatenate | solution.py:248
  5.7 22.2 %shard_map.100 = f32[32,32,312]{2,1,0:T(8,128)} custom-call(f32[16,16,312]{2,1,0:T(8,128)} %pad_maximum_fusion.in_ref), custom_call_target="tpu_custom_call" | custom-call | tf_op jit(solution)/shard_map/pallas_call | solution.py:186
  27.9 12.5 %slice_reduce_fusion.15 = (f32[32,32]{1,0:T(8,128)S(1)}, f32[32,32]{1,0:T(8,128)S(1)}, f32[32,32]{1,0:T(8,128)S(1)}, f32[32,32]{1,0:T(8,128)S(1)}, f32[32,32]{1,...) fusion(f32[32,32,312]{2,1,0:T(8,128)} %shard_map.100), kind=kLoop, calls=%fused_computation.90 | loop fusion | bytes 155648 | tf_op jit(solution)/shard_map/slice | solution.py:73
  40.4 1.4 %slice_reduce_fusion.23 = (f32[32,32]{1,0:T(8,128)S(1)}, f32[32,32]{1,0:T(8,128)S(1)}, f32[32,32]{1,0:T(8,128)S(1)}, f32[32,32]{1,0:T(8,128)S(1)}, f32[32,32]{1,0:T(8,128)S(1)}) fusion(f32[32,32,312]{2,1,0:T(8,128)S(1)} %copy-done), kind=kLoop, calls=%fused_computation.98 | loop fusion | bytes 40960 | tf_op jit(solution)/shard_map/slice | solution.py:73
  42.4 1.2 %fusion.14 = (f32[32,32,288]{2,1,0:T(8,128)S(1)}, f32[32,32,288]{2,1,0:T(8,128)S(1)}) fusion(f32[288]{0:T(512)S(1)} %get-tuple-element.56, f32[32,32]{1,0:T(8,128)S(1)} %get-tuple-element.21, f32[32,32]{1,0:T(8,128)S(1)} %get-tuple-element.22, f32[32,32]{1,0:T(8,128)S(1)} %get-tuple-element.23, f32[32,32]{1,0:T(8,128)S(1)} %get-tuple-element.25, ...), kind=kLoop, calls=%fused_computation.30 | loop fusion | flops 5308416 | bytes 2396800 | tf_op jit(solution)/shard_map/mul | solution.py:260
  43.6 1.7 %subtract_multiply_fusion = f32[32,29,288]{2,1,0:T(8,128)S(1)} fusion(f32[32,32,312]{2,1,0:T(8,128)S(1)} %copy-done, f32[32,32,288]{2,1,0:T(8,128)S(1)} %get-tuple-element.45), kind=kLoop, calls=%fused_computation.4 | loop fusion | flops 5879808 | bytes 7483392 | tf_op jit(solution)/shard_map/mul | solution.py:32
  45.4 0.4 fusion
  45.8 1.0 %fusion.5 = f32[29,28,288]{2,1,0:T(8,128)S(1)} fusion(f32[32,28,288]{2,1,0:T(8,128)S(1)} %fusion, f32[32,32,288]{2,1,0:T(8,128)S(1)} %get-tuple-element.44), kind=kLoop, calls=%fused_computation.12 | loop fusion | flops 5144832 | bytes 6547968 | tf_op jit(solution)/shard_map/mul | solution.py:32
  47.0 2.5 %multiply_subtract_fusion = f32[32,32,288]{2,1,0:T(8,128)S(1)} fusion(f32[288]{0:T(512)S(1)} %get-tuple-element.54, f32[32,32]{1,0:T(8,128)S(1)} %get-tuple-element.18, f32[32,32]{1,0:T(8,128)S(1)} %get-tuple-element.19, f32[32,32]{1,0:T(8,128)S(1)} %get-tuple-element.20, f32[32,32]{1,0:T(8,128)S(1)} %get-tuple-element.6, f32[32,32]{1,0:T(8,128)S(1)} %get-tuple-element.7, ...), kind=kLoop, calls=%fused_computation.3 | loop fusion | flops 9732096 | bytes 1249792 | tf_op jit(solution)/shard_map/sub | solution.py:262
  49.5 2.3 %subtract_multiply_fusion.1 = f32[28,28,288]{2,1,0:T(8,128)S(1)} fusion(f32[28,28,288]{2,1,0:T(8,128)S(1)} %fusion.12, f32[32,32,288]{2,1,0:T(8,128)S(1)} %multiply_subtract_fusion, pred[288]{0:T(512)(128)(4,1)S(1)} %get-tuple-element.59, pred[288]{0:T(512)(128)(4,1)S(1)} %get-tuple-element.60, pred[288]{0:T(512)(128)(4,1)S(1)} %add_compare_fusion.2), kind=kLoop, calls=%fused_computation.27 | loop fusion | flops 5193216 | bytes 2710368 | tf_op jit(solution)/shard_map/mul | solution.py:32
  51.8 0.8 %subtract_subtract_fusion = f32[28,28,288]{2,1,0:T(8,128)S(1)} fusion(f32[28,28,288]{2,1,0:T(8,128)S(1)} %fusion.12, f32[28,28,288]{2,1,0:T(8,128)S(1)} %subtract_multiply_fusion.1, pred[288]{0:T(512)(128)(4,1)S(1)} %get-tuple-element.60), kind=kLoop, calls=%fused_computation.26 | loop fusion | flops 677376 | bytes 2709792 | tf_op jit(solution)/shard_map/sub | solution.py:69
  52.6 1.4 %fusion.10 = f32[28,25,288]{2,1,0:T(8,128)S(1)} fusion(f32[28,28,288]{2,1,0:T(8,128)S(1)} %subtract_subtract_fusion, f32[32,32,288]{2,1,0:T(8,128)S(1)} %get-tuple-element.45), kind=kLoop, calls=%fused_computation.20 | loop fusion | flops 4435200 | bytes 5644800 | tf_op jit(solution)/shard_map/mul | solution.py:32
  54.1 0.3 fusion.13
  54.3 0.6 fusion.19
  55.2 1.5 %subtract_multiply_fusion.2 = f32[24,24,288]{2,1,0:T(8,128)S(1)} fusion(f32[24,24,288]{2,1,0:T(8,128)S(1)} %fusion.27, f32[32,32,288]{2,1,0:T(8,128)S(1)} %multiply_subtract_fusion, pred[288]{0:T(512)(128)(4,1)S(1)} %get-tuple-element.59, pred[288]{0:T(512)(128)(4,1)S(1)} %get-tuple-element.60, pred[288]{0:T(512)(128)(4,1)S(1)} %add_compare_fusion.2), kind=kLoop, calls=%fused_computation.53 | loop fusion | flops 3815424 | bytes 1991520 | tf_op jit(solution)/shard_map/mul | solution.py:32
  56.6 0.5 subtract_subtract_fusion.1
  57.2 0.9 %fusion.25 = f32[24,21,288]{2,1,0:T(8,128)S(1)} fusion(f32[24,24,288]{2,1,0:T(8,128)S(1)} %subtract_subtract_fusion.1, f32[32,32,288]{2,1,0:T(8,128)S(1)} %get-tuple-element.45), kind=kLoop, calls=%fused_computation.46 | loop fusion | flops 3193344 | bytes 4064256 | tf_op jit(solution)/shard_map/mul | solution.py:32
  58.3 0.5 fusion.32
  59.0 1.2 %subtract_multiply_fusion.3 = f32[20,20,288]{2,1,0:T(8,128)S(1)} fusion(f32[20,20,288]{2,1,0:T(8,128)S(1)} %fusion.39, f32[32,32,288]{2,1,0:T(8,128)S(1)} %multiply_subtract_fusion, pred[288]{0:T(512)(128)(4,1)S(1)} %get-tuple-element.59, pred[288]{0:T(512)(128)(4,1)S(1)} %get-tuple-element.60, pred[288]{0:T(512)(128)(4,1)S(1)} %add_compare_fusion.2), kind=kLoop, calls=%fused_computation.74 | loop fusion | flops 2649600 | bytes 1383264 | tf_op jit(solution)/shard_map/mul | solution.py:32
  60.2 0.5 subtract_subtract_fusion.2
  60.6 0.7 %fusion.37 = f32[20,17,288]{2,1,0:T(8,128)S(1)} fusion(f32[20,20,288]{2,1,0:T(8,128)S(1)} %subtract_subtract_fusion.2, f32[32,32,288]{2,1,0:T(8,128)S(1)} %get-tuple-element.45), kind=kLoop, calls=%fused_computation.67 | loop fusion | flops 2154240 | bytes 2741760 | tf_op jit(solution)/shard_map/mul | solution.py:32
  61.5 0.3 fusion.45
  61.9 0.7 subtract_multiply_fusion.4
  62.6 0.4 multiply_reduce_fusion
  63.0 0.8 %collective-permute-start = (f32[2,16,16]{2,1,0:T(8,128)S(1)}, f32[2,16,16]{2,1,0:T(8,128)S(1)}, u32[]{:S(2)}, u32[]{:S(2)}) collective-permute-start(f32[2,16,16]{2,1,0:T(8,128)S(1)} %pad_maximum_fusion.1), channel_id=1, source_target_pairs={{0,1},{1,0},{2,3},{3,2},{4,5},{5,4},{6,7},{7,6},{8,9},{9,8},{10,11... | collective-permute-start | bytes 6152 | tf_op jit(solution)/shard_map/ppermute | solution.py:277
  64.1 2.8 %collective-permute-done = f32[2,16,16]{2,1,0:T(8,128)S(1)} collective-permute-done((f32[2,16,16]{2,1,0:T(8,128)S(1)}, f32[2,16,16]{2,1,0:T(8,128)S(1)}, u32[]{:S(2)}, u32[]{:S(2)}) %collective-permute-start) | collective-permute-done | bytes 2080 | tf_op jit(solution)/shard_map/ppermute | solution.py:277
  66.8 2.3 %fusion.49 = f32[16,16,288]{2,1,0:T(8,128)} fusion(f32[16,16,288]{2,1,0:T(8,128)S(1)} %get-tuple-element.41, f32[288]{0:T(512)S(1)} %dynamic_slice.11, f32[16,16]{1,0:T(8,128)S(1)} %convert_element_type.96, f32[16,16]{1,0:T(8,128)S(1)} %get-tuple-element.47, f32[16,16]{1,0:T(8,128)S(1)} %get-tuple-element.46, f32[288]{0:T(512)S(1)} %get-tuple-element.51, ...), kind=kLoop, calls=%fused_computation.115 | loop fusion | flops 811008 | bytes 600576 | tf_op jit(solution)/shard_map/mul | solution.py:113
  (42 shorter events, 2.4 us)
Async XLA Ops:
  27.9 12.5 %copy-start = (f32[32,32,312]{2,1,0:T(8,128)S(1)}, f32[32,32,312]{2,1,0:T(8,128)}, u32[]{:S(2)}) copy-start(f32[32,32,312]{2,1,0:T(8,128)} %shard_map.100) | copy-start | bytes 3833860
  61.9 1.9 %copy-start.2 = (f32[16,16]{1,0:T(8,128)S(1)}, f32[16,16]{1,0:T(8,128)}, u32[]{:S(2)}) copy-start(f32[16,16]{1,0:T(8,128)} %param.17) | copy-start | bytes 3076
  61.9 1.9 %copy-start.4 = (f32[16]{0:T(128)S(1)}, f32[16]{0:T(128)}, u32[]{:S(2)}) copy-start(f32[16]{0:T(128)} %param.19) | copy-start | bytes 196
  61.9 2.1 %copy-start.3 = (s32[16,16]{1,0:T(8,128)S(1)}, s32[16,16]{1,0:T(8,128)}, u32[]{:S(2)}) copy-start(s32[16,16]{1,0:T(8,128)} %param.12) | copy-start | bytes 3076
  61.9 4.9 %copy-start.1 = (f32[16,16]{1,0:T(8,128)S(1)}, f32[16,16]{1,0:T(8,128)}, u32[]{:S(2)}) copy-start(f32[16,16]{1,0:T(8,128)} %param.18) | copy-start | bytes 3076
  63.0 3.8 %collective-permute-start = (f32[2,16,16]{2,1,0:T(8,128)S(1)}, f32[2,16,16]{2,1,0:T(8,128)S(1)}, u32[]{:S(2)}, u32[]{:S(2)}) collective-permute-start(f32[2,16,16]{2,1,0:T(8,128)S(1)} %pad_maximum_fusion.1), channel_id=1, source_target_pairs={{0,1},{1,0},{2,3},{3,2},{4,5},{5,4},{6,7},{7,6},{8,9},{9,8},{10,11... | collective-permute-start | bytes 6152 | tf_op jit(solution)/shard_map/ppermute | solution.py:277

commit v12 on v8

--- a/solution.py
+++ b/solution.py
@@ -100,12 +100,11 @@
     mean_level = jnp.maximum(moment, 1.0) / jnp.maximum(energy_sum, 1.0)
     energy = energy_sum / NCOMP
     breaking = break_coef * levels * levels / mean_level[..., None] * (energy * energy)[..., None]
-    growth = (
-        wind_gain
-        * wind_speed[..., None]
-        * levels
-        * jnp.maximum(jnp.cos(heading - wind_dir[..., None]), 0.0)
-    )
+    alignment = (
+        jnp.cos(heading) * jnp.cos(wind_dir)[..., None]
+        + jnp.sin(heading) * jnp.sin(wind_dir)[..., None]
+    )
+    growth = wind_gain * wind_speed[..., None] * levels * jnp.maximum(alignment, 0.0)
     damping = ice_share[..., None] * ice_loss
     return sea_share[..., None] * density * jnp.exp(growth - breaking - damping)
 

time: 55.9 us -> 54.6 us (0.977)
  other arithmetic: 23.2 us -> 22 us
    mul x1, other arithmetic: 2.34 us -> 1.07 us  [sources(): return sea_share[..., None] * density * jnp.exp(growth - breaking - damping)]
  transfers between devices with their start and end apart: 1 -> 1, of which waited for: 1 -> 1; matrix products, arithmetic and copies ran while one was open for 0% -> 1% of each run, Pallas kernels for 0% -> 0%
where the time goes in v12:
time: 54.6 us; the launch traced here: 54.1 us
  Pallas kernels  22.2 us (41%)
  other arithmetic  22 us (40%)
  matrix products  3.87 us (7%)
  waiting for transfers between devices  2.7 us (5%)
  local copies, waits for them, and re-layouts  2.24 us (4%)
  starting transfers between devices  0.77 us (1%)
    pallas_call x1, Pallas kernels, halo_exchange(): pl.pallas_call(functools.partial(halo_kernel, halo=halo), out_shape=jax.S...  22.2 us
    mul x12, other arithmetic, quickest(): return courant * face_value  13 us
    dot_general x3, matrix products, expand(): return jnp.dot(per_freq, spread, precision=lax.Precision.HIGHEST)  3.87 us
    ppermute x1, waiting for transfers between devices, per_device(): other = lax.ppermute(partial, 'band', [(0, 1), (1, 0)])  2.7 us
    sub x3, other arithmetic, refract(): return density - (fluxes - rotate(fluxes, -1))  1.81 us
    mul x1, other arithmetic, per_device(): density = spectrum * sea_share[..., None]  1.09 us
  transfers between devices with their start and end apart: 1, of which 1 were waited for; matrix products, arithmetic and copies ran while one was open for 1% of the time, Pallas kernels for 0%

profile of v12, /device:TPU:2, one launch (start us, length us, event | category | flops | bytes accessed | tf_op | source)
XLA Modules:
  0.0 54.1 jit_solution(5687434906973957159)
XLA Ops:
  0.6 0.7 %iota_compare_fusion = pred[16,16,8]{1,2,0:T(8,128)(4,1)S(1)} fusion(s32[16,16]{1,0:T(8,128)} %param.13), kind=kLoop, calls=%fused_computation.107 | loop fusion | flops 2048 | bytes 3072 | tf_op jit(solution)/shard_map/eq | solution.py:237
  1.3 0.8 %constant_dynamic-slice_fusion = (f32[8,8]{1,0:T(8,128)S(1)}, f32[8,8]{1,0:T(8,128)S(1)}) fusion(f32[8,16]{1,0:T(8,128)} %param.15, s32[]{:T(128)S(6)} %select_n.240, f32[8,16]{1,0:T(8,128)} %param.14), kind=kLoop, calls=%fused_computation.157 | loop fusion | bytes 1028 | tf_op jit(solution)/shard_map/dynamic_slice | solution.py:236
  2.1 0.3 select_reduce_fusion.1
  2.5 0.7 %convert_element_type.40 = f32[16,16]{1,0:T(8,128)S(1)} convert(s32[16,16]{1,0:T(8,128)} %param.11) | non-fusion elementwise | flops 256 | bytes 2048 | tf_op jit(solution)/shard_map/convert_element_type | solution.py:233
  3.2 0.7 %slice_bitcast_fusion.3 = (f32[16,16]{1,0:T(8,128)S(1)}, f32[16,16]{1,0:T(8,128)S(1)}) fusion(f32[2,16,16]{2,1,0:T(8,128)} %param.16), kind=kLoop, calls=%fused_computation.119 | loop fusion | bytes 4096 | tf_op jit(solution)/shard_map/mul | solution.py:240
  4.0 1.1 %broadcast_multiply_fusion.1 = f32[16,16,288]{2,1,0:T(8,128)S(1)} fusion(f32[16,16,288]{2,1,0:T(8,128)} %param.10, f32[16,16]{1,0:T(8,128)S(1)} %convert_element_type.40), kind=kLoop, calls=%fused_computation.103 | loop fusion | flops 73728 | bytes 590848 | tf_op jit(solution)/shard_map/mul | solution.py:242
  5.2 0.9 %pad_maximum_fusion.in_ref = f32[16,16,312]{2,1,0:T(8,128)} fusion(f32[16,16,8]{2,1,0:T(8,128)S(1)} %get-tuple-element.13, f32[16,16,8]{2,1,0:T(8,128)S(1)} %get-tuple-element.12, f32[16,16,8]{2,1,0:T(8,128)S(1)} %get-tuple-element.20, f32[16,16,288]{2,1,0:T(8,128)S(1)} %broadcast_multiply_fusion.1), kind=kLoop, calls=%fused_computation.99 | loop fusion | flops 239616 | bytes 638976 | tf_op jit(solution)/shard_map/concatenate | solution.py:244
  6.2 22.2 %shard_map.100 = f32[32,32,312]{2,1,0:T(8,128)} custom-call(f32[16,16,312]{2,1,0:T(8,128)} %pad_maximum_fusion.in_ref), custom_call_target="tpu_custom_call" | custom-call | tf_op jit(solution)/shard_map/pallas_call | solution.py:182
  28.4 2.0 %fusion.40 = f32[32,32,288]{2,1,0:T(8,128)S(1)} fusion(f32[32,32,312]{2,1,0:T(8,128)} %shard_map.100, s32[288]{0:T(512)S(1)} %add_select_fusion.2), kind=kOutput, calls=%fused_computation.75 | convolution fusion | flops 28313856 | bytes 1705088 | tf_op jit(solution)/shard_map/dot_general | solution.py:73
  30.4 0.9 %broadcast_multiply_fusion = (f32[32,32,288]{2,1,0:T(8,128)S(1)}, f32[32,32,288]{2,1,0:T(8,128)S(1)}) fusion(f32[288]{0:T(512)S(1)} %get-tuple-element.24, f32[32]{0:T(128)S(1)} %cosine_divide_fusion, f32[288]{0:T(512)S(1)} %fusion.82, s32[288]{0:T(512)S(1)} %add_select_fusion.2, f32[32,32,312]{2,1,0:T(8,128)S(1)} %copy-done), kind=kOutput, calls=%fused_computation.52 | convolution fusion | flops 29198592 | bytes 2890240 | tf_op jit(solution)/shard_map/dot_general | solution.py:73
  31.3 1.6 %subtract_multiply_fusion = f32[32,29,288]{2,1,0:T(8,128)S(1)} fusion(f32[32,32,312]{2,1,0:T(8,128)S(1)} %copy-done, f32[32,32,288]{2,1,0:T(8,128)S(1)} %get-tuple-element.11), kind=kLoop, calls=%fused_computation.4 | loop fusion | flops 5879808 | bytes 7483392 | tf_op jit(solution)/shard_map/mul | solution.py:32
  32.9 0.4 fusion
  33.3 1.0 %fusion.5 = f32[29,28,288]{2,1,0:T(8,128)S(1)} fusion(f32[32,28,288]{2,1,0:T(8,128)S(1)} %fusion, f32[32,32,288]{2,1,0:T(8,128)S(1)} %get-tuple-element.10), kind=kLoop, calls=%fused_computation.11 | loop fusion | flops 5144832 | bytes 6547968 | tf_op jit(solution)/shard_map/mul | solution.py:32
  34.5 1.0 %multiply_subtract_fusion = f32[32,32,288]{2,1,0:T(8,128)S(1)} fusion(f32[32,32,288]{2,1,0:T(8,128)S(1)} %fusion.40, f32[288]{0:T(512)S(1)} %get-tuple-element.22, f32[288]{0:T(512)S(1)} %get-tuple-element.23, f32[32,32,312]{2,1,0:T(8,128)S(1)} %copy-done, s32[288]{0:T(512)S(1)} %add_select_fusion.2), kind=kOutput, calls=%fused_computation.3 | convolution fusion | flops 29198592 | bytes 3282944 | tf_op jit(solution)/shard_map/dot_general | solution.py:73
  35.5 2.5 %subtract_multiply_fusion.1 = f32[28,28,288]{2,1,0:T(8,128)S(1)} fusion(f32[28,28,288]{2,1,0:T(8,128)S(1)} %fusion.12, f32[32,32,288]{2,1,0:T(8,128)S(1)} %multiply_subtract_fusion, pred[288]{0:T(512)(128)(4,1)S(1)} %get-tuple-element.27, pred[288]{0:T(512)(128)(4,1)S(1)} %get-tuple-element.28, pred[288]{0:T(512)(128)(4,1)S(1)} %add_compare_fusion.2), kind=kLoop, calls=%fused_computation.26 | loop fusion | flops 5193216 | bytes 2710368 | tf_op jit(solution)/shard_map/mul | solution.py:32
  38.0 0.8 %subtract_subtract_fusion = f32[28,28,288]{2,1,0:T(8,128)S(1)} fusion(f32[28,28,288]{2,1,0:T(8,128)S(1)} %fusion.12, f32[28,28,288]{2,1,0:T(8,128)S(1)} %subtract_multiply_fusion.1, pred[288]{0:T(512)(128)(4,1)S(1)} %get-tuple-element.28), kind=kLoop, calls=%fused_computation.25 | loop fusion | flops 677376 | bytes 2709792 | tf_op jit(solution)/shard_map/sub | solution.py:69
  38.8 1.4 %fusion.10 = f32[28,25,288]{2,1,0:T(8,128)S(1)} fusion(f32[28,28,288]{2,1,0:T(8,128)S(1)} %subtract_subtract_fusion, f32[32,32,288]{2,1,0:T(8,128)S(1)} %get-tuple-element.11), kind=kLoop, calls=%fused_computation.19 | loop fusion | flops 4435200 | bytes 5644800 | tf_op jit(solution)/shard_map/mul | solution.py:32
  40.3 0.3 fusion.13
  40.5 0.6 %fusion.18 = f32[25,24,288]{2,1,0:T(8,128)S(1)} fusion(f32[28,24,288]{2,1,0:T(8,128)S(1)} %fusion.13, f32[32,32,288]{2,1,0:T(8,128)S(1)} %get-tuple-element.10), kind=kLoop, calls=%fused_computation.34 | loop fusion | flops 3801600 | bytes 4838400 | tf_op jit(solution)/shard_map/mul | solution.py:32
  41.4 1.5 %subtract_multiply_fusion.2 = f32[24,24,288]{2,1,0:T(8,128)S(1)} fusion(f32[24,24,288]{2,1,0:T(8,128)S(1)} %fusion.26, f32[32,32,288]{2,1,0:T(8,128)S(1)} %multiply_subtract_fusion, pred[288]{0:T(512)(128)(4,1)S(1)} %get-tuple-element.27, pred[288]{0:T(512)(128)(4,1)S(1)} %get-tuple-element.28, pred[288]{0:T(512)(128)(4,1)S(1)} %add_compare_fusion.2), kind=kLoop, calls=%fused_computation.51 | loop fusion | flops 3815424 | bytes 1991520 | tf_op jit(solution)/shard_map/mul | solution.py:32
  42.8 0.5 subtract_subtract_fusion.1
  43.3 0.9 %fusion.24 = f32[24,21,288]{2,1,0:T(8,128)S(1)} fusion(f32[24,24,288]{2,1,0:T(8,128)S(1)} %subtract_subtract_fusion.1, f32[32,32,288]{2,1,0:T(8,128)S(1)} %get-tuple-element.11), kind=kLoop, calls=%fused_computation.44 | loop fusion | flops 3193344 | bytes 4064256 | tf_op jit(solution)/shard_map/mul | solution.py:32
  44.5 0.5 %fusion.31 = f32[21,20,288]{2,1,0:T(8,128)S(1)} fusion(f32[24,20,288]{2,1,0:T(8,128)S(1)} %fusion.19, f32[32,32,288]{2,1,0:T(8,128)S(1)} %get-tuple-element.10), kind=kLoop, calls=%fused_computation.58 | loop fusion | flops 2661120 | bytes 3386880 | tf_op jit(solution)/shard_map/mul | solution.py:32
  45.1 1.2 %subtract_multiply_fusion.3 = f32[20,20,288]{2,1,0:T(8,128)S(1)} fusion(f32[20,20,288]{2,1,0:T(8,128)S(1)} %fusion.38, f32[32,32,288]{2,1,0:T(8,128)S(1)} %multiply_subtract_fusion, pred[288]{0:T(512)(128)(4,1)S(1)} %get-tuple-element.27, pred[288]{0:T(512)(128)(4,1)S(1)} %get-tuple-element.28, pred[288]{0:T(512)(128)(4,1)S(1)} %add_compare_fusion.2), kind=kLoop, calls=%fused_computation.73 | loop fusion | flops 2649600 | bytes 1383264 | tf_op jit(solution)/shard_map/mul | solution.py:32
  46.4 0.5 subtract_subtract_fusion.2
  46.8 0.7 %fusion.36 = f32[20,17,288]{2,1,0:T(8,128)S(1)} fusion(f32[20,20,288]{2,1,0:T(8,128)S(1)} %subtract_subtract_fusion.2, f32[32,32,288]{2,1,0:T(8,128)S(1)} %get-tuple-element.11), kind=kLoop, calls=%fused_computation.66 | loop fusion | flops 2154240 | bytes 2741760 | tf_op jit(solution)/shard_map/mul | solution.py:32
  47.7 0.3 fusion.49
  48.1 0.7 %subtract_multiply_fusion.4 = f32[16,16,288]{2,1,0:T(8,128)S(1)} fusion(f32[16,16,288]{2,1,0:T(8,128)S(1)} %fusion.55, f32[32,32,288]{2,1,0:T(8,128)S(1)} %multiply_subtract_fusion, pred[288]{0:T(512)(128)(4,1)S(1)} %get-tuple-element.27, pred[288]{0:T(512)(128)(4,1)S(1)} %get-tuple-element.28, pred[288]{0:T(512)(128)(4,1)S(1)} %add_compare_fusion.2), kind=kLoop, calls=%fused_computation.102 | loop fusion | flops 1695744 | bytes 885600 | tf_op jit(solution)/shard_map/mul | solution.py:32
  48.8 0.4 multiply_reduce_fusion
  49.2 0.8 %collective-permute-start = (f32[2,16,16]{2,1,0:T(8,128)S(1)}, f32[2,16,16]{2,1,0:T(8,128)S(1)}, u32[]{:S(2)}, u32[]{:S(2)}) collective-permute-start(f32[2,16,16]{2,1,0:T(8,128)S(1)} %pad_maximum_fusion.1), channel_id=1, source_target_pairs={{0,1},{1,0},{2,3},{3,2},{4,5},{5,4},{6,7},{7,6},{8,9},{9,8},{10,11... | collective-permute-start | bytes 6152 | tf_op jit(solution)/shard_map/ppermute | solution.py:273
  50.3 2.7 %collective-permute-done = f32[2,16,16]{2,1,0:T(8,128)S(1)} collective-permute-done((f32[2,16,16]{2,1,0:T(8,128)S(1)}, f32[2,16,16]{2,1,0:T(8,128)S(1)}, u32[]{:S(2)}, u32[]{:S(2)}) %collective-permute-start) | collective-permute-done | bytes 2080 | tf_op jit(solution)/shard_map/ppermute | solution.py:273
  53.0 1.1 %fusion.53 = f32[16,16,288]{2,1,0:T(8,128)} fusion(f32[16,16,288]{2,1,0:T(8,128)S(1)} %get-tuple-element.9, f32[288]{0:T(512)S(1)} %dynamic_slice.11, f32[16,16]{1,0:T(8,128)S(1)} %convert_element_type.44, f32[16,16]{1,0:T(8,128)S(1)} %get-tuple-element.15, f32[16,16]{1,0:T(8,128)S(1)} %get-tuple-element.14, f32[288]{0:T(512)S(1)} %multiply_multiply_fusion.4, ...), kind=kLoop, calls=%fused_computation.95 | loop fusion | flops 958464 | bytes 602752 | tf_op jit(solution)/shard_map/mul | solution.py:109
  (39 shorter events, 2.1 us)
Async XLA Ops:
  28.4 2.0 %copy-start = (f32[32,32,312]{2,1,0:T(8,128)S(1)}, f32[32,32,312]{2,1,0:T(8,128)}, u32[]{:S(2)}) copy-start(f32[32,32,312]{2,1,0:T(8,128)} %shard_map.100) | copy-start | bytes 3833860
  48.1 1.9 %copy-start.1 = (f32[16,16]{1,0:T(8,128)S(1)}, f32[16,16]{1,0:T(8,128)}, u32[]{:S(2)}) copy-start(f32[16,16]{1,0:T(8,128)} %param.18) | copy-start | bytes 3076
  48.1 1.9 %copy-start.2 = (f32[16,16]{1,0:T(8,128)S(1)}, f32[16,16]{1,0:T(8,128)}, u32[]{:S(2)}) copy-start(f32[16,16]{1,0:T(8,128)} %param.17) | copy-start | bytes 3076
  48.1 2.0 %copy-start.4 = (f32[16]{0:T(128)S(1)}, f32[16]{0:T(128)}, u32[]{:S(2)}) copy-start(f32[16]{0:T(128)} %param.19) | copy-start | bytes 196
  48.1 2.1 %copy-start.3 = (s32[16,16]{1,0:T(8,128)S(1)}, s32[16,16]{1,0:T(8,128)}, u32[]{:S(2)}) copy-start(s32[16,16]{1,0:T(8,128)} %param.12) | copy-start | bytes 3076
  49.2 3.8 %collective-permute-start = (f32[2,16,16]{2,1,0:T(8,128)S(1)}, f32[2,16,16]{2,1,0:T(8,128)S(1)}, u32[]{:S(2)}, u32[]{:S(2)}) collective-permute-start(f32[2,16,16]{2,1,0:T(8,128)S(1)} %pad_maximum_fusion.1), channel_id=1, source_target_pairs={{0,1},{1,0},{2,3},{3,2},{4,5},{5,4},{6,7},{7,6},{8,9},{9,8},{10,11... | collective-permute-start | bytes 6152 | tf_op jit(solution)/shard_map/ppermute | solution.py:273

commit v13 on v12

--- a/solution.py
+++ b/solution.py
@@ -239,12 +239,11 @@
     turning = jnp.sum(jnp.where(chosen, refr_local, 0.0), axis=2) * sea_share[..., None]
     turn_x = turning * depth_slope[0][..., None]
     turn_y = turning * depth_slope[1][..., None]
-    density = spectrum * sea_share[..., None]
-
-    stacked = jnp.concatenate([density, group_speed, turn_x, turn_y], axis=-1)
+
+    stacked = jnp.concatenate([spectrum, group_speed, turn_x, turn_y, sea_share[..., None]], axis=-1)
     stacked = halo_exchange(stacked, halo)
-    density = stacked[..., :comps_dev]
-    fields = stacked[..., comps_dev:]
+    density = stacked[..., :comps_dev] * stacked[..., -1:]
+    fields = stacked[..., comps_dev:-1]
 
     total_rows = rows_dev * lax.axis_size("lat")
     first_row = lax.axis_index("lat") * rows_dev - halo

time: 54.6 us -> 55.8 us (1.022)
  local copies, waits for them, and re-layouts: 2.24 us -> 4.91 us
  matrix products: 3.87 us -> 2.72 us
    slice x0 -> x1, local copies, waits for them, and re-layouts: none -> 1.42 us  [per_device(): density = stacked[..., :comps_dev] * stacked[..., -1:]]
    dot_general x3, matrix products: 3.87 us -> 2.72 us  [expand(): return jnp.dot(per_freq, spread, precision=lax.Precision.HIGHEST)]
    concatenate x0 -> x1, local copies, waits for them, and re-layouts: none -> 0.95 us  [per_device(): jnp.concatenate([spectrum, group_speed, turn_x, turn_y, sea_share[..., No...]
    concatenate x1 -> x0, other arithmetic: 0.92 us -> none  [per_device(): stacked = jnp.concatenate([density, group_speed, turn_x, turn_y], axis=-1)]
    broadcast_in_dim x0 -> x1, other arithmetic: none -> 0.71 us  [sources(): return sea_share[..., None] * density * jnp.exp(growth - breaking - damping)]
    convert_element_type x1 -> x0, other arithmetic: 0.71 us -> none  [per_device(): sea_share = sea_mask.astype(jnp.float32)]
    mul x2, other arithmetic: 1.26 us -> 1.89 us  [the longest x1 1.73 us: per_device(): density = stacked[..., :comps_dev] * stacked[..., -1:]]
where the time goes in v13:
time: 55.8 us; the launch traced here: 55.3 us
  Pallas kernels  22.2 us (40%)
  other arithmetic  21.7 us (39%)
  local copies, waits for them, and re-layouts  4.91 us (9%)
  matrix products  2.72 us (5%)
  waiting for transfers between devices  2.71 us (5%)
  starting transfers between devices  0.76 us (1%)
    pallas_call x1, Pallas kernels, halo_exchange(): pl.pallas_call(functools.partial(halo_kernel, halo=halo), out_shape=jax.S...  22.2 us
    mul x12, other arithmetic, quickest(): return courant * face_value  13 us
    dot_general x3, matrix products, expand(): return jnp.dot(per_freq, spread, precision=lax.Precision.HIGHEST)  2.72 us
    ppermute x1, waiting for transfers between devices, per_device(): other = lax.ppermute(partial, 'band', [(0, 1), (1, 0)])  2.71 us
    sub x3, other arithmetic, refract(): return density - (fluxes - rotate(fluxes, -1))  1.78 us
    mul x1, other arithmetic, per_device(): density = stacked[..., :comps_dev] * stacked[..., -1:]  1.73 us
    slice x1, local copies, waits for them, and re-layouts, per_device(): density = stacked[..., :comps_dev] * stacked[..., -1:]  1.42 us
  transfers between devices with their start and end apart: 1, of which 1 were waited for; matrix products, arithmetic and copies ran while one was open for 1% of the time, Pallas kernels for 0%

profile of v13, /device:TPU:2, one launch (start us, length us, event | category | flops | bytes accessed | tf_op | source)
XLA Modules:
  0.0 55.3 jit_solution(15250219033715984746)
XLA Ops:
  0.6 0.7 %iota_compare_fusion = pred[16,16,8]{1,2,0:T(8,128)(4,1)S(1)} fusion(s32[16,16]{1,0:T(8,128)} %param.13), kind=kLoop, calls=%fused_computation.113 | loop fusion | flops 2048 | bytes 3072 | tf_op jit(solution)/shard_map/eq | solution.py:237
  1.3 0.8 %constant_dynamic-slice_fusion = (f32[8,8]{1,0:T(8,128)S(1)}, f32[8,8]{1,0:T(8,128)S(1)}) fusion(f32[8,16]{1,0:T(8,128)} %param.15, s32[]{:T(128)S(6)} %select_n.240, f32[8,16]{1,0:T(8,128)} %param.14), kind=kLoop, calls=%fused_computation.163 | loop fusion | bytes 1028 | tf_op jit(solution)/shard_map/dynamic_slice | solution.py:236
  2.5 0.7 %convert_bitcast_fusion = (f32[16,16,1]{1,0,2:T(8,128)S(1)}, f32[16,16]{1,0:T(8,128)S(1)}) fusion(s32[16,16]{1,0:T(8,128)} %param.11), kind=kLoop, calls=%fused_computation.166 | loop fusion | flops 256 | bytes 3072 | tf_op jit(solution)/shard_map/broadcast_in_dim | solution.py:109
  3.3 0.7 %slice_bitcast_fusion.2 = (f32[16,16]{1,0:T(8,128)S(1)}, f32[16,16]{1,0:T(8,128)S(1)}) fusion(f32[2,16,16]{2,1,0:T(8,128)} %param.16), kind=kLoop, calls=%fused_computation.124 | loop fusion | bytes 4096 | tf_op jit(solution)/shard_map/mul | solution.py:241
  4.3 0.9 %concatenate.3.in_ref = f32[16,16,313]{2,1,0:T(8,128)} concatenate(f32[16,16,288]{2,1,0:T(8,128)S(1)} %copy-done.1, f32[16,16,8]{2,1,0:T(8,128)S(1)} %get-tuple-element.22, f32[16,16,8]{2,1,0:T(8,128)S(1)} %get-tuple-element.13, f32[16,16,8]{2,1,0:T(8,128)S(1)} %get-tuple-element.12, f32[16,16,1]{2,1,0:T(8,128)S(1)} %copy.20), dimensions={2} | concatenate | bytes 641024 | tf_op jit(solution)/shard_map/concatenate | solution.py:243
  5.3 22.2 %shard_map.100 = f32[32,32,313]{2,1,0:T(8,128)} custom-call(f32[16,16,313]{2,1,0:T(8,128)} %concatenate.3.in_ref), custom_call_target="tpu_custom_call" | custom-call | tf_op jit(solution)/shard_map/pallas_call | solution.py:182
  27.5 1.4 %slice_reduce_fusion = f32[32,32]{1,0:T(8,128)S(1)} fusion(f32[32,32,313]{2,1,0:T(8,128)} %shard_map.100), kind=kLoop, calls=%fused_computation.86 | loop fusion | bytes 8192 | tf_op jit(solution)/shard_map/slice | solution.py:245
  28.9 1.7 %slice_multiply_fusion = f32[32,32,288]{2,1,0:T(8,128)S(1)} fusion(f32[32,32,313]{2,1,0:T(8,128)} %shard_map.100, f32[32,32]{1,0:T(8,128)S(1)} %slice_reduce_fusion), kind=kLoop, calls=%fused_computation.12 | loop fusion | flops 294912 | bytes 2363392 | tf_op jit(solution)/shard_map/mul | solution.py:245
  30.8 0.8 %fusion.45 = f32[32,32,288]{2,1,0:T(8,128)S(1)} fusion(f32[32,32,313]{2,1,0:T(8,128)S(1)} %copy-done, s32[288]{0:T(512)S(1)} %add_select_fusion.2), kind=kOutput, calls=%fused_computation.82 | convolution fusion | flops 28313856 | bytes 1705984 | tf_op jit(solution)/shard_map/dot_general | solution.py:73
  31.6 0.9 %broadcast_multiply_fusion = (f32[32,32,288]{2,1,0:T(8,128)S(1)}, f32[32,32,288]{2,1,0:T(8,128)S(1)}) fusion(f32[288]{0:T(512)S(1)} %get-tuple-element.26, f32[32]{0:T(128)S(1)} %cosine_divide_fusion, f32[288]{0:T(512)S(1)} %fusion.87, s32[288]{0:T(512)S(1)} %add_select_fusion.2, f32[32,32,313]{2,1,0:T(8,128)S(1)} %copy-done), kind=kOutput, calls=%fused_computation.59 | convolution fusion | flops 29198592 | bytes 2890240 | tf_op jit(solution)/shard_map/dot_general | solution.py:73
  32.6 1.6 %fusion.5 = f32[32,29,288]{2,1,0:T(8,128)S(1)} fusion(f32[32,32,288]{2,1,0:T(8,128)S(1)} %slice_multiply_fusion, f32[32,32,288]{2,1,0:T(8,128)S(1)} %get-tuple-element.11), kind=kLoop, calls=%fused_computation.7 | loop fusion | flops 5879808 | bytes 7483392 | tf_op jit(solution)/shard_map/mul | solution.py:32
  34.2 0.4 fusion
  34.6 1.0 %fusion.10 = f32[29,28,288]{2,1,0:T(8,128)S(1)} fusion(f32[32,28,288]{2,1,0:T(8,128)S(1)} %fusion, f32[32,32,288]{2,1,0:T(8,128)S(1)} %get-tuple-element.10), kind=kLoop, calls=%fused_computation.18 | loop fusion | flops 5144832 | bytes 6547968 | tf_op jit(solution)/shard_map/mul | solution.py:32
  35.8 1.0 %multiply_subtract_fusion = f32[32,32,288]{2,1,0:T(8,128)S(1)} fusion(f32[32,32,288]{2,1,0:T(8,128)S(1)} %fusion.45, f32[288]{0:T(512)S(1)} %get-tuple-element.24, f32[288]{0:T(512)S(1)} %get-tuple-element.25, f32[32,32,313]{2,1,0:T(8,128)S(1)} %copy-done, s32[288]{0:T(512)S(1)} %add_select_fusion.2), kind=kOutput, calls=%fused_computation.10 | convolution fusion | flops 29198592 | bytes 3282944 | tf_op jit(solution)/shard_map/dot_general | solution.py:73
  36.7 2.5 %subtract_multiply_fusion = f32[28,28,288]{2,1,0:T(8,128)S(1)} fusion(f32[28,28,288]{2,1,0:T(8,128)S(1)} %fusion.17, f32[32,32,288]{2,1,0:T(8,128)S(1)} %multiply_subtract_fusion, pred[288]{0:T(512)(128)(4,1)S(1)} %get-tuple-element.29, pred[288]{0:T(512)(128)(4,1)S(1)} %get-tuple-element.30, pred[288]{0:T(512)(128)(4,1)S(1)} %add_compare_fusion.2), kind=kLoop, calls=%fused_computation.33 | loop fusion | flops 5193216 | bytes 2710368 | tf_op jit(solution)/shard_map/mul | solution.py:32
  39.3 0.8 %subtract_subtract_fusion = f32[28,28,288]{2,1,0:T(8,128)S(1)} fusion(f32[28,28,288]{2,1,0:T(8,128)S(1)} %fusion.17, f32[28,28,288]{2,1,0:T(8,128)S(1)} %subtract_multiply_fusion, pred[288]{0:T(512)(128)(4,1)S(1)} %get-tuple-element.30), kind=kLoop, calls=%fused_computation.32 | loop fusion | flops 677376 | bytes 2709792 | tf_op jit(solution)/shard_map/sub | solution.py:69
  40.1 1.4 %fusion.15 = f32[28,25,288]{2,1,0:T(8,128)S(1)} fusion(f32[28,28,288]{2,1,0:T(8,128)S(1)} %subtract_subtract_fusion, f32[32,32,288]{2,1,0:T(8,128)S(1)} %get-tuple-element.11), kind=kLoop, calls=%fused_computation.26 | loop fusion | flops 4435200 | bytes 5644800 | tf_op jit(solution)/shard_map/mul | solution.py:32
  41.5 0.3 fusion.18
  41.8 0.6 %fusion.23 = f32[25,24,288]{2,1,0:T(8,128)S(1)} fusion(f32[28,24,288]{2,1,0:T(8,128)S(1)} %fusion.18, f32[32,32,288]{2,1,0:T(8,128)S(1)} %get-tuple-element.10), kind=kLoop, calls=%fused_computation.41 | loop fusion | flops 3801600 | bytes 4838400 | tf_op jit(solution)/shard_map/mul | solution.py:32
  42.6 1.5 %subtract_multiply_fusion.1 = f32[24,24,288]{2,1,0:T(8,128)S(1)} fusion(f32[24,24,288]{2,1,0:T(8,128)S(1)} %fusion.31, f32[32,32,288]{2,1,0:T(8,128)S(1)} %multiply_subtract_fusion, pred[288]{0:T(512)(128)(4,1)S(1)} %get-tuple-element.29, pred[288]{0:T(512)(128)(4,1)S(1)} %get-tuple-element.30, pred[288]{0:T(512)(128)(4,1)S(1)} %add_compare_fusion.2), kind=kLoop, calls=%fused_computation.58 | loop fusion | flops 3815424 | bytes 1991520 | tf_op jit(solution)/shard_map/mul | solution.py:32
  44.0 0.5 subtract_subtract_fusion.1
  44.6 0.9 %fusion.29 = f32[24,21,288]{2,1,0:T(8,128)S(1)} fusion(f32[24,24,288]{2,1,0:T(8,128)S(1)} %subtract_subtract_fusion.1, f32[32,32,288]{2,1,0:T(8,128)S(1)} %get-tuple-element.11), kind=kLoop, calls=%fused_computation.51 | loop fusion | flops 3193344 | bytes 4064256 | tf_op jit(solution)/shard_map/mul | solution.py:32
  45.7 0.5 fusion.36
  46.4 1.2 %subtract_multiply_fusion.2 = f32[20,20,288]{2,1,0:T(8,128)S(1)} fusion(f32[20,20,288]{2,1,0:T(8,128)S(1)} %fusion.43, f32[32,32,288]{2,1,0:T(8,128)S(1)} %multiply_subtract_fusion, pred[288]{0:T(512)(128)(4,1)S(1)} %get-tuple-element.29, pred[288]{0:T(512)(128)(4,1)S(1)} %get-tuple-element.30, pred[288]{0:T(512)(128)(4,1)S(1)} %add_compare_fusion.2), kind=kLoop, calls=%fused_computation.80 | loop fusion | flops 2649600 | bytes 1383264 | tf_op jit(solution)/shard_map/mul | solution.py:32
  47.6 0.5 subtract_subtract_fusion.2
  48.0 0.7 %fusion.41 = f32[20,17,288]{2,1,0:T(8,128)S(1)} fusion(f32[20,20,288]{2,1,0:T(8,128)S(1)} %subtract_subtract_fusion.2, f32[32,32,288]{2,1,0:T(8,128)S(1)} %get-tuple-element.11), kind=kLoop, calls=%fused_computation.73 | loop fusion | flops 2154240 | bytes 2741760 | tf_op jit(solution)/shard_map/mul | solution.py:32
  48.9 0.3 fusion.54
  49.3 0.7 %subtract_multiply_fusion.3 = f32[16,16,288]{2,1,0:T(8,128)S(1)} fusion(f32[16,16,288]{2,1,0:T(8,128)S(1)} %fusion.60, f32[32,32,288]{2,1,0:T(8,128)S(1)} %multiply_subtract_fusion, pred[288]{0:T(512)(128)(4,1)S(1)} %get-tuple-element.29, pred[288]{0:T(512)(128)(4,1)S(1)} %get-tuple-element.30, pred[288]{0:T(512)(128)(4,1)S(1)} %add_compare_fusion.2), kind=kLoop, calls=%fused_computation.109 | loop fusion | flops 1695744 | bytes 885600 | tf_op jit(solution)/shard_map/mul | solution.py:32
  50.0 0.4 multiply_reduce_fusion
  50.4 0.8 %collective-permute-start = (f32[2,16,16]{2,1,0:T(8,128)S(1)}, f32[2,16,16]{2,1,0:T(8,128)S(1)}, u32[]{:S(2)}, u32[]{:S(2)}) collective-permute-start(f32[2,16,16]{2,1,0:T(8,128)S(1)} %pad_maximum_fusion), channel_id=1, source_target_pairs={{0,1},{1,0},{2,3},{3,2},{4,5},{5,4},{6,7},{7,6},{8,9},{9,8},{10,11... | collective-permute-start | bytes 6152 | tf_op jit(solution)/shard_map/ppermute | solution.py:272
  51.5 2.7 %collective-permute-done = f32[2,16,16]{2,1,0:T(8,128)S(1)} collective-permute-done((f32[2,16,16]{2,1,0:T(8,128)S(1)}, f32[2,16,16]{2,1,0:T(8,128)S(1)}, u32[]{:S(2)}, u32[]{:S(2)}) %collective-permute-start) | collective-permute-done | bytes 2080 | tf_op jit(solution)/shard_map/ppermute | solution.py:272
  54.2 1.1 %fusion.58 = f32[16,16,288]{2,1,0:T(8,128)} fusion(f32[16,16,288]{2,1,0:T(8,128)S(1)} %get-tuple-element.9, f32[288]{0:T(512)S(1)} %dynamic_slice.11, f32[16,16]{1,0:T(8,128)S(1)} %convert_element_type.44, f32[16,16]{1,0:T(8,128)S(1)} %get-tuple-element.15, f32[16,16]{1,0:T(8,128)S(1)} %get-tuple-element.14, f32[288]{0:T(512)S(1)} %multiply_multiply_fusion.4, ...), kind=kLoop, calls=%fused_computation.103 | loop fusion | flops 958464 | bytes 602752 | tf_op jit(solution)/shard_map/mul | solution.py:109
  (43 shorter events, 2.7 us)
Async XLA Ops:
  0.0 4.3 %copy-start.1 = (f32[16,16,288]{2,1,0:T(8,128)S(1)}, f32[16,16,288]{2,1,0:T(8,128)}, u32[]{:S(2)}) copy-start(f32[16,16,288]{2,1,0:T(8,128)} %param.10) | copy-start | bytes 884740
  28.9 1.9 %copy-start = (f32[32,32,313]{2,1,0:T(8,128)S(1)}, f32[32,32,313]{2,1,0:T(8,128)}, u32[]{:S(2)}) copy-start(f32[32,32,313]{2,1,0:T(8,128)} %shard_map.100) | copy-start | bytes 3846148
  49.3 1.9 %copy-start.2 = (f32[16,16]{1,0:T(8,128)S(1)}, f32[16,16]{1,0:T(8,128)}, u32[]{:S(2)}) copy-start(f32[16,16]{1,0:T(8,128)} %param.18) | copy-start | bytes 3076
  49.3 1.9 %copy-start.3 = (f32[16,16]{1,0:T(8,128)S(1)}, f32[16,16]{1,0:T(8,128)}, u32[]{:S(2)}) copy-start(f32[16,16]{1,0:T(8,128)} %param.17) | copy-start | bytes 3076
  49.3 2.0 %copy-start.5 = (f32[16]{0:T(128)S(1)}, f32[16]{0:T(128)}, u32[]{:S(2)}) copy-start(f32[16]{0:T(128)} %param.19) | copy-start | bytes 196
  49.3 2.1 %copy-start.4 = (s32[16,16]{1,0:T(8,128)S(1)}, s32[16,16]{1,0:T(8,128)}, u32[]{:S(2)}) copy-start(s32[16,16]{1,0:T(8,128)} %param.12) | copy-start | bytes 3076
  50.4 3.8 %collective-permute-start = (f32[2,16,16]{2,1,0:T(8,128)S(1)}, f32[2,16,16]{2,1,0:T(8,128)S(1)}, u32[]{:S(2)}, u32[]{:S(2)}) collective-permute-start(f32[2,16,16]{2,1,0:T(8,128)S(1)} %pad_maximum_fusion), channel_id=1, source_target_pairs={{0,1},{1,0},{2,3},{3,2},{4,5},{5,4},{6,7},{7,6},{8,9},{9,8},{10,11... | collective-permute-start | bytes 6152 | tf_op jit(solution)/shard_map/ppermute | solution.py:272

commit v14 on v12

--- a/solution.py
+++ b/solution.py
@@ -99,7 +99,7 @@
 ):
     mean_level = jnp.maximum(moment, 1.0) / jnp.maximum(energy_sum, 1.0)
     energy = energy_sum / NCOMP
-    breaking = break_coef * levels * levels / mean_level[..., None] * (energy * energy)[..., None]
+    breaking = break_coef * levels * levels * ((energy * energy) / mean_level)[..., None]
     alignment = (
         jnp.cos(heading) * jnp.cos(wind_dir)[..., None]
         + jnp.sin(heading) * jnp.sin(wind_dir)[..., None]

time: 54.6 us -> 54.6 us (level)
  no operation moved by 1% of the time
where the time goes in v14:
time: 54.6 us; the launch traced here: 54.1 us
  Pallas kernels  22.2 us (41%)
  other arithmetic  22 us (40%)
  matrix products  3.87 us (7%)
  waiting for transfers between devices  2.7 us (5%)
  local copies, waits for them, and re-layouts  2.24 us (4%)
  starting transfers between devices  0.77 us (1%)
    pallas_call x1, Pallas kernels, halo_exchange(): pl.pallas_call(functools.partial(halo_kernel, halo=halo), out_shape=jax.S...  22.2 us
    mul x12, other arithmetic, quickest(): return courant * face_value  13 us
    dot_general x3, matrix products, expand(): return jnp.dot(per_freq, spread, precision=lax.Precision.HIGHEST)  3.87 us
    ppermute x1, waiting for transfers between devices, per_device(): other = lax.ppermute(partial, 'band', [(0, 1), (1, 0)])  2.7 us
    sub x3, other arithmetic, refract(): return density - (fluxes - rotate(fluxes, -1))  1.81 us
    mul x1, other arithmetic, per_device(): density = spectrum * sea_share[..., None]  1.09 us
  transfers between devices with their start and end apart: 1, of which 1 were waited for; matrix products, arithmetic and copies ran while one was open for 1% of the time, Pallas kernels for 0%

profile of v14, /device:TPU:2, one launch (start us, length us, event | category | flops | bytes accessed | tf_op | source)
XLA Modules:
  0.0 54.1 jit_solution(18314005184414139731)
XLA Ops:
  0.6 0.7 %iota_compare_fusion = pred[16,16,8]{1,2,0:T(8,128)(4,1)S(1)} fusion(s32[16,16]{1,0:T(8,128)} %param.13), kind=kLoop, calls=%fused_computation.103 | loop fusion | flops 2048 | bytes 3072 | tf_op jit(solution)/shard_map/eq | solution.py:237
  1.3 0.8 %constant_dynamic-slice_fusion = (f32[8,8]{1,0:T(8,128)S(1)}, f32[8,8]{1,0:T(8,128)S(1)}) fusion(f32[8,16]{1,0:T(8,128)} %param.15, s32[]{:T(128)S(6)} %select_n.240, f32[8,16]{1,0:T(8,128)} %param.14), kind=kLoop, calls=%fused_computation.152 | loop fusion | bytes 1028 | tf_op jit(solution)/shard_map/dynamic_slice | solution.py:236
  2.1 0.3 select_reduce_fusion.1
  2.5 0.7 %convert_element_type.40 = f32[16,16]{1,0:T(8,128)S(1)} convert(s32[16,16]{1,0:T(8,128)} %param.11) | non-fusion elementwise | flops 256 | bytes 2048 | tf_op jit(solution)/shard_map/convert_element_type | solution.py:233
  3.2 0.7 %slice_bitcast_fusion.3 = (f32[16,16]{1,0:T(8,128)S(1)}, f32[16,16]{1,0:T(8,128)S(1)}) fusion(f32[2,16,16]{2,1,0:T(8,128)} %param.16), kind=kLoop, calls=%fused_computation.114 | loop fusion | bytes 4096 | tf_op jit(solution)/shard_map/mul | solution.py:240
  4.0 1.1 %broadcast_multiply_fusion.1 = f32[16,16,288]{2,1,0:T(8,128)S(1)} fusion(f32[16,16,288]{2,1,0:T(8,128)} %param.10, f32[16,16]{1,0:T(8,128)S(1)} %convert_element_type.40), kind=kLoop, calls=%fused_computation.99 | loop fusion | flops 73728 | bytes 590848 | tf_op jit(solution)/shard_map/mul | solution.py:242
  5.2 0.9 %pad_maximum_fusion.in_ref = f32[16,16,312]{2,1,0:T(8,128)} fusion(f32[16,16,8]{2,1,0:T(8,128)S(1)} %get-tuple-element.13, f32[16,16,8]{2,1,0:T(8,128)S(1)} %get-tuple-element.12, f32[16,16,8]{2,1,0:T(8,128)S(1)} %get-tuple-element.18, f32[16,16,288]{2,1,0:T(8,128)S(1)} %broadcast_multiply_fusion.1), kind=kLoop, calls=%fused_computation.94 | loop fusion | flops 239616 | bytes 638976 | tf_op jit(solution)/shard_map/concatenate | solution.py:244
  6.2 22.2 %shard_map.100 = f32[32,32,312]{2,1,0:T(8,128)} custom-call(f32[16,16,312]{2,1,0:T(8,128)} %pad_maximum_fusion.in_ref), custom_call_target="tpu_custom_call" | custom-call | tf_op jit(solution)/shard_map/pallas_call | solution.py:182
  28.4 2.0 %fusion.40 = f32[32,32,288]{2,1,0:T(8,128)S(1)} fusion(f32[32,32,312]{2,1,0:T(8,128)} %shard_map.100, s32[288]{0:T(512)S(1)} %add_select_fusion.2), kind=kOutput, calls=%fused_computation.75 | convolution fusion | flops 28313856 | bytes 1705088 | tf_op jit(solution)/shard_map/dot_general | solution.py:73
  30.4 0.9 %broadcast_multiply_fusion = (f32[32,32,288]{2,1,0:T(8,128)S(1)}, f32[32,32,288]{2,1,0:T(8,128)S(1)}) fusion(f32[288]{0:T(512)S(1)} %get-tuple-element.22, f32[32]{0:T(128)S(1)} %cosine_divide_fusion, f32[288]{0:T(512)S(1)} %fusion.78, s32[288]{0:T(512)S(1)} %add_select_fusion.2, f32[32,32,312]{2,1,0:T(8,128)S(1)} %copy-done), kind=kOutput, calls=%fused_computation.52 | convolution fusion | flops 29198592 | bytes 2890240 | tf_op jit(solution)/shard_map/dot_general | solution.py:73
  31.3 1.6 %subtract_multiply_fusion = f32[32,29,288]{2,1,0:T(8,128)S(1)} fusion(f32[32,32,312]{2,1,0:T(8,128)S(1)} %copy-done, f32[32,32,288]{2,1,0:T(8,128)S(1)} %get-tuple-element.11), kind=kLoop, calls=%fused_computation.4 | loop fusion | flops 5879808 | bytes 7483392 | tf_op jit(solution)/shard_map/mul | solution.py:32
  32.9 0.4 fusion
  33.3 1.0 %fusion.5 = f32[29,28,288]{2,1,0:T(8,128)S(1)} fusion(f32[32,28,288]{2,1,0:T(8,128)S(1)} %fusion, f32[32,32,288]{2,1,0:T(8,128)S(1)} %get-tuple-element.10), kind=kLoop, calls=%fused_computation.11 | loop fusion | flops 5144832 | bytes 6547968 | tf_op jit(solution)/shard_map/mul | solution.py:32
  34.5 1.0 %multiply_subtract_fusion = f32[32,32,288]{2,1,0:T(8,128)S(1)} fusion(f32[32,32,288]{2,1,0:T(8,128)S(1)} %fusion.40, f32[288]{0:T(512)S(1)} %get-tuple-element.20, f32[288]{0:T(512)S(1)} %get-tuple-element.21, f32[32,32,312]{2,1,0:T(8,128)S(1)} %copy-done, s32[288]{0:T(512)S(1)} %add_select_fusion.2), kind=kOutput, calls=%fused_computation.3 | convolution fusion | flops 29198592 | bytes 3282944 | tf_op jit(solution)/shard_map/dot_general | solution.py:73
  35.5 2.5 %subtract_multiply_fusion.1 = f32[28,28,288]{2,1,0:T(8,128)S(1)} fusion(f32[28,28,288]{2,1,0:T(8,128)S(1)} %fusion.12, f32[32,32,288]{2,1,0:T(8,128)S(1)} %multiply_subtract_fusion, pred[288]{0:T(512)(128)(4,1)S(1)} %get-tuple-element.25, pred[288]{0:T(512)(128)(4,1)S(1)} %get-tuple-element.26, pred[288]{0:T(512)(128)(4,1)S(1)} %add_compare_fusion.2), kind=kLoop, calls=%fused_computation.26 | loop fusion | flops 5193216 | bytes 2710368 | tf_op jit(solution)/shard_map/mul | solution.py:32
  38.0 0.8 %subtract_subtract_fusion = f32[28,28,288]{2,1,0:T(8,128)S(1)} fusion(f32[28,28,288]{2,1,0:T(8,128)S(1)} %fusion.12, f32[28,28,288]{2,1,0:T(8,128)S(1)} %subtract_multiply_fusion.1, pred[288]{0:T(512)(128)(4,1)S(1)} %get-tuple-element.26), kind=kLoop, calls=%fused_computation.25 | loop fusion | flops 677376 | bytes 2709792 | tf_op jit(solution)/shard_map/sub | solution.py:69
  38.8 1.4 %fusion.10 = f32[28,25,288]{2,1,0:T(8,128)S(1)} fusion(f32[28,28,288]{2,1,0:T(8,128)S(1)} %subtract_subtract_fusion, f32[32,32,288]{2,1,0:T(8,128)S(1)} %get-tuple-element.11), kind=kLoop, calls=%fused_computation.19 | loop fusion | flops 4435200 | bytes 5644800 | tf_op jit(solution)/shard_map/mul | solution.py:32
  40.3 0.3 fusion.13
  40.5 0.6 %fusion.18 = f32[25,24,288]{2,1,0:T(8,128)S(1)} fusion(f32[28,24,288]{2,1,0:T(8,128)S(1)} %fusion.13, f32[32,32,288]{2,1,0:T(8,128)S(1)} %get-tuple-element.10), kind=kLoop, calls=%fused_computation.34 | loop fusion | flops 3801600 | bytes 4838400 | tf_op jit(solution)/shard_map/mul | solution.py:32
  41.4 1.5 %subtract_multiply_fusion.2 = f32[24,24,288]{2,1,0:T(8,128)S(1)} fusion(f32[24,24,288]{2,1,0:T(8,128)S(1)} %fusion.26, f32[32,32,288]{2,1,0:T(8,128)S(1)} %multiply_subtract_fusion, pred[288]{0:T(512)(128)(4,1)S(1)} %get-tuple-element.25, pred[288]{0:T(512)(128)(4,1)S(1)} %get-tuple-element.26, pred[288]{0:T(512)(128)(4,1)S(1)} %add_compare_fusion.2), kind=kLoop, calls=%fused_computation.51 | loop fusion | flops 3815424 | bytes 1991520 | tf_op jit(solution)/shard_map/mul | solution.py:32
  42.8 0.5 subtract_subtract_fusion.1
  43.4 0.9 %fusion.24 = f32[24,21,288]{2,1,0:T(8,128)S(1)} fusion(f32[24,24,288]{2,1,0:T(8,128)S(1)} %subtract_subtract_fusion.1, f32[32,32,288]{2,1,0:T(8,128)S(1)} %get-tuple-element.11), kind=kLoop, calls=%fused_computation.44 | loop fusion | flops 3193344 | bytes 4064256 | tf_op jit(solution)/shard_map/mul | solution.py:32
  44.5 0.5 %fusion.31 = f32[21,20,288]{2,1,0:T(8,128)S(1)} fusion(f32[24,20,288]{2,1,0:T(8,128)S(1)} %fusion.19, f32[32,32,288]{2,1,0:T(8,128)S(1)} %get-tuple-element.10), kind=kLoop, calls=%fused_computation.58 | loop fusion | flops 2661120 | bytes 3386880 | tf_op jit(solution)/shard_map/mul | solution.py:32
  45.2 1.2 %subtract_multiply_fusion.3 = f32[20,20,288]{2,1,0:T(8,128)S(1)} fusion(f32[20,20,288]{2,1,0:T(8,128)S(1)} %fusion.38, f32[32,32,288]{2,1,0:T(8,128)S(1)} %multiply_subtract_fusion, pred[288]{0:T(512)(128)(4,1)S(1)} %get-tuple-element.25, pred[288]{0:T(512)(128)(4,1)S(1)} %get-tuple-element.26, pred[288]{0:T(512)(128)(4,1)S(1)} %add_compare_fusion.2), kind=kLoop, calls=%fused_computation.73 | loop fusion | flops 2649600 | bytes 1383264 | tf_op jit(solution)/shard_map/mul | solution.py:32
  46.4 0.5 subtract_subtract_fusion.2
  46.8 0.7 %fusion.36 = f32[20,17,288]{2,1,0:T(8,128)S(1)} fusion(f32[20,20,288]{2,1,0:T(8,128)S(1)} %subtract_subtract_fusion.2, f32[32,32,288]{2,1,0:T(8,128)S(1)} %get-tuple-element.11), kind=kLoop, calls=%fused_computation.66 | loop fusion | flops 2154240 | bytes 2741760 | tf_op jit(solution)/shard_map/mul | solution.py:32
  47.7 0.3 fusion.49
  48.1 0.7 %subtract_multiply_fusion.4 = f32[16,16,288]{2,1,0:T(8,128)S(1)} fusion(f32[16,16,288]{2,1,0:T(8,128)S(1)} %fusion.51, f32[32,32,288]{2,1,0:T(8,128)S(1)} %multiply_subtract_fusion, pred[288]{0:T(512)(128)(4,1)S(1)} %get-tuple-element.25, pred[288]{0:T(512)(128)(4,1)S(1)} %get-tuple-element.26, pred[288]{0:T(512)(128)(4,1)S(1)} %add_compare_fusion.2), kind=kLoop, calls=%fused_computation.98 | loop fusion | flops 1695744 | bytes 885600 | tf_op jit(solution)/shard_map/mul | solution.py:32
  48.8 0.4 fusion.79
  49.2 0.8 %collective-permute-start = (f32[2,16,16]{2,1,0:T(8,128)S(1)}, f32[2,16,16]{2,1,0:T(8,128)S(1)}, u32[]{:S(2)}, u32[]{:S(2)}) collective-permute-start(f32[2,16,16]{2,1,0:T(8,128)S(1)} %pad_maximum_fusion.1), channel_id=1, source_target_pairs={{0,1},{1,0},{2,3},{3,2},{4,5},{5,4},{6,7},{7,6},{8,9},{9,8},{10,11... | collective-permute-start | bytes 6152 | tf_op jit(solution)/shard_map/ppermute | solution.py:273
  50.3 2.7 %collective-permute-done = f32[2,16,16]{2,1,0:T(8,128)S(1)} collective-permute-done((f32[2,16,16]{2,1,0:T(8,128)S(1)}, f32[2,16,16]{2,1,0:T(8,128)S(1)}, u32[]{:S(2)}, u32[]{:S(2)}) %collective-permute-start) | collective-permute-done | bytes 2080 | tf_op jit(solution)/shard_map/ppermute | solution.py:273
  53.0 1.0 %exponential_multiply_fusion = f32[16,16,288]{2,1,0:T(8,128)} fusion(f32[16,16,288]{2,1,0:T(8,128)S(1)} %get-tuple-element.9, f32[288]{0:T(512)S(1)} %dynamic_slice.11, f32[16,16]{1,0:T(8,128)S(1)} %convert_element_type.44, f32[16,16]{1,0:T(8,128)S(1)} %fusion.58, f32[288]{0:T(512)S(1)} %multiply_multiply_fusion.3, f32[16,16]{1,0:T(8,128)S(1)} %get-tuple-element.17, ...), kind=kLoop, calls=%fused_computation.95 | loop fusion | flops 884736 | bytes 601728 | tf_op jit(solution)/shard_map/mul | solution.py:109
  (39 shorter events, 2.1 us)
Async XLA Ops:
  28.4 2.0 %copy-start = (f32[32,32,312]{2,1,0:T(8,128)S(1)}, f32[32,32,312]{2,1,0:T(8,128)}, u32[]{:S(2)}) copy-start(f32[32,32,312]{2,1,0:T(8,128)} %shard_map.100) | copy-start | bytes 3833860
  48.1 1.9 %copy-start.1 = (f32[16,16]{1,0:T(8,128)S(1)}, f32[16,16]{1,0:T(8,128)}, u32[]{:S(2)}) copy-start(f32[16,16]{1,0:T(8,128)} %param.18) | copy-start | bytes 3076
  48.1 1.9 %copy-start.2 = (f32[16,16]{1,0:T(8,128)S(1)}, f32[16,16]{1,0:T(8,128)}, u32[]{:S(2)}) copy-start(f32[16,16]{1,0:T(8,128)} %param.17) | copy-start | bytes 3076
  48.1 2.0 %copy-start.4 = (f32[16]{0:T(128)S(1)}, f32[16]{0:T(128)}, u32[]{:S(2)}) copy-start(f32[16]{0:T(128)} %param.19) | copy-start | bytes 196
  48.1 2.1 %copy-start.3 = (s32[16,16]{1,0:T(8,128)S(1)}, s32[16,16]{1,0:T(8,128)}, u32[]{:S(2)}) copy-start(s32[16,16]{1,0:T(8,128)} %param.12) | copy-start | bytes 3076
  49.2 3.8 %collective-permute-start = (f32[2,16,16]{2,1,0:T(8,128)S(1)}, f32[2,16,16]{2,1,0:T(8,128)S(1)}, u32[]{:S(2)}, u32[]{:S(2)}) collective-permute-start(f32[2,16,16]{2,1,0:T(8,128)S(1)} %pad_maximum_fusion.1), channel_id=1, source_target_pairs={{0,1},{1,0},{2,3},{3,2},{4,5},{5,4},{6,7},{7,6},{8,9},{9,8},{10,11... | collective-permute-start | bytes 6152 | tf_op jit(solution)/shard_map/ppermute | solution.py:273

commit v15 on v12

--- a/solution.py
+++ b/solution.py
@@ -70,7 +70,7 @@
 
 
 def expand(per_freq, spread):
-    return jnp.dot(per_freq, spread, precision=lax.Precision.HIGHEST)
+    return jnp.dot(per_freq, spread, precision=lax.Precision.HIGH)
 
 
 def lookup(classes, lookup_table):

time: 54.6 us -> 54.1 us (level)
  matrix products: 3.87 us -> 3.24 us
    dot_general x3, matrix products: 3.87 us -> 3.24 us  [expand(): return jnp.dot(per_freq, spread, precision=lax.Precision.HIGH)]
where the time goes in v15:
time: 54.1 us; the launch traced here: 53.5 us
  Pallas kernels  22.2 us (41%)
  other arithmetic  22 us (41%)
  matrix products  3.24 us (6%)
  waiting for transfers between devices  2.71 us (5%)
  local copies, waits for them, and re-layouts  2.24 us (4%)
  starting transfers between devices  0.77 us (1%)
    pallas_call x1, Pallas kernels, halo_exchange(): pl.pallas_call(functools.partial(halo_kernel, halo=halo), out_shape=jax.S...  22.2 us
    mul x12, other arithmetic, quickest(): return courant * face_value  13 us
    dot_general x3, matrix products, expand(): return jnp.dot(per_freq, spread, precision=lax.Precision.HIGH)  3.24 us
    ppermute x1, waiting for transfers between devices, per_device(): other = lax.ppermute(partial, 'band', [(0, 1), (1, 0)])  2.71 us
    sub x3, other arithmetic, refract(): return density - (fluxes - rotate(fluxes, -1))  1.81 us
    mul x1, other arithmetic, per_device(): density = spectrum * sea_share[..., None]  1.09 us
  transfers between devices with their start and end apart: 1, of which 1 were waited for; matrix products, arithmetic and copies ran while one was open for 1% of the time, Pallas kernels for 0%

profile of v15, /device:TPU:2, one launch (start us, length us, event | category | flops | bytes accessed | tf_op | source)
XLA Modules:
  0.0 53.5 jit_solution(11180247445503129935)
XLA Ops:
  0.6 0.7 %iota_compare_fusion = pred[16,16,8]{1,2,0:T(8,128)(4,1)S(1)} fusion(s32[16,16]{1,0:T(8,128)} %param.13), kind=kLoop, calls=%fused_computation.107 | loop fusion | flops 2048 | bytes 3072 | tf_op jit(solution)/shard_map/eq | solution.py:237
  1.3 0.8 %constant_dynamic-slice_fusion = (f32[8,8]{1,0:T(8,128)S(1)}, f32[8,8]{1,0:T(8,128)S(1)}) fusion(f32[8,16]{1,0:T(8,128)} %param.15, s32[]{:T(128)S(6)} %select_n.240, f32[8,16]{1,0:T(8,128)} %param.14), kind=kLoop, calls=%fused_computation.157 | loop fusion | bytes 1028 | tf_op jit(solution)/shard_map/dynamic_slice | solution.py:236
  2.1 0.3 select_reduce_fusion.1
  2.5 0.7 %convert_element_type.40 = f32[16,16]{1,0:T(8,128)S(1)} convert(s32[16,16]{1,0:T(8,128)} %param.11) | non-fusion elementwise | flops 256 | bytes 2048 | tf_op jit(solution)/shard_map/convert_element_type | solution.py:233
  3.2 0.7 %slice_bitcast_fusion.3 = (f32[16,16]{1,0:T(8,128)S(1)}, f32[16,16]{1,0:T(8,128)S(1)}) fusion(f32[2,16,16]{2,1,0:T(8,128)} %param.16), kind=kLoop, calls=%fused_computation.119 | loop fusion | bytes 4096 | tf_op jit(solution)/shard_map/mul | solution.py:240
  4.0 1.1 %broadcast_multiply_fusion.1 = f32[16,16,288]{2,1,0:T(8,128)S(1)} fusion(f32[16,16,288]{2,1,0:T(8,128)} %param.10, f32[16,16]{1,0:T(8,128)S(1)} %convert_element_type.40), kind=kLoop, calls=%fused_computation.103 | loop fusion | flops 73728 | bytes 590848 | tf_op jit(solution)/shard_map/mul | solution.py:242
  5.2 0.9 %pad_maximum_fusion.in_ref = f32[16,16,312]{2,1,0:T(8,128)} fusion(f32[16,16,8]{2,1,0:T(8,128)S(1)} %get-tuple-element.13, f32[16,16,8]{2,1,0:T(8,128)S(1)} %get-tuple-element.12, f32[16,16,8]{2,1,0:T(8,128)S(1)} %get-tuple-element.20, f32[16,16,288]{2,1,0:T(8,128)S(1)} %broadcast_multiply_fusion.1), kind=kLoop, calls=%fused_computation.99 | loop fusion | flops 239616 | bytes 638976 | tf_op jit(solution)/shard_map/concatenate | solution.py:244
  6.2 22.2 %shard_map.100 = f32[32,32,312]{2,1,0:T(8,128)} custom-call(f32[16,16,312]{2,1,0:T(8,128)} %pad_maximum_fusion.in_ref), custom_call_target="tpu_custom_call" | custom-call | tf_op jit(solution)/shard_map/pallas_call | solution.py:182
  28.4 1.8 %fusion.40 = f32[32,32,288]{2,1,0:T(8,128)S(1)} fusion(f32[32,32,312]{2,1,0:T(8,128)} %shard_map.100, s32[288]{0:T(512)S(1)} %add_select_fusion.2), kind=kOutput, calls=%fused_computation.75 | convolution fusion | flops 14158080 | bytes 1705088 | tf_op jit(solution)/shard_map/dot_general | solution.py:73
  30.2 0.7 %broadcast_multiply_fusion = (f32[32,32,288]{2,1,0:T(8,128)S(1)}, f32[32,32,288]{2,1,0:T(8,128)S(1)}) fusion(f32[288]{0:T(512)S(1)} %get-tuple-element.24, f32[32]{0:T(128)S(1)} %cosine_divide_fusion, f32[288]{0:T(512)S(1)} %fusion.82, s32[288]{0:T(512)S(1)} %add_select_fusion.2, f32[32,32,312]{2,1,0:T(8,128)S(1)} %copy-done), kind=kOutput, calls=%fused_computation.52 | convolution fusion | flops 15042816 | bytes 2890240 | tf_op jit(solution)/shard_map/dot_general | solution.py:73
  30.9 1.6 %subtract_multiply_fusion = f32[32,29,288]{2,1,0:T(8,128)S(1)} fusion(f32[32,32,312]{2,1,0:T(8,128)S(1)} %copy-done, f32[32,32,288]{2,1,0:T(8,128)S(1)} %get-tuple-element.11), kind=kLoop, calls=%fused_computation.4 | loop fusion | flops 5879808 | bytes 7483392 | tf_op jit(solution)/shard_map/mul | solution.py:32
  32.5 0.4 fusion
  32.9 1.0 %fusion.5 = f32[29,28,288]{2,1,0:T(8,128)S(1)} fusion(f32[32,28,288]{2,1,0:T(8,128)S(1)} %fusion, f32[32,32,288]{2,1,0:T(8,128)S(1)} %get-tuple-element.10), kind=kLoop, calls=%fused_computation.11 | loop fusion | flops 5144832 | bytes 6547968 | tf_op jit(solution)/shard_map/mul | solution.py:32
  34.1 0.7 %multiply_subtract_fusion = f32[32,32,288]{2,1,0:T(8,128)S(1)} fusion(f32[32,32,288]{2,1,0:T(8,128)S(1)} %fusion.40, f32[288]{0:T(512)S(1)} %get-tuple-element.22, f32[288]{0:T(512)S(1)} %get-tuple-element.23, f32[32,32,312]{2,1,0:T(8,128)S(1)} %copy-done, s32[288]{0:T(512)S(1)} %add_select_fusion.2), kind=kOutput, calls=%fused_computation.3 | convolution fusion | flops 15042816 | bytes 3282944 | tf_op jit(solution)/shard_map/dot_general | solution.py:73
  34.8 2.5 %subtract_multiply_fusion.1 = f32[28,28,288]{2,1,0:T(8,128)S(1)} fusion(f32[28,28,288]{2,1,0:T(8,128)S(1)} %fusion.12, f32[32,32,288]{2,1,0:T(8,128)S(1)} %multiply_subtract_fusion, pred[288]{0:T(512)(128)(4,1)S(1)} %get-tuple-element.27, pred[288]{0:T(512)(128)(4,1)S(1)} %get-tuple-element.28, pred[288]{0:T(512)(128)(4,1)S(1)} %add_compare_fusion.2), kind=kLoop, calls=%fused_computation.26 | loop fusion | flops 5193216 | bytes 2710368 | tf_op jit(solution)/shard_map/mul | solution.py:32
  37.4 0.8 %subtract_subtract_fusion = f32[28,28,288]{2,1,0:T(8,128)S(1)} fusion(f32[28,28,288]{2,1,0:T(8,128)S(1)} %fusion.12, f32[28,28,288]{2,1,0:T(8,128)S(1)} %subtract_multiply_fusion.1, pred[288]{0:T(512)(128)(4,1)S(1)} %get-tuple-element.28), kind=kLoop, calls=%fused_computation.25 | loop fusion | flops 677376 | bytes 2709792 | tf_op jit(solution)/shard_map/sub | solution.py:69
  38.2 1.4 %fusion.10 = f32[28,25,288]{2,1,0:T(8,128)S(1)} fusion(f32[28,28,288]{2,1,0:T(8,128)S(1)} %subtract_subtract_fusion, f32[32,32,288]{2,1,0:T(8,128)S(1)} %get-tuple-element.11), kind=kLoop, calls=%fused_computation.19 | loop fusion | flops 4435200 | bytes 5644800 | tf_op jit(solution)/shard_map/mul | solution.py:32
  39.6 0.3 fusion.13
  39.9 0.6 %fusion.18 = f32[25,24,288]{2,1,0:T(8,128)S(1)} fusion(f32[28,24,288]{2,1,0:T(8,128)S(1)} %fusion.13, f32[32,32,288]{2,1,0:T(8,128)S(1)} %get-tuple-element.10), kind=kLoop, calls=%fused_computation.34 | loop fusion | flops 3801600 | bytes 4838400 | tf_op jit(solution)/shard_map/mul | solution.py:32
  40.7 1.5 %subtract_multiply_fusion.2 = f32[24,24,288]{2,1,0:T(8,128)S(1)} fusion(f32[24,24,288]{2,1,0:T(8,128)S(1)} %fusion.26, f32[32,32,288]{2,1,0:T(8,128)S(1)} %multiply_subtract_fusion, pred[288]{0:T(512)(128)(4,1)S(1)} %get-tuple-element.27, pred[288]{0:T(512)(128)(4,1)S(1)} %get-tuple-element.28, pred[288]{0:T(512)(128)(4,1)S(1)} %add_compare_fusion.2), kind=kLoop, calls=%fused_computation.51 | loop fusion | flops 3815424 | bytes 1991520 | tf_op jit(solution)/shard_map/mul | solution.py:32
  42.2 0.5 subtract_subtract_fusion.1
  42.7 0.9 %fusion.24 = f32[24,21,288]{2,1,0:T(8,128)S(1)} fusion(f32[24,24,288]{2,1,0:T(8,128)S(1)} %subtract_subtract_fusion.1, f32[32,32,288]{2,1,0:T(8,128)S(1)} %get-tuple-element.11), kind=kLoop, calls=%fused_computation.44 | loop fusion | flops 3193344 | bytes 4064256 | tf_op jit(solution)/shard_map/mul | solution.py:32
  43.8 0.5 %fusion.31 = f32[21,20,288]{2,1,0:T(8,128)S(1)} fusion(f32[24,20,288]{2,1,0:T(8,128)S(1)} %fusion.19, f32[32,32,288]{2,1,0:T(8,128)S(1)} %get-tuple-element.10), kind=kLoop, calls=%fused_computation.58 | loop fusion | flops 2661120 | bytes 3386880 | tf_op jit(solution)/shard_map/mul | solution.py:32
  44.5 1.2 %subtract_multiply_fusion.3 = f32[20,20,288]{2,1,0:T(8,128)S(1)} fusion(f32[20,20,288]{2,1,0:T(8,128)S(1)} %fusion.38, f32[32,32,288]{2,1,0:T(8,128)S(1)} %multiply_subtract_fusion, pred[288]{0:T(512)(128)(4,1)S(1)} %get-tuple-element.27, pred[288]{0:T(512)(128)(4,1)S(1)} %get-tuple-element.28, pred[288]{0:T(512)(128)(4,1)S(1)} %add_compare_fusion.2), kind=kLoop, calls=%fused_computation.73 | loop fusion | flops 2649600 | bytes 1383264 | tf_op jit(solution)/shard_map/mul | solution.py:32
  45.7 0.5 subtract_subtract_fusion.2
  46.2 0.7 %fusion.36 = f32[20,17,288]{2,1,0:T(8,128)S(1)} fusion(f32[20,20,288]{2,1,0:T(8,128)S(1)} %subtract_subtract_fusion.2, f32[32,32,288]{2,1,0:T(8,128)S(1)} %get-tuple-element.11), kind=kLoop, calls=%fused_computation.66 | loop fusion | flops 2154240 | bytes 2741760 | tf_op jit(solution)/shard_map/mul | solution.py:32
  47.0 0.3 fusion.49
  47.5 0.7 %subtract_multiply_fusion.4 = f32[16,16,288]{2,1,0:T(8,128)S(1)} fusion(f32[16,16,288]{2,1,0:T(8,128)S(1)} %fusion.55, f32[32,32,288]{2,1,0:T(8,128)S(1)} %multiply_subtract_fusion, pred[288]{0:T(512)(128)(4,1)S(1)} %get-tuple-element.27, pred[288]{0:T(512)(128)(4,1)S(1)} %get-tuple-element.28, pred[288]{0:T(512)(128)(4,1)S(1)} %add_compare_fusion.2), kind=kLoop, calls=%fused_computation.102 | loop fusion | flops 1695744 | bytes 885600 | tf_op jit(solution)/shard_map/mul | solution.py:32
  48.2 0.4 multiply_reduce_fusion
  48.6 0.8 %collective-permute-start = (f32[2,16,16]{2,1,0:T(8,128)S(1)}, f32[2,16,16]{2,1,0:T(8,128)S(1)}, u32[]{:S(2)}, u32[]{:S(2)}) collective-permute-start(f32[2,16,16]{2,1,0:T(8,128)S(1)} %pad_maximum_fusion.1), channel_id=1, source_target_pairs={{0,1},{1,0},{2,3},{3,2},{4,5},{5,4},{6,7},{7,6},{8,9},{9,8},{10,11... | collective-permute-start | bytes 6152 | tf_op jit(solution)/shard_map/ppermute | solution.py:273
  49.7 2.7 %collective-permute-done = f32[2,16,16]{2,1,0:T(8,128)S(1)} collective-permute-done((f32[2,16,16]{2,1,0:T(8,128)S(1)}, f32[2,16,16]{2,1,0:T(8,128)S(1)}, u32[]{:S(2)}, u32[]{:S(2)}) %collective-permute-start) | collective-permute-done | bytes 2080 | tf_op jit(solution)/shard_map/ppermute | solution.py:273
  52.4 1.1 %fusion.53 = f32[16,16,288]{2,1,0:T(8,128)} fusion(f32[16,16,288]{2,1,0:T(8,128)S(1)} %get-tuple-element.9, f32[288]{0:T(512)S(1)} %dynamic_slice.11, f32[16,16]{1,0:T(8,128)S(1)} %convert_element_type.44, f32[16,16]{1,0:T(8,128)S(1)} %get-tuple-element.15, f32[16,16]{1,0:T(8,128)S(1)} %get-tuple-element.14, f32[288]{0:T(512)S(1)} %multiply_multiply_fusion.4, ...), kind=kLoop, calls=%fused_computation.95 | loop fusion | flops 958464 | bytes 602752 | tf_op jit(solution)/shard_map/mul | solution.py:109
  (39 shorter events, 2.1 us)
Async XLA Ops:
  28.4 1.8 %copy-start = (f32[32,32,312]{2,1,0:T(8,128)S(1)}, f32[32,32,312]{2,1,0:T(8,128)}, u32[]{:S(2)}) copy-start(f32[32,32,312]{2,1,0:T(8,128)} %shard_map.100) | copy-start | bytes 3833860
  47.4 1.9 %copy-start.1 = (f32[16,16]{1,0:T(8,128)S(1)}, f32[16,16]{1,0:T(8,128)}, u32[]{:S(2)}) copy-start(f32[16,16]{1,0:T(8,128)} %param.18) | copy-start | bytes 3076
  47.4 1.9 %copy-start.2 = (f32[16,16]{1,0:T(8,128)S(1)}, f32[16,16]{1,0:T(8,128)}, u32[]{:S(2)}) copy-start(f32[16,16]{1,0:T(8,128)} %param.17) | copy-start | bytes 3076
  47.4 2.0 %copy-start.4 = (f32[16]{0:T(128)S(1)}, f32[16]{0:T(128)}, u32[]{:S(2)}) copy-start(f32[16]{0:T(128)} %param.19) | copy-start | bytes 196
  47.5 2.1 %copy-start.3 = (s32[16,16]{1,0:T(8,128)S(1)}, s32[16,16]{1,0:T(8,128)}, u32[]{:S(2)}) copy-start(s32[16,16]{1,0:T(8,128)} %param.12) | copy-start | bytes 3076
  48.6 3.8 %collective-permute-start = (f32[2,16,16]{2,1,0:T(8,128)S(1)}, f32[2,16,16]{2,1,0:T(8,128)S(1)}, u32[]{:S(2)}, u32[]{:S(2)}) collective-permute-start(f32[2,16,16]{2,1,0:T(8,128)S(1)} %pad_maximum_fusion.1), channel_id=1, source_target_pairs={{0,1},{1,0},{2,3},{3,2},{4,5},{5,4},{6,7},{7,6},{8,9},{9,8},{10,11... | collective-permute-start | bytes 6152 | tf_op jit(solution)/shard_map/ppermute | solution.py:273

commit v16 on v15

--- a/solution.py
+++ b/solution.py
@@ -111,10 +111,10 @@
 
 INTERPRET = False
 MESH_ID = pl.DeviceIdType.MESH
-OFFSETS = [(a, b) for a in (-1, 0, 1) for b in (-1, 0, 1) if (a, b) != (0, 0)]
-
-
-def halo_kernel(in_ref, out_ref, send_sem, recv_sem, *, halo):
+OFFSETS = [(-1, -1), (-1, 1), (1, -1), (1, 1), (-1, 0), (1, 0), (0, -1), (0, 1)]
+
+
+def halo_kernel(in_ref, out_ref, send_sem, recv_sem, own_sem, *, halo):
     lon = lax.axis_index("lon")
     lat = lax.axis_index("lat")
     nlon = lax.axis_size("lon")
@@ -160,7 +160,8 @@
         pl.when(has(a))(copy.start)
         copies.append((a, copy))
 
-    out_ref[pl.ds(halo, rows), pl.ds(halo, cols)] = in_ref[...]
+    own = pltpu.make_async_copy(in_ref, out_ref.at[pl.ds(halo, rows), pl.ds(halo, cols)], own_sem)
+    own.start()
     ghost = jnp.zeros((halo,) + out_ref.shape[1:], out_ref.dtype)
 
     @pl.when(lat == 0)
@@ -174,6 +175,7 @@
     for a, copy in copies:
         pl.when(has(a))(copy.wait_send)
         pl.when(has(-a))(copy.wait_recv)
+    own.wait()
 
 
 def halo_exchange(cells, halo):
@@ -184,7 +186,11 @@
         out_shape=jax.ShapeDtypeStruct((rows + 2 * halo, cols + 2 * halo, chans), cells.dtype),
         in_specs=[vmem],
         out_specs=vmem,
-        scratch_shapes=[pltpu.SemaphoreType.DMA((8,)), pltpu.SemaphoreType.DMA((8,))],
+        scratch_shapes=[
+            pltpu.SemaphoreType.DMA((8,)),
+            pltpu.SemaphoreType.DMA((8,)),
+            pltpu.SemaphoreType.DMA(()),
+        ],
         compiler_params=pltpu.CompilerParams(collective_id=0, has_side_effects=True),
         interpret=pltpu.InterpretParams(detect_races=True) if INTERPRET else False,
     )(cells)

time: 54.1 us -> 53.8 us (level)
  no operation moved by 1% of the time
where the time goes in v16:
time: 53.8 us; the launch traced here: 53.4 us
  Pallas kernels  22.1 us (41%)
  other arithmetic  22 us (41%)
  matrix products  3.24 us (6%)
  waiting for transfers between devices  2.76 us (5%)
  local copies, waits for them, and re-layouts  2.24 us (4%)
  starting transfers between devices  0.72 us (1%)
    pallas_call x1, Pallas kernels, halo_exchange(): pl.pallas_call(functools.partial(halo_kernel, halo=halo), out_shape=jax.S...  22.1 us
    mul x12, other arithmetic, quickest(): return courant * face_value  13 us
    dot_general x3, matrix products, expand(): return jnp.dot(per_freq, spread, precision=lax.Precision.HIGH)  3.24 us
    ppermute x1, waiting for transfers between devices, per_device(): other = lax.ppermute(partial, 'band', [(0, 1), (1, 0)])  2.76 us
    sub x3, other arithmetic, refract(): return density - (fluxes - rotate(fluxes, -1))  1.81 us
    mul x1, other arithmetic, per_device(): density = spectrum * sea_share[..., None]  1.09 us
  transfers between devices with their start and end apart: 1, of which 1 were waited for; matrix products, arithmetic and copies ran while one was open for 1% of the time, Pallas kernels for 0%

profile of v16, /device:TPU:2, one launch (start us, length us, event | category | flops | bytes accessed | tf_op | source)
XLA Modules:
  0.0 53.4 jit_solution(12651540341756606776)
XLA Ops:
  0.6 0.7 %iota_compare_fusion = pred[16,16,8]{1,2,0:T(8,128)(4,1)S(1)} fusion(s32[16,16]{1,0:T(8,128)} %param.13), kind=kLoop, calls=%fused_computation.107 | loop fusion | flops 2048 | bytes 3072 | tf_op jit(solution)/shard_map/eq | solution.py:243
  1.3 0.8 %constant_dynamic-slice_fusion = (f32[8,8]{1,0:T(8,128)S(1)}, f32[8,8]{1,0:T(8,128)S(1)}) fusion(f32[8,16]{1,0:T(8,128)} %param.15, s32[]{:T(128)S(6)} %select_n.240, f32[8,16]{1,0:T(8,128)} %param.14), kind=kLoop, calls=%fused_computation.157 | loop fusion | bytes 1028 | tf_op jit(solution)/shard_map/dynamic_slice | solution.py:242
  2.1 0.3 select_reduce_fusion.1
  2.5 0.7 %convert_element_type.40 = f32[16,16]{1,0:T(8,128)S(1)} convert(s32[16,16]{1,0:T(8,128)} %param.11) | non-fusion elementwise | flops 256 | bytes 2048 | tf_op jit(solution)/shard_map/convert_element_type | solution.py:239
  3.2 0.7 %slice_bitcast_fusion.3 = (f32[16,16]{1,0:T(8,128)S(1)}, f32[16,16]{1,0:T(8,128)S(1)}) fusion(f32[2,16,16]{2,1,0:T(8,128)} %param.16), kind=kLoop, calls=%fused_computation.119 | loop fusion | bytes 4096 | tf_op jit(solution)/shard_map/mul | solution.py:246
  4.0 1.1 %broadcast_multiply_fusion.1 = f32[16,16,288]{2,1,0:T(8,128)S(1)} fusion(f32[16,16,288]{2,1,0:T(8,128)} %param.10, f32[16,16]{1,0:T(8,128)S(1)} %convert_element_type.40), kind=kLoop, calls=%fused_computation.103 | loop fusion | flops 73728 | bytes 590848 | tf_op jit(solution)/shard_map/mul | solution.py:248
  5.2 0.9 %pad_maximum_fusion.in_ref = f32[16,16,312]{2,1,0:T(8,128)} fusion(f32[16,16,8]{2,1,0:T(8,128)S(1)} %get-tuple-element.13, f32[16,16,8]{2,1,0:T(8,128)S(1)} %get-tuple-element.12, f32[16,16,8]{2,1,0:T(8,128)S(1)} %get-tuple-element.20, f32[16,16,288]{2,1,0:T(8,128)S(1)} %broadcast_multiply_fusion.1), kind=kLoop, calls=%fused_computation.99 | loop fusion | flops 239616 | bytes 638976 | tf_op jit(solution)/shard_map/concatenate | solution.py:250
  6.2 22.1 %shard_map.100 = f32[32,32,312]{2,1,0:T(8,128)} custom-call(f32[16,16,312]{2,1,0:T(8,128)} %pad_maximum_fusion.in_ref), custom_call_target="tpu_custom_call" | custom-call | tf_op jit(solution)/shard_map/pallas_call | solution.py:184
  28.3 1.8 %fusion.40 = f32[32,32,288]{2,1,0:T(8,128)S(1)} fusion(f32[32,32,312]{2,1,0:T(8,128)} %shard_map.100, s32[288]{0:T(512)S(1)} %add_select_fusion.2), kind=kOutput, calls=%fused_computation.75 | convolution fusion | flops 14158080 | bytes 1705088 | tf_op jit(solution)/shard_map/dot_general | solution.py:73
  30.1 0.7 %broadcast_multiply_fusion = (f32[32,32,288]{2,1,0:T(8,128)S(1)}, f32[32,32,288]{2,1,0:T(8,128)S(1)}) fusion(f32[288]{0:T(512)S(1)} %get-tuple-element.24, f32[32]{0:T(128)S(1)} %cosine_divide_fusion, f32[288]{0:T(512)S(1)} %fusion.82, s32[288]{0:T(512)S(1)} %add_select_fusion.2, f32[32,32,312]{2,1,0:T(8,128)S(1)} %copy-done), kind=kOutput, calls=%fused_computation.52 | convolution fusion | flops 15042816 | bytes 2890240 | tf_op jit(solution)/shard_map/dot_general | solution.py:73
  30.9 1.6 %subtract_multiply_fusion = f32[32,29,288]{2,1,0:T(8,128)S(1)} fusion(f32[32,32,312]{2,1,0:T(8,128)S(1)} %copy-done, f32[32,32,288]{2,1,0:T(8,128)S(1)} %get-tuple-element.11), kind=kLoop, calls=%fused_computation.4 | loop fusion | flops 5879808 | bytes 7483392 | tf_op jit(solution)/shard_map/mul | solution.py:32
  32.5 0.4 fusion
  32.9 1.0 %fusion.5 = f32[29,28,288]{2,1,0:T(8,128)S(1)} fusion(f32[32,28,288]{2,1,0:T(8,128)S(1)} %fusion, f32[32,32,288]{2,1,0:T(8,128)S(1)} %get-tuple-element.10), kind=kLoop, calls=%fused_computation.11 | loop fusion | flops 5144832 | bytes 6547968 | tf_op jit(solution)/shard_map/mul | solution.py:32
  34.1 0.7 %multiply_subtract_fusion = f32[32,32,288]{2,1,0:T(8,128)S(1)} fusion(f32[32,32,288]{2,1,0:T(8,128)S(1)} %fusion.40, f32[288]{0:T(512)S(1)} %get-tuple-element.22, f32[288]{0:T(512)S(1)} %get-tuple-element.23, f32[32,32,312]{2,1,0:T(8,128)S(1)} %copy-done, s32[288]{0:T(512)S(1)} %add_select_fusion.2), kind=kOutput, calls=%fused_computation.3 | convolution fusion | flops 15042816 | bytes 3282944 | tf_op jit(solution)/shard_map/dot_general | solution.py:73
  34.8 2.5 %subtract_multiply_fusion.1 = f32[28,28,288]{2,1,0:T(8,128)S(1)} fusion(f32[28,28,288]{2,1,0:T(8,128)S(1)} %fusion.12, f32[32,32,288]{2,1,0:T(8,128)S(1)} %multiply_subtract_fusion, pred[288]{0:T(512)(128)(4,1)S(1)} %get-tuple-element.27, pred[288]{0:T(512)(128)(4,1)S(1)} %get-tuple-element.28, pred[288]{0:T(512)(128)(4,1)S(1)} %add_compare_fusion.2), kind=kLoop, calls=%fused_computation.26 | loop fusion | flops 5193216 | bytes 2710368 | tf_op jit(solution)/shard_map/mul | solution.py:32
  37.3 0.8 %subtract_subtract_fusion = f32[28,28,288]{2,1,0:T(8,128)S(1)} fusion(f32[28,28,288]{2,1,0:T(8,128)S(1)} %fusion.12, f32[28,28,288]{2,1,0:T(8,128)S(1)} %subtract_multiply_fusion.1, pred[288]{0:T(512)(128)(4,1)S(1)} %get-tuple-element.28), kind=kLoop, calls=%fused_computation.25 | loop fusion | flops 677376 | bytes 2709792 | tf_op jit(solution)/shard_map/sub | solution.py:69
  38.2 1.4 %fusion.10 = f32[28,25,288]{2,1,0:T(8,128)S(1)} fusion(f32[28,28,288]{2,1,0:T(8,128)S(1)} %subtract_subtract_fusion, f32[32,32,288]{2,1,0:T(8,128)S(1)} %get-tuple-element.11), kind=kLoop, calls=%fused_computation.19 | loop fusion | flops 4435200 | bytes 5644800 | tf_op jit(solution)/shard_map/mul | solution.py:32
  39.6 0.3 fusion.13
  39.9 0.6 %fusion.18 = f32[25,24,288]{2,1,0:T(8,128)S(1)} fusion(f32[28,24,288]{2,1,0:T(8,128)S(1)} %fusion.13, f32[32,32,288]{2,1,0:T(8,128)S(1)} %get-tuple-element.10), kind=kLoop, calls=%fused_computation.34 | loop fusion | flops 3801600 | bytes 4838400 | tf_op jit(solution)/shard_map/mul | solution.py:32
  40.7 1.5 %subtract_multiply_fusion.2 = f32[24,24,288]{2,1,0:T(8,128)S(1)} fusion(f32[24,24,288]{2,1,0:T(8,128)S(1)} %fusion.26, f32[32,32,288]{2,1,0:T(8,128)S(1)} %multiply_subtract_fusion, pred[288]{0:T(512)(128)(4,1)S(1)} %get-tuple-element.27, pred[288]{0:T(512)(128)(4,1)S(1)} %get-tuple-element.28, pred[288]{0:T(512)(128)(4,1)S(1)} %add_compare_fusion.2), kind=kLoop, calls=%fused_computation.51 | loop fusion | flops 3815424 | bytes 1991520 | tf_op jit(solution)/shard_map/mul | solution.py:32
  42.1 0.5 subtract_subtract_fusion.1
  42.7 0.9 %fusion.24 = f32[24,21,288]{2,1,0:T(8,128)S(1)} fusion(f32[24,24,288]{2,1,0:T(8,128)S(1)} %subtract_subtract_fusion.1, f32[32,32,288]{2,1,0:T(8,128)S(1)} %get-tuple-element.11), kind=kLoop, calls=%fused_computation.44 | loop fusion | flops 3193344 | bytes 4064256 | tf_op jit(solution)/shard_map/mul | solution.py:32
  43.8 0.5 %fusion.31 = f32[21,20,288]{2,1,0:T(8,128)S(1)} fusion(f32[24,20,288]{2,1,0:T(8,128)S(1)} %fusion.19, f32[32,32,288]{2,1,0:T(8,128)S(1)} %get-tuple-element.10), kind=kLoop, calls=%fused_computation.58 | loop fusion | flops 2661120 | bytes 3386880 | tf_op jit(solution)/shard_map/mul | solution.py:32
  44.5 1.2 %subtract_multiply_fusion.3 = f32[20,20,288]{2,1,0:T(8,128)S(1)} fusion(f32[20,20,288]{2,1,0:T(8,128)S(1)} %fusion.38, f32[32,32,288]{2,1,0:T(8,128)S(1)} %multiply_subtract_fusion, pred[288]{0:T(512)(128)(4,1)S(1)} %get-tuple-element.27, pred[288]{0:T(512)(128)(4,1)S(1)} %get-tuple-element.28, pred[288]{0:T(512)(128)(4,1)S(1)} %add_compare_fusion.2), kind=kLoop, calls=%fused_computation.73 | loop fusion | flops 2649600 | bytes 1383264 | tf_op jit(solution)/shard_map/mul | solution.py:32
  45.7 0.5 subtract_subtract_fusion.2
  46.2 0.7 %fusion.36 = f32[20,17,288]{2,1,0:T(8,128)S(1)} fusion(f32[20,20,288]{2,1,0:T(8,128)S(1)} %subtract_subtract_fusion.2, f32[32,32,288]{2,1,0:T(8,128)S(1)} %get-tuple-element.11), kind=kLoop, calls=%fused_computation.66 | loop fusion | flops 2154240 | bytes 2741760 | tf_op jit(solution)/shard_map/mul | solution.py:32
  47.0 0.3 fusion.49
  47.4 0.7 %subtract_multiply_fusion.4 = f32[16,16,288]{2,1,0:T(8,128)S(1)} fusion(f32[16,16,288]{2,1,0:T(8,128)S(1)} %fusion.55, f32[32,32,288]{2,1,0:T(8,128)S(1)} %multiply_subtract_fusion, pred[288]{0:T(512)(128)(4,1)S(1)} %get-tuple-element.27, pred[288]{0:T(512)(128)(4,1)S(1)} %get-tuple-element.28, pred[288]{0:T(512)(128)(4,1)S(1)} %add_compare_fusion.2), kind=kLoop, calls=%fused_computation.102 | loop fusion | flops 1695744 | bytes 885600 | tf_op jit(solution)/shard_map/mul | solution.py:32
  48.1 0.4 multiply_reduce_fusion
  48.5 0.7 %collective-permute-start = (f32[2,16,16]{2,1,0:T(8,128)S(1)}, f32[2,16,16]{2,1,0:T(8,128)S(1)}, u32[]{:S(2)}, u32[]{:S(2)}) collective-permute-start(f32[2,16,16]{2,1,0:T(8,128)S(1)} %pad_maximum_fusion.1), channel_id=1, source_target_pairs={{0,1},{1,0},{2,3},{3,2},{4,5},{5,4},{6,7},{7,6},{8,9},{9,8},{10,11... | collective-permute-start | bytes 6152 | tf_op jit(solution)/shard_map/ppermute | solution.py:279
  49.6 2.8 %collective-permute-done = f32[2,16,16]{2,1,0:T(8,128)S(1)} collective-permute-done((f32[2,16,16]{2,1,0:T(8,128)S(1)}, f32[2,16,16]{2,1,0:T(8,128)S(1)}, u32[]{:S(2)}, u32[]{:S(2)}) %collective-permute-start) | collective-permute-done | bytes 2080 | tf_op jit(solution)/shard_map/ppermute | solution.py:279
  52.4 1.1 %fusion.53 = f32[16,16,288]{2,1,0:T(8,128)} fusion(f32[16,16,288]{2,1,0:T(8,128)S(1)} %get-tuple-element.9, f32[288]{0:T(512)S(1)} %dynamic_slice.11, f32[16,16]{1,0:T(8,128)S(1)} %convert_element_type.44, f32[16,16]{1,0:T(8,128)S(1)} %get-tuple-element.15, f32[16,16]{1,0:T(8,128)S(1)} %get-tuple-element.14, f32[288]{0:T(512)S(1)} %multiply_multiply_fusion.4, ...), kind=kLoop, calls=%fused_computation.95 | loop fusion | flops 958464 | bytes 602752 | tf_op jit(solution)/shard_map/mul | solution.py:109
  (39 shorter events, 2.1 us)
Async XLA Ops:
  28.3 1.8 %copy-start = (f32[32,32,312]{2,1,0:T(8,128)S(1)}, f32[32,32,312]{2,1,0:T(8,128)}, u32[]{:S(2)}) copy-start(f32[32,32,312]{2,1,0:T(8,128)} %shard_map.100) | copy-start | bytes 3833860
  47.4 1.9 %copy-start.1 = (f32[16,16]{1,0:T(8,128)S(1)}, f32[16,16]{1,0:T(8,128)}, u32[]{:S(2)}) copy-start(f32[16,16]{1,0:T(8,128)} %param.18) | copy-start | bytes 3076
  47.4 1.8 %copy-start.2 = (f32[16,16]{1,0:T(8,128)S(1)}, f32[16,16]{1,0:T(8,128)}, u32[]{:S(2)}) copy-start(f32[16,16]{1,0:T(8,128)} %param.17) | copy-start | bytes 3076
  47.4 1.9 %copy-start.4 = (f32[16]{0:T(128)S(1)}, f32[16]{0:T(128)}, u32[]{:S(2)}) copy-start(f32[16]{0:T(128)} %param.19) | copy-start | bytes 196
  47.4 2.1 %copy-start.3 = (s32[16,16]{1,0:T(8,128)S(1)}, s32[16,16]{1,0:T(8,128)}, u32[]{:S(2)}) copy-start(s32[16,16]{1,0:T(8,128)} %param.12) | copy-start | bytes 3076
  48.5 3.8 %collective-permute-start = (f32[2,16,16]{2,1,0:T(8,128)S(1)}, f32[2,16,16]{2,1,0:T(8,128)S(1)}, u32[]{:S(2)}, u32[]{:S(2)}) collective-permute-start(f32[2,16,16]{2,1,0:T(8,128)S(1)} %pad_maximum_fusion.1), channel_id=1, source_target_pairs={{0,1},{1,0},{2,3},{3,2},{4,5},{5,4},{6,7},{7,6},{8,9},{9,8},{10,11... | collective-permute-start | bytes 6152 | tf_op jit(solution)/shard_map/ppermute | solution.py:279

commit v17 on v16

--- a/solution.py
+++ b/solution.py
@@ -260,10 +260,10 @@
     gs_ext = expand(fields[..., :freqs_dev], spread)
     along_x = gs_ext * cos_head * stretch_rows[:, None, None]
     along_y = gs_ext * sin_head
-    along_t = (
-        expand(fields[..., freqs_dev : 2 * freqs_dev], spread) * sin_face
-        - expand(fields[..., 2 * freqs_dev :], spread) * cos_face
-    )
+    turns = expand(
+        jnp.stack([fields[..., freqs_dev : 2 * freqs_dev], fields[..., 2 * freqs_dev :]]), spread
+    )
+    along_t = turns[0] * sin_face - turns[1] * cos_face
     for substep in range(ITERS):
         density = advect(density, along_x, 1)
         along_x, along_y, along_t = [trim(a, 1, 2) for a in (along_x, along_y, along_t)]

time: 53.8 us -> 62.1 us (1.15)
  local copies, waits for them, and re-layouts: 2.24 us -> 7.35 us
  other arithmetic: 22 us -> 26.6 us
  matrix products: 3.24 us -> 1.74 us
    another operation x0 -> x3, local copies, waits for them, and re-layouts: none -> 5.1 us  [per_device(): jnp.stack([fields[..., freqs_dev:2 * freqs_dev], fields[..., 2 * freqs_de...]
    mul x12, other arithmetic: 13 us -> 16.3 us  [quickest(): return courant * face_value]
    dot_general x3 -> x2, matrix products: 3.24 us -> 1.74 us  [expand(): return jnp.dot(per_freq, spread, precision=lax.Precision.HIGH)]
    sub x4, other arithmetic: 0.93 us -> 2.07 us  [advect(): piece(density, 2, length - 2)]
  transfers between devices with their start and end apart: 1 -> 1, of which waited for: 1 -> 1; matrix products, arithmetic and copies ran while one was open for 1% -> 0% of each run, Pallas kernels for 0% -> 0%
where the time goes in v17:
time: 62.1 us; the launch traced here: 61.7 us
  other arithmetic  26.6 us (43%)
  Pallas kernels  22.1 us (36%)
  local copies, waits for them, and re-layouts  7.35 us (12%)
  waiting for transfers between devices  2.76 us (4%)
  matrix products  1.74 us (3%)
  starting transfers between devices  0.72 us (1%)
    pallas_call x1, Pallas kernels, halo_exchange(): pl.pallas_call(functools.partial(halo_kernel, halo=halo), out_shape=jax.S...  22.1 us
    mul x12, other arithmetic, quickest(): return courant * face_value  16.3 us
    another operation x3, local copies, waits for them, and re-layouts, per_device(): jnp.stack([fields[..., freqs_dev:2 * freqs_dev], fields[..., 2 * freqs_de...  5.1 us
    ppermute x1, waiting for transfers between devices, per_device(): other = lax.ppermute(partial, 'band', [(0, 1), (1, 0)])  2.76 us
    sub x4, other arithmetic, advect(): piece(density, 2, length - 2)  2.07 us
    sub x3, other arithmetic, refract(): return density - (fluxes - rotate(fluxes, -1))  1.79 us
    dot_general x2, matrix products, expand(): return jnp.dot(per_freq, spread, precision=lax.Precision.HIGH)  1.74 us
  transfers between devices with their start and end apart: 1, of which 1 were waited for; matrix products, arithmetic and copies ran while one was open for 0% of the time, Pallas kernels for 0%

profile of v17, /device:TPU:2, one launch (start us, length us, event | category | flops | bytes accessed | tf_op | source)
XLA Modules:
  0.0 61.7 jit_solution(11698635580562174706)
XLA Ops:
  0.6 0.7 %iota_compare_fusion = pred[16,16,8]{1,2,0:T(8,128)(4,1)S(1)} fusion(s32[16,16]{1,0:T(8,128)} %param.13), kind=kLoop, calls=%fused_computation.114 | loop fusion | flops 2048 | bytes 3072 | tf_op jit(solution)/shard_map/eq | solution.py:243
  1.3 0.8 %constant_dynamic-slice_fusion = (f32[8,8]{1,0:T(8,128)S(1)}, f32[8,8]{1,0:T(8,128)S(1)}) fusion(f32[8,16]{1,0:T(8,128)} %param.15, s32[]{:T(128)S(6)} %select_n.238, f32[8,16]{1,0:T(8,128)} %param.14), kind=kLoop, calls=%fused_computation.164 | loop fusion | bytes 1028 | tf_op jit(solution)/shard_map/dynamic_slice | solution.py:242
  2.4 0.7 %slice_bitcast_fusion.7 = (f32[16,16]{1,0:T(8,128)S(1)}, f32[16,16]{1,0:T(8,128)S(1)}) fusion(f32[2,16,16]{2,1,0:T(8,128)} %param.16), kind=kLoop, calls=%fused_computation.127 | loop fusion | bytes 4096 | tf_op jit(solution)/shard_map/mul | solution.py:246
  3.2 0.7 %convert_element_type.40 = f32[16,16]{1,0:T(8,128)S(1)} convert(s32[16,16]{1,0:T(8,128)} %param.11) | non-fusion elementwise | flops 256 | bytes 2048 | tf_op jit(solution)/shard_map/convert_element_type | solution.py:239
  4.0 1.1 %broadcast_multiply_fusion.1 = f32[16,16,288]{2,1,0:T(8,128)S(1)} fusion(f32[16,16,288]{2,1,0:T(8,128)} %param.10, f32[16,16]{1,0:T(8,128)S(1)} %convert_element_type.40), kind=kLoop, calls=%fused_computation.110 | loop fusion | flops 73728 | bytes 590848 | tf_op jit(solution)/shard_map/mul | solution.py:248
  5.2 0.9 %pad_maximum_fusion.in_ref = f32[16,16,312]{2,1,0:T(8,128)} fusion(f32[16,16,8]{2,1,0:T(8,128)S(1)} %get-tuple-element.15, f32[16,16,8]{2,1,0:T(8,128)S(1)} %get-tuple-element.14, f32[16,16,8]{2,1,0:T(8,128)S(1)} %get-tuple-element.22, f32[16,16,288]{2,1,0:T(8,128)S(1)} %broadcast_multiply_fusion.1), kind=kLoop, calls=%fused_computation.102 | loop fusion | flops 239616 | bytes 638976 | tf_op jit(solution)/shard_map/concatenate | solution.py:250
  6.2 22.1 %shard_map.100 = f32[32,32,312]{2,1,0:T(8,128)} custom-call(f32[16,16,312]{2,1,0:T(8,128)} %pad_maximum_fusion.in_ref), custom_call_target="tpu_custom_call" | custom-call | tf_op jit(solution)/shard_map/pallas_call | solution.py:184
  28.3 2.6 %slice_bitcast_fusion.3 = (f32[1,32,32,8]{3,2,1,0:T(8,128)}, f32[1,32,32,8]{3,2,1,0:T(8,128)}) fusion(f32[32,32,312]{2,1,0:T(8,128)} %shard_map.100), kind=kLoop, calls=%fused_computation.79 | loop fusion | bytes 131072 | tf_op jit(solution)/shard_map/stack | solution.py:264
  31.0 0.7 %broadcast_multiply_fusion = (f32[32,32,288]{2,1,0:T(8,128)S(1)}, f32[32,32,288]{2,1,0:T(8,128)S(1)}) fusion(f32[288]{0:T(512)S(1)} %get-tuple-element.26, f32[32]{0:T(128)S(1)} %cosine_divide_fusion, f32[288]{0:T(512)S(1)} %fusion.85, s32[288]{0:T(512)S(1)} %add_select_fusion.2, f32[32,32,312]{2,1,0:T(8,128)S(1)} %copy-done), kind=kOutput, calls=%fused_computation.56 | convolution fusion | flops 15042816 | bytes 2890240 | tf_op jit(solution)/shard_map/dot_general | solution.py:73
  31.7 1.6 %subtract_multiply_fusion = f32[32,29,288]{2,1,0:T(8,128)S(1)} fusion(f32[32,32,312]{2,1,0:T(8,128)S(1)} %copy-done, f32[32,32,288]{2,1,0:T(8,128)S(1)} %get-tuple-element.13), kind=kLoop, calls=%fused_computation.8 | loop fusion | flops 5879808 | bytes 7483392 | tf_op jit(solution)/shard_map/mul | solution.py:32
  33.3 1.5 %fusion.3 = f32[32,28,288]{2,1,0:T(8,128)} fusion(f32[32,29,288]{2,1,0:T(8,128)S(1)} %subtract_multiply_fusion, f32[32,32,312]{2,1,0:T(8,128)S(1)} %copy-done), kind=kLoop, calls=%fused_computation.6 | loop fusion | flops 516096 | bytes 4128768 | tf_op jit(solution)/shard_map/sub | solution.py:50
  34.8 1.2 %copy.20 = f32[1,32,32,8]{2,3,1,0:T(8,128)S(1)} copy(f32[1,32,32,8]{3,2,1,0:T(8,128)} %get-tuple-element.11) | data formatting | bytes 65536 | tf_op jit(solution)/shard_map/stack | solution.py:264
  36.0 1.2 %copy.19 = f32[1,32,32,8]{2,3,1,0:T(8,128)S(1)} copy(f32[1,32,32,8]{3,2,1,0:T(8,128)} %get-tuple-element.10) | data formatting | bytes 65536 | tf_op jit(solution)/shard_map/stack | solution.py:264
  37.3 4.2 %fusion.8 = f32[29,28,288]{2,1,0:T(8,128)S(1)} fusion(f32[32,28,288]{2,1,0:T(8,128)} %fusion.3, f32[32,32,288]{2,1,0:T(8,128)S(1)} %get-tuple-element.12), kind=kLoop, calls=%fused_computation.15 | loop fusion | flops 5144832 | bytes 6547968 | tf_op jit(solution)/shard_map/mul | solution.py:32
  41.7 1.0 %fusion.56 = f32[2,32,32,288]{3,2,1,0:T(8,128)S(1)} fusion(f32[1,32,32,8]{2,3,1,0:T(8,128)S(1)} %copy.20, f32[1,32,32,8]{2,3,1,0:T(8,128)S(1)} %copy.19, s32[288]{0:T(512)S(1)} %add_select_fusion.2), kind=kOutput, calls=%fused_computation.106 | convolution fusion | flops 28330240 | bytes 2425984 | tf_op jit(solution)/shard_map/dot_general | solution.py:73
  42.8 0.3 fusion.1
  43.1 2.5 %subtract_multiply_fusion.1 = f32[28,28,288]{2,1,0:T(8,128)S(1)} fusion(f32[28,28,288]{2,1,0:T(8,128)S(1)} %fusion.15, f32[32,32,288]{2,1,0:T(8,128)S(1)} %fusion.1, pred[288]{0:T(512)(128)(4,1)S(1)} %get-tuple-element.29, pred[288]{0:T(512)(128)(4,1)S(1)} %get-tuple-element.30, pred[288]{0:T(512)(128)(4,1)S(1)} %add_compare_fusion.2), kind=kLoop, calls=%fused_computation.30 | loop fusion | flops 5193216 | bytes 2710368 | tf_op jit(solution)/shard_map/mul | solution.py:32
  45.6 0.8 %subtract_subtract_fusion = f32[28,28,288]{2,1,0:T(8,128)S(1)} fusion(f32[28,28,288]{2,1,0:T(8,128)S(1)} %fusion.15, f32[28,28,288]{2,1,0:T(8,128)S(1)} %subtract_multiply_fusion.1, pred[288]{0:T(512)(128)(4,1)S(1)} %get-tuple-element.30), kind=kLoop, calls=%fused_computation.29 | loop fusion | flops 677376 | bytes 2709792 | tf_op jit(solution)/shard_map/sub | solution.py:69
  46.4 1.4 %fusion.13 = f32[28,25,288]{2,1,0:T(8,128)S(1)} fusion(f32[28,28,288]{2,1,0:T(8,128)S(1)} %subtract_subtract_fusion, f32[32,32,288]{2,1,0:T(8,128)S(1)} %get-tuple-element.13), kind=kLoop, calls=%fused_computation.23 | loop fusion | flops 4435200 | bytes 5644800 | tf_op jit(solution)/shard_map/mul | solution.py:32
  48.1 0.6 %fusion.21 = f32[25,24,288]{2,1,0:T(8,128)S(1)} fusion(f32[28,24,288]{2,1,0:T(8,128)S(1)} %fusion.16, f32[32,32,288]{2,1,0:T(8,128)S(1)} %get-tuple-element.12), kind=kLoop, calls=%fused_computation.38 | loop fusion | flops 3801600 | bytes 4838400 | tf_op jit(solution)/shard_map/mul | solution.py:32
  48.9 1.5 %subtract_multiply_fusion.2 = f32[24,24,288]{2,1,0:T(8,128)S(1)} fusion(f32[24,24,288]{2,1,0:T(8,128)S(1)} %fusion.29, f32[32,32,288]{2,1,0:T(8,128)S(1)} %fusion.1, pred[288]{0:T(512)(128)(4,1)S(1)} %get-tuple-element.29, pred[288]{0:T(512)(128)(4,1)S(1)} %get-tuple-element.30, pred[288]{0:T(512)(128)(4,1)S(1)} %add_compare_fusion.2), kind=kLoop, calls=%fused_computation.55 | loop fusion | flops 3815424 | bytes 1991520 | tf_op jit(solution)/shard_map/mul | solution.py:32
  50.4 0.5 subtract_subtract_fusion.1
  50.9 0.9 %fusion.27 = f32[24,21,288]{2,1,0:T(8,128)S(1)} fusion(f32[24,24,288]{2,1,0:T(8,128)S(1)} %subtract_subtract_fusion.1, f32[32,32,288]{2,1,0:T(8,128)S(1)} %get-tuple-element.13), kind=kLoop, calls=%fused_computation.48 | loop fusion | flops 3193344 | bytes 4064256 | tf_op jit(solution)/shard_map/mul | solution.py:32
  52.0 0.5 fusion.34
  52.7 1.2 %subtract_multiply_fusion.3 = f32[20,20,288]{2,1,0:T(8,128)S(1)} fusion(f32[20,20,288]{2,1,0:T(8,128)S(1)} %fusion.41, f32[32,32,288]{2,1,0:T(8,128)S(1)} %fusion.1, pred[288]{0:T(512)(128)(4,1)S(1)} %get-tuple-element.29, pred[288]{0:T(512)(128)(4,1)S(1)} %get-tuple-element.30, pred[288]{0:T(512)(128)(4,1)S(1)} %add_compare_fusion.2), kind=kLoop, calls=%fused_computation.77 | loop fusion | flops 2649600 | bytes 1383264 | tf_op jit(solution)/shard_map/mul | solution.py:32
  53.9 0.5 subtract_subtract_fusion.2
  54.4 0.7 %fusion.39 = f32[20,17,288]{2,1,0:T(8,128)S(1)} fusion(f32[20,20,288]{2,1,0:T(8,128)S(1)} %subtract_subtract_fusion.2, f32[32,32,288]{2,1,0:T(8,128)S(1)} %get-tuple-element.13), kind=kLoop, calls=%fused_computation.70 | loop fusion | flops 2154240 | bytes 2741760 | tf_op jit(solution)/shard_map/mul | solution.py:32
  55.7 0.7 %subtract_multiply_fusion.4 = f32[16,16,288]{2,1,0:T(8,128)S(1)} fusion(f32[16,16,288]{2,1,0:T(8,128)S(1)} %fusion.55, f32[32,32,288]{2,1,0:T(8,128)S(1)} %fusion.1, pred[288]{0:T(512)(128)(4,1)S(1)} %get-tuple-element.29, pred[288]{0:T(512)(128)(4,1)S(1)} %get-tuple-element.30, pred[288]{0:T(512)(128)(4,1)S(1)} %add_compare_fusion.2), kind=kLoop, calls=%fused_computation.105 | loop fusion | flops 1695744 | bytes 885600 | tf_op jit(solution)/shard_map/mul | solution.py:32
  56.3 0.4 multiply_reduce_fusion
  56.7 0.7 %collective-permute-start = (f32[2,16,16]{2,1,0:T(8,128)S(1)}, f32[2,16,16]{2,1,0:T(8,128)S(1)}, u32[]{:S(2)}, u32[]{:S(2)}) collective-permute-start(f32[2,16,16]{2,1,0:T(8,128)S(1)} %pad_maximum_fusion.1), channel_id=1, source_target_pairs={{0,1},{1,0},{2,3},{3,2},{4,5},{5,4},{6,7},{7,6},{8,9},{9,8},{10,11... | collective-permute-start | bytes 6152 | tf_op jit(solution)/shard_map/ppermute | solution.py:279
  57.8 2.8 %collective-permute-done = f32[2,16,16]{2,1,0:T(8,128)S(1)} collective-permute-done((f32[2,16,16]{2,1,0:T(8,128)S(1)}, f32[2,16,16]{2,1,0:T(8,128)S(1)}, u32[]{:S(2)}, u32[]{:S(2)}) %collective-permute-start) | collective-permute-done | bytes 2080 | tf_op jit(solution)/shard_map/ppermute | solution.py:279
  60.6 1.1 %fusion.53 = f32[16,16,288]{2,1,0:T(8,128)} fusion(f32[16,16,288]{2,1,0:T(8,128)S(1)} %get-tuple-element.9, f32[288]{0:T(512)S(1)} %dynamic_slice.11, f32[16,16]{1,0:T(8,128)S(1)} %convert_element_type.44, f32[16,16]{1,0:T(8,128)S(1)} %get-tuple-element.17, f32[16,16]{1,0:T(8,128)S(1)} %get-tuple-element.16, f32[288]{0:T(512)S(1)} %multiply_multiply_fusion.4, ...), kind=kLoop, calls=%fused_computation.98 | loop fusion | flops 958464 | bytes 602752 | tf_op jit(solution)/shard_map/mul | solution.py:109
  (44 shorter events, 2.9 us)
Async XLA Ops:
  28.3 2.7 %copy-start = (f32[32,32,312]{2,1,0:T(8,128)S(1)}, f32[32,32,312]{2,1,0:T(8,128)}, u32[]{:S(2)}) copy-start(f32[32,32,312]{2,1,0:T(8,128)} %shard_map.100) | copy-start | bytes 3833860
  37.3 4.2 %copy-start.1 = (f32[32,28,288]{2,1,0:T(8,128)S(1)}, f32[32,28,288]{2,1,0:T(8,128)}, u32[]{:S(2)}) copy-start(f32[32,28,288]{2,1,0:T(8,128)} %fusion.3) | copy-start | bytes 3096580
  55.6 1.9 %copy-start.2 = (f32[16,16]{1,0:T(8,128)S(1)}, f32[16,16]{1,0:T(8,128)}, u32[]{:S(2)}) copy-start(f32[16,16]{1,0:T(8,128)} %param.18) | copy-start | bytes 3076
  55.6 1.9 %copy-start.3 = (f32[16,16]{1,0:T(8,128)S(1)}, f32[16,16]{1,0:T(8,128)}, u32[]{:S(2)}) copy-start(f32[16,16]{1,0:T(8,128)} %param.17) | copy-start | bytes 3076
  55.6 1.9 %copy-start.5 = (f32[16]{0:T(128)S(1)}, f32[16]{0:T(128)}, u32[]{:S(2)}) copy-start(f32[16]{0:T(128)} %param.19) | copy-start | bytes 196
  55.6 2.1 %copy-start.4 = (s32[16,16]{1,0:T(8,128)S(1)}, s32[16,16]{1,0:T(8,128)}, u32[]{:S(2)}) copy-start(s32[16,16]{1,0:T(8,128)} %param.12) | copy-start | bytes 3076
  56.7 3.8 %collective-permute-start = (f32[2,16,16]{2,1,0:T(8,128)S(1)}, f32[2,16,16]{2,1,0:T(8,128)S(1)}, u32[]{:S(2)}, u32[]{:S(2)}) collective-permute-start(f32[2,16,16]{2,1,0:T(8,128)S(1)} %pad_maximum_fusion.1), channel_id=1, source_target_pairs={{0,1},{1,0},{2,3},{3,2},{4,5},{5,4},{6,7},{7,6},{8,9},{9,8},{10,11... | collective-permute-start | bytes 6152 | tf_op jit(solution)/shard_map/ppermute | solution.py:279
